TPU v7x, 512 devices: a whole 4x4x16 slice. The times are simulated.
512 devices in a mesh: gx: 32 (over y, z_hi, core), gy: 16 (over z_lo, x).
Axes of the slice: x: 4, y: 4, z: 16 (z_hi: 4, z_lo: 4; z = z_hi * 4 + z_lo), core: 2. Of those that a mesh axis runs over, the one named last changes fastest.
Arguments:
- features: bfloat16 [32, 16, 4, 6144], P('gx', 'gy'), may hold values from -6 to 6
- cotangent: bfloat16 [32, 16, 4, 6144], P('gx', 'gy'), may hold values from -6 to 6
- brick_slot: int32 [32, 16, 2, 2, 2], P('gx', 'gy'), may hold values from 0 to 4, as said below
- weight_one: bfloat16 [27, 96, 96], replicated, may hold values from -0.125 to 0.125
- weight_two: bfloat16 [27, 96, 96], replicated, may hold values from -0.125 to 0.125
- gain: float32 [96], replicated, may hold values from 0.1 to 1.9
- bias: float32 [96], replicated, may hold values from -0.5 to 0.5
Outputs:
- out: bfloat16 [32, 16, 4, 6144], P('gx', 'gy')
- grad_features: bfloat16 [32, 16, 4, 6144], P('gx', 'gy')
- grad_weight_one: float32 [27, 96, 96], replicated
- grad_weight_two: float32 [27, 96, 96], replicated
- grad_gain: float32 [96], replicated
- grad_bias: float32 [96], replicated
Inputs may be any that keep to these rules, and one draw needn't show every extreme that they name: `brick_slot`: on each slab the values below 4 are the slots 0 to n - 1, each in exactly one cell, for some n from 2 to 4; all other cells hold 4. At least one slab has n = 4.
All inputs are finite; a program needn't handle non-finite values.
Results may differ from a plain program's by a relative error of at most 0.003.
Values may be sent and summed in bfloat16 or wider, within the bound.
No kernel may reach another device: no remote copies, remote signals or barrier semaphores. Data moves between devices by JAX's collectives and lax.ppermute only.
A program may use at most 64 MiB of HBM per device.

v0:
```python
import math

import jax
import jax.numpy as jnp
from jax import lax
from jax.sharding import PartitionSpec as P


def passed_along(block, axis, distance):
    devices = range(lax.axis_size(axis))
    route = [(i - distance, i) for i in devices if i - distance in devices]
    return lax.ppermute(block, axis, route)


def brick_layout(slot_cells, count_slots, cells_side, column):
    total_cells = slot_cells.shape[0]
    cell_ids = (
        jnp.zeros((count_slots + 1,), jnp.int32)
        .at[slot_cells]
        .set(jnp.arange(total_cells, dtype=jnp.int32))[:count_slots]
    )
    filled = jnp.sum((slot_cells < count_slots).astype(jnp.int32))
    live = (jnp.arange(count_slots, dtype=jnp.int32) < filled).astype(jnp.float32)
    cell_x = cell_ids // (cells_side * column)
    cell_y = cell_ids // column % cells_side
    cell_z = cell_ids % column
    return ((cell_x, cell_y, cell_z), live)


def assemble(ext_flat, cells, span_y, span_z):
    pieces_at = {-1: slice(3, 4), 0: slice(0, 4), 1: slice(0, 1)}
    planes = []
    for along_x in (-1, 0, 1):
        lines = []
        for along_y in (-1, 0, 1):
            blocks = []
            for along_z in (-1, 0, 1):
                rows_index = (
                    ((cells[0] + 1 + along_x) * span_y + cells[1] + 1 + along_y) * span_z
                    + cells[2]
                    + 1
                    + along_z
                )
                whole_bricks = jnp.take(ext_flat, rows_index, axis=0)
                blocks.append(
                    whole_bricks[:, pieces_at[along_x], pieces_at[along_y], pieces_at[along_z], :]
                )
            lines.append(jnp.concatenate(blocks, axis=3))
        planes.append(jnp.concatenate(lines, axis=2))
    return jnp.concatenate(planes, axis=1)


def plane_windows(padded, along_x):
    channels = padded.shape[-1]
    windows = []
    for along_y in (-1, 0, 1):
        for along_z in (-1, 0, 1):
            window = padded[
                :,
                1 + along_x : 5 + along_x,
                1 + along_y : 5 + along_y,
                1 + along_z : 5 + along_z,
                :,
            ]
            windows.append(window.reshape(-1, channels))
    return jnp.stack(windows, axis=0)


def conv_taps(padded, kernel):
    channels = kernel.shape[1]
    total = None
    for along_x in (-1, 0, 1):
        first_tap = 9 * (along_x + 1)
        stacked = plane_windows(padded, along_x)
        term = jnp.einsum(
            "trc,tcd->rd",
            stacked,
            kernel[first_tap : first_tap + 9],
            preferred_element_type=jnp.float32,
        )
        total = term if total is None else total + term
    return total.reshape(padded.shape[0], 4, 4, 4, channels)


def weight_taps(padded, grads):
    channels = grads.shape[-1]
    flat_grads = grads.reshape(-1, channels)
    results = []
    for along_x in (-1, 0, 1):
        stacked = plane_windows(padded, along_x)
        results.append(
            jnp.einsum("trc,rd->tcd", stacked, flat_grads, preferred_element_type=jnp.float32)
        )
    return jnp.concatenate(results, axis=0)


def flipped(kernel):
    return jnp.transpose(jnp.flip(kernel, 0), (0, 2, 1))


def edge_plane(dense_grid, cell_axis, cell_at, plane_at):
    return jnp.take(jnp.take(dense_grid, cell_at, axis=cell_axis), plane_at, axis=cell_axis + 2)


def flat_rows(message):
    return message.reshape(message.shape[0] * message.shape[1], -1)


def as_brick(received, cell_axis, plane_at):
    opened = jnp.expand_dims(received, cell_axis + 2)
    blank = jnp.zeros_like(opened)
    pieces = [opened if spot == plane_at else blank for spot in range(4)]
    return jnp.expand_dims(jnp.concatenate(pieces, axis=cell_axis + 2), cell_axis)


def attach(dense_grid, cell_axis, from_below, from_above):
    low_brick = as_brick(from_below, cell_axis, 3)
    high_brick = as_brick(from_above, cell_axis, 0)
    return jnp.concatenate([low_brick, dense_grid, high_brick], axis=cell_axis)


def halo_grid(dense_grid):
    cells_side = dense_grid.shape[0]
    high_rim = edge_plane(dense_grid, 0, cells_side - 1, 3)
    low_rim = edge_plane(dense_grid, 0, 0, 0)
    from_below = passed_along(flat_rows(high_rim), "gx", 1).reshape(high_rim.shape)
    from_above = passed_along(flat_rows(low_rim), "gx", -1).reshape(low_rim.shape)
    widened = attach(dense_grid, 0, from_below, from_above)
    high_rim = edge_plane(widened, 1, cells_side - 1, 3)
    low_rim = edge_plane(widened, 1, 0, 0)
    from_below = passed_along(flat_rows(high_rim), "gy", 1).reshape(high_rim.shape)
    from_above = passed_along(flat_rows(low_rim), "gy", -1).reshape(low_rim.shape)
    return attach(widened, 1, from_below, from_above)


def body(features, cotangent, brick_slot, weight_one, weight_two, gain, bias):
    count_slots = features.shape[2]
    channels = gain.shape[0]
    cells_side = brick_slot.shape[2]
    column = brick_slot.shape[4]
    slot_cells = brick_slot.reshape(-1)
    cells, live = brick_layout(slot_cells, count_slots, cells_side, column)
    live_five = live[:, None, None, None, None]
    inputs = features.reshape(count_slots, 4, 4, 4, channels)
    upstream = cotangent.reshape(count_slots, 4, 4, 4, channels)

    def padded_field(values):
        source_rows = jnp.concatenate(
            [values, jnp.zeros((1,) + values.shape[1:], values.dtype)], axis=0
        )
        dense_grid = jnp.take(source_rows, slot_cells, axis=0).reshape(
            (cells_side, cells_side, column) + values.shape[1:]
        )
        extended = halo_grid(dense_grid)
        blank = jnp.zeros(
            (extended.shape[0], extended.shape[1], 1) + extended.shape[3:], extended.dtype
        )
        extended = jnp.concatenate([blank, extended, blank], axis=2)
        ext_flat = extended.reshape((-1,) + extended.shape[3:])
        return assemble(ext_flat, cells, extended.shape[1], extended.shape[2])

    padded_inputs = padded_field(inputs)
    first_conv = conv_taps(padded_inputs, weight_one) * live_five
    pre = first_conv * gain + bias
    hidden = (jax.nn.silu(pre) * live_five).astype(jnp.bfloat16)
    padded_hidden = padded_field(hidden)
    out = (
        (inputs.astype(jnp.float32) + conv_taps(padded_hidden, weight_two) * live_five) * live_five
    ).astype(jnp.bfloat16)
    masked_cotangent = (upstream.astype(jnp.float32) * live_five).astype(jnp.bfloat16)
    grad_two_local = weight_taps(padded_hidden, masked_cotangent)
    back_hidden = conv_taps(padded_field(masked_cotangent), flipped(weight_two)) * live_five
    sigmoid = jax.nn.sigmoid(pre)
    back_pre = back_hidden * (sigmoid * (1.0 + pre * (1.0 - sigmoid)))
    gain_local = jnp.sum(back_pre * first_conv, axis=(0, 1, 2, 3))
    bias_local = jnp.sum(back_pre, axis=(0, 1, 2, 3))
    back_conv = (back_pre * gain).astype(jnp.bfloat16)
    grad_one_local = weight_taps(padded_inputs, back_conv)
    back_inputs = conv_taps(padded_field(back_conv), flipped(weight_one)) * live_five
    grad_features = ((upstream.astype(jnp.float32) + back_inputs) * live_five).astype(jnp.bfloat16)
    grad_one_total, grad_two_total, gain_total, bias_total = lax.psum(
        (grad_one_local, grad_two_local, gain_local, bias_local), ("gx", "gy")
    )
    slabs_all = lax.axis_size("gx") * lax.axis_size("gy")
    scale = 1.0 / math.sqrt(slabs_all * count_slots * 64)
    return (
        out.reshape(features.shape),
        grad_features.reshape(features.shape),
        grad_one_total * scale,
        grad_two_total * scale,
        gain_total * scale,
        bias_total * scale,
    )


def solution(mesh):
    in_specs = (
        P("gx", "gy", None, None),
        P("gx", "gy", None, None),
        P("gx", "gy", None, None, None),
        P(),
        P(),
        P(),
        P(),
    )
    out_specs = (P("gx", "gy", None, None), P("gx", "gy", None, None), P(), P(), P(), P())
    return jax.shard_map(body, mesh=mesh, in_specs=in_specs, out_specs=out_specs, check_vma=False)
```

profile of v0, /device:TPU:1, one launch (start us, length us, event | category | flops | bytes accessed | tf_op | source)
XLA Modules:
  0.0 1040.3 jit_solution(16663844304694006693)
XLA Ops:
  15.8 10.3 collective-permute-start.8
  26.3 1.9 collective-permute-start.9
  28.4 1.9 collective-permute-start.1
  30.4 7.5 collective-permute-start
  58.8 4.0 collective-permute-start.10
  65.6 4.6 collective-permute-start.2
  76.5 2.2 pad_maximum_fusion.8
  78.7 1.4 gather_fusion.27
  94.9 1.4 gather_fusion.21
  110.5 1.4 gather_fusion.15
  113.2 1.4 gather_fusion.14
  115.9 1.4 gather_fusion.13
  122.7 1.4 gather_fusion.66
  124.0 1.5 gather_fusion.10
  125.5 1.5 gather_fusion.65
  127.0 1.5 gather_fusion.9
  128.5 1.5 gather_fusion.64
  132.7 1.4 gather_fusion.7
  154.3 1.4 broadcast_select_fusion.17
  155.7 1.4 slice_select_fusion.4
  157.1 1.4 broadcast_select_fusion.21
  161.3 1.4 broadcast_select_fusion.65
  169.8 1.4 broadcast_select_fusion.37
  180.5 1.5 copy.108
  182.1 1.5 copy.109
  186.5 1.6 copy.113
  199.9 1.4 broadcast_select_fusion.69
  201.2 1.4 slice_select_fusion.22
  203.9 1.4 broadcast_select_fusion.41
  205.4 1.4 slice_select_fusion.7
  206.8 1.4 broadcast_select_fusion.45
  233.5 1.6 copy.25
  244.7 4.7 collective-permute-start.12
  249.6 1.9 collective-permute-start.13
  251.7 7.5 collective-permute-start.4
  259.4 1.9 collective-permute-start.5
  261.3 110.9 %all-reduce.20 = (f32[96]{0:T(128)S(1)}, f32[96]{0:T(128)S(1)}) all-reduce(f32[96]{0:T(128)S(1)} %get-tuple-element.105, f32[96]{0:T(128)S(1)} %get-tuple-element.104), channel_id=1, replica_groups=mesh['gx'=32,'gy'=16] {'gx','gy'}, use_global_device_ids=true, to_apply=%region_5.16 | all-reduce | flops 192 | bytes 1536 | tf_op jit(solution)/shard_map/psum | solution.py:181
  376.4 4.0 collective-permute-start.14
  382.4 4.0 collective-permute-start.6
  387.5 2.3 pad_maximum_fusion
  390.3 1.4 gather_fusion.111
  393.0 1.7 copy.60
  421.8 1.4 gather_fusion.44
  427.6 1.4 gather_fusion.96
  434.6 1.5 gather_fusion.93
  438.7 1.4 gather_fusion.36
  479.9 1.6 copy.151
  481.5 1.6 copy.152
  489.6 1.6 copy.142
  491.2 1.5 copy.143
  492.7 1.6 copy.144
  495.0 1.5 copy.146
  497.3 1.6 copy.147
  510.0 1.4 broadcast_select_fusion.68
  514.0 1.4 broadcast_select_fusion.40
  515.5 1.4 slice_select_fusion.3
  516.9 1.4 broadcast_select_fusion.44
  525.1 1.6 copy.133
  526.6 1.6 copy.134
  528.2 1.5 copy.135
  529.7 1.5 copy.136
  531.3 1.7 copy.137
  545.2 484.3 %all-reduce.24.cloned.1.call-done = (f32[27,96,96]{2,1,0:T(8,128)}, f32[27,96,96]{2,1,0:T(8,128)}) async-done(((f32[27,96,96]{2,1,0:T(8,128)}, f32[27,96,96]{2,1,0:T(8,128)}), (f32[27,96,96]{2,1,0:T(8,128)}, f32[27,96,96]{2,1,0:T(8,128)})) %all-reduce.24.cloned.1.call-update) | async-done | bytes 1990672 | tf_op jit(solution)/shard_map/psum | solution.py:181
  1029.4 2.6 broadcast_multiply_fusion.1
  (817 shorter events, 285.1 us)
Async XLA Ops:
  7.2 1022.3 %all-reduce.24.cloned.1.call-start = ((), (), s32[]{:S(2)}) async-start(), calls=%async_computation | async-start | bytes 5308416 | tf_op jit(solution)/shard_map/psum | solution.py:181
  10.1 18.2 %copy-start.125 = (pred[8]{0:T(512)(128)(4,1)}, pred[8]{0:T(512)(128)(4,1)S(1)}, u32[]{:S(2)}) copy-start(pred[8]{0:T(512)(128)(4,1)S(1)} %compare_and_fusion.1) | copy-start | bytes 28
  12.3 43.0 %copy-start.67 = (f32[4]{0:T(128)}, f32[4]{0:T(128)S(1)}, u32[]{:S(2)}) copy-start(f32[4]{0:T(128)S(1)} %compare_convert_fusion.1) | copy-start | bytes 52
  13.4 40.1 %copy-start.10 = (bf16[1,1,4,6144]{3,2,1,0:T(4,128)(2,1)S(1)}, bf16[1,1,4,6144]{3,2,1,0:T(4,128)(2,1)}, u32[]{:S(2)}) copy-start(bf16[1,1,4,6144]{3,2,1,0:T(4,128)(2,1)} %param.28) | copy-start | bytes 147460
  13.4 40.1 %copy-start.1 = (bf16[27,96,96]{2,1,0:T(8,128)(2,1)S(1)}, bf16[27,96,96]{2,1,0:T(8,128)(2,1)}, u32[]{:S(2)}) copy-start(bf16[27,96,96]{2,1,0:T(8,128)(2,1)} %param.31) | copy-start | bytes 1492996
  15.7 38.8 %copy-start = (bf16[27,96,96]{2,1,0:T(8,128)(2,1)S(1)}, bf16[27,96,96]{2,1,0:T(8,128)(2,1)}, u32[]{:S(2)}) copy-start(bf16[27,96,96]{2,1,0:T(8,128)(2,1)} %param.30) | copy-start | bytes 1492996
  15.8 41.0 %collective-permute-start.8 = (bf16[4,1536]{1,0:T(4,128)(2,1)S(1)}, bf16[4,1536]{1,0:T(4,128)(2,1)S(1)}, u32[]{:S(2)}, u32[]{:S(2)}) collective-permute-start(bf16[4,1536]{1,0:T(4,128)(2,1)S(1)} %reshape.236), channel_id=1, source_target_pairs={{0,16},{16,32},{32,48},{48,64},{64,80},{80,96},{96,112},{112,128},... | collective-permute-start | bytes 36872 | tf_op jit(solution)/shard_map/ppermute | solution.py:12
  26.3 30.7 %collective-permute-start.9 = (bf16[4,1536]{1,0:T(4,128)(2,1)S(1)}, bf16[4,1536]{1,0:T(4,128)(2,1)S(1)}, u32[]{:S(2)}, u32[]{:S(2)}) collective-permute-start(bf16[4,1536]{1,0:T(4,128)(2,1)S(1)} %reshape.237), channel_id=1, source_target_pairs={{16,0},{32,16},{48,32},{64,48},{80,64},{96,80},{112,96},{128,112},... | collective-permute-start | bytes 36872 | tf_op jit(solution)/shard_map/ppermute | solution.py:12
  28.4 34.4 %collective-permute-start.1 = (bf16[4,1536]{1,0:T(4,128)(2,1)S(1)}, bf16[4,1536]{1,0:T(4,128)(2,1)S(1)}, u32[]{:S(2)}, u32[]{:S(2)}) collective-permute-start(bf16[4,1536]{1,0:T(4,128)(2,1)S(1)} %reshape.222), channel_id=1, source_target_pairs={{16,0},{32,16},{48,32},{64,48},{80,64},{96,80},{112,96},{128,112},... | collective-permute-start | bytes 36872 | tf_op jit(solution)/shard_map/ppermute | solution.py:12
  30.4 32.5 %collective-permute-start = (bf16[4,1536]{1,0:T(4,128)(2,1)S(1)}, bf16[4,1536]{1,0:T(4,128)(2,1)S(1)}, u32[]{:S(2)}, u32[]{:S(2)}) collective-permute-start(bf16[4,1536]{1,0:T(4,128)(2,1)S(1)} %reshape.221), channel_id=1, source_target_pairs={{0,16},{16,32},{32,48},{48,64},{64,80},{80,96},{96,112},{112,128},... | collective-permute-start | bytes 36872 | tf_op jit(solution)/shard_map/ppermute | solution.py:12
  57.4 12.8 %collective-permute-start.11 = (bf16[8,1536]{1,0:T(8,128)(2,1)S(1)}, bf16[8,1536]{1,0:T(8,128)(2,1)S(1)}, u32[]{:S(2)}, u32[]{:S(2)}) collective-permute-start(bf16[8,1536]{1,0:T(8,128)(2,1)S(1)} %reshape.239), channel_id=1, source_target_pairs={{1,0},{2,1},{3,2},{4,3},{5,4},{6,5},{7,6},{8,7},{9,8},{10,9},{11,1... | collective-permute-start | bytes 73736 | tf_op jit(solution)/shard_map/ppermute | solution.py:12
  58.8 11.5 %collective-permute-start.10 = (bf16[8,1536]{1,0:T(8,128)(2,1)S(1)}, bf16[8,1536]{1,0:T(8,128)(2,1)S(1)}, u32[]{:S(2)}, u32[]{:S(2)}) collective-permute-start(bf16[8,1536]{1,0:T(8,128)(2,1)S(1)} %reshape.238), channel_id=1, source_target_pairs={{0,1},{1,2},{2,3},{3,4},{4,5},{5,6},{6,7},{7,8},{8,9},{9,10},{10,1... | collective-permute-start | bytes 73736 | tf_op jit(solution)/shard_map/ppermute | solution.py:12
  63.6 8.6 collective-permute-start.3
  65.6 7.9 collective-permute-start.2
  122.7 27.6 %copy-start.115 = (pred[4]{0:T(512)(128)(4,1)S(1)}, pred[4]{0:T(512)(128)(4,1)}, u32[]{:S(2)}) copy-start(pred[4]{0:T(512)(128)(4,1)} %get-tuple-element.455) | copy-start | bytes 16
  122.7 28.9 %copy-start.113 = (pred[4]{0:T(512)(128)(4,1)S(1)}, pred[4]{0:T(512)(128)(4,1)}, u32[]{:S(2)}) copy-start(pred[4]{0:T(512)(128)(4,1)} %get-tuple-element.164) | copy-start | bytes 16
  122.7 30.3 %copy-start.111 = (pred[4]{0:T(512)(128)(4,1)S(1)}, pred[4]{0:T(512)(128)(4,1)}, u32[]{:S(2)}) copy-start(pred[4]{0:T(512)(128)(4,1)} %get-tuple-element.454) | copy-start | bytes 16
  122.7 31.6 %copy-start.97 = (pred[4]{0:T(512)(128)(4,1)S(1)}, pred[4]{0:T(512)(128)(4,1)}, u32[]{:S(2)}) copy-start(pred[4]{0:T(512)(128)(4,1)} %get-tuple-element.465) | copy-start | bytes 16
  122.7 33.0 %copy-start.95 = (pred[4]{0:T(512)(128)(4,1)S(1)}, pred[4]{0:T(512)(128)(4,1)}, u32[]{:S(2)}) copy-start(pred[4]{0:T(512)(128)(4,1)} %get-tuple-element.468) | copy-start | bytes 16
  124.0 33.1 %copy-start.93 = (pred[4]{0:T(512)(128)(4,1)S(1)}, pred[4]{0:T(512)(128)(4,1)}, u32[]{:S(2)}) copy-start(pred[4]{0:T(512)(128)(4,1)} %get-tuple-element.467) | copy-start | bytes 16
  124.0 34.5 %copy-start.109 = (pred[4]{0:T(512)(128)(4,1)S(1)}, pred[4]{0:T(512)(128)(4,1)}, u32[]{:S(2)}) copy-start(pred[4]{0:T(512)(128)(4,1)} %get-tuple-element.449) | copy-start | bytes 16
  124.0 35.9 %copy-start.107 = (pred[4]{0:T(512)(128)(4,1)S(1)}, pred[4]{0:T(512)(128)(4,1)}, u32[]{:S(2)}) copy-start(pred[4]{0:T(512)(128)(4,1)} %get-tuple-element.152) | copy-start | bytes 16
  124.0 37.2 %copy-start.105 = (pred[4]{0:T(512)(128)(4,1)S(1)}, pred[4]{0:T(512)(128)(4,1)}, u32[]{:S(2)}) copy-start(pred[4]{0:T(512)(128)(4,1)} %get-tuple-element.448) | copy-start | bytes 16
  125.5 37.1 %copy-start.90 = (pred[4]{0:T(512)(128)(4,1)S(1)}, pred[4]{0:T(512)(128)(4,1)}, u32[]{:S(2)}) copy-start(pred[4]{0:T(512)(128)(4,1)} %get-tuple-element.470) | copy-start | bytes 16
  125.5 37.9 %copy-start.87 = (pred[4]{0:T(512)(128)(4,1)S(1)}, pred[4]{0:T(512)(128)(4,1)}, u32[]{:S(2)}) copy-start(pred[4]{0:T(512)(128)(4,1)} %get-tuple-element.473) | copy-start | bytes 16
  125.5 38.8 %copy-start.85 = (pred[4]{0:T(512)(128)(4,1)S(1)}, pred[4]{0:T(512)(128)(4,1)}, u32[]{:S(2)}) copy-start(pred[4]{0:T(512)(128)(4,1)} %get-tuple-element.472) | copy-start | bytes 16
  127.0 38.2 %copy-start.92 = (pred[4]{0:T(512)(128)(4,1)S(1)}, pred[4]{0:T(512)(128)(4,1)}, u32[]{:S(2)}) copy-start(pred[4]{0:T(512)(128)(4,1)} %get-tuple-element.443) | copy-start | bytes 16
  128.5 37.6 %copy-start.89 = (pred[4]{0:T(512)(128)(4,1)S(1)}, pred[4]{0:T(512)(128)(4,1)}, u32[]{:S(2)}) copy-start(pred[4]{0:T(512)(128)(4,1)} %get-tuple-element.140) | copy-start | bytes 16
  165.1 49.8 %copy-start.29 = (bf16[4,4,1,1,96]{4,3,2,1,0:T(2,128)(2,1)}, bf16[4,4,1,1,96]{4,3,2,1,0:T(2,128)(2,1)S(1)}, u32[]{:S(2)}) copy-start(bf16[4,4,1,1,96]{4,3,2,1,0:T(2,128)(2,1)S(1)} %get-tuple-element.404) | copy-start | bytes 9220
  169.0 45.9 %copy-start.33 = (bf16[4,4,1,1,96]{4,3,2,1,0:T(2,128)(2,1)}, bf16[4,4,1,1,96]{4,3,2,1,0:T(2,128)(2,1)S(1)}, u32[]{:S(2)}) copy-start(bf16[4,4,1,1,96]{4,3,2,1,0:T(2,128)(2,1)S(1)} %get-tuple-element.396) | copy-start | bytes 9220
  178.3 17.6 %copy-start.3 = (bf16[27,96,96]{2,1,0:T(8,128)(2,1)S(1)}, bf16[27,96,96]{2,1,0:T(8,128)(2,1)}, u32[]{:S(2)}) copy-start(bf16[27,96,96]{2,1,0:T(8,128)(2,1)} %rev.7) | copy-start | bytes 1492996
  196.0 14.9 %copy-start.117 = (pred[4]{0:T(512)(128)(4,1)S(1)}, pred[4]{0:T(512)(128)(4,1)}, u32[]{:S(2)}) copy-start(pred[4]{0:T(512)(128)(4,1)} %get-tuple-element.430) | copy-start | bytes 16
  196.0 16.3 %copy-start.46 = (bf16[4,4,1,1,96]{4,3,2,1,0:T(2,128)(2,1)S(1)}, bf16[4,4,1,1,96]{4,3,2,1,0:T(2,128)(2,1)}, u32[]{:S(2)}) copy-start(bf16[4,4,1,1,96]{4,3,2,1,0:T(2,128)(2,1)} %copy-done.45) | copy-start | bytes 9220
  196.0 16.2 %copy-start.48 = (bf16[4,4,1,1,96]{4,3,2,1,0:T(2,128)(2,1)S(1)}, bf16[4,4,1,1,96]{4,3,2,1,0:T(2,128)(2,1)}, u32[]{:S(2)}) copy-start(bf16[4,4,1,1,96]{4,3,2,1,0:T(2,128)(2,1)} %copy-done.47) | copy-start | bytes 9220
  196.0 16.2 %copy-start.50 = (bf16[4,4,1,1,96]{4,3,2,1,0:T(2,128)(2,1)S(1)}, bf16[4,4,1,1,96]{4,3,2,1,0:T(2,128)(2,1)}, u32[]{:S(2)}) copy-start(bf16[4,4,1,1,96]{4,3,2,1,0:T(2,128)(2,1)} %copy-done.49) | copy-start | bytes 9220
  196.0 16.2 %copy-start.52 = (bf16[4,4,1,1,96]{4,3,2,1,0:T(2,128)(2,1)S(1)}, bf16[4,4,1,1,96]{4,3,2,1,0:T(2,128)(2,1)}, u32[]{:S(2)}) copy-start(bf16[4,4,1,1,96]{4,3,2,1,0:T(2,128)(2,1)} %copy-done.51) | copy-start | bytes 9220
  244.7 129.7 %collective-permute-start.12 = (bf16[4,1536]{1,0:T(4,128)(2,1)S(1)}, bf16[4,1536]{1,0:T(4,128)(2,1)S(1)}, u32[]{:S(2)}, u32[]{:S(2)}) collective-permute-start(bf16[4,1536]{1,0:T(4,128)(2,1)S(1)} %reshape.243), channel_id=1, source_target_pairs={{0,16},{16,32},{32,48},{48,64},{64,80},{80,96},{96,112},{112,128},... | collective-permute-start | bytes 36872 | tf_op jit(solution)/shard_map/ppermute | solution.py:12
  249.6 125.0 %collective-permute-start.13 = (bf16[4,1536]{1,0:T(4,128)(2,1)S(1)}, bf16[4,1536]{1,0:T(4,128)(2,1)S(1)}, u32[]{:S(2)}, u32[]{:S(2)}) collective-permute-start(bf16[4,1536]{1,0:T(4,128)(2,1)S(1)} %reshape.244), channel_id=1, source_target_pairs={{16,0},{32,16},{48,32},{64,48},{80,64},{96,80},{112,96},{128,112},... | collective-permute-start | bytes 36872 | tf_op jit(solution)/shard_map/ppermute | solution.py:12
  251.7 128.7 %collective-permute-start.4 = (bf16[4,1536]{1,0:T(4,128)(2,1)S(1)}, bf16[4,1536]{1,0:T(4,128)(2,1)S(1)}, u32[]{:S(2)}, u32[]{:S(2)}) collective-permute-start(bf16[4,1536]{1,0:T(4,128)(2,1)S(1)} %reshape.229), channel_id=1, source_target_pairs={{0,16},{16,32},{32,48},{48,64},{64,80},{80,96},{96,112},{112,128},... | collective-permute-start | bytes 36872 | tf_op jit(solution)/shard_map/ppermute | solution.py:12
  259.4 121.2 %collective-permute-start.5 = (bf16[4,1536]{1,0:T(4,128)(2,1)S(1)}, bf16[4,1536]{1,0:T(4,128)(2,1)S(1)}, u32[]{:S(2)}, u32[]{:S(2)}) collective-permute-start(bf16[4,1536]{1,0:T(4,128)(2,1)S(1)} %reshape.230), channel_id=1, source_target_pairs={{16,0},{32,16},{48,32},{64,48},{80,64},{96,80},{112,96},{128,112},... | collective-permute-start | bytes 36872 | tf_op jit(solution)/shard_map/ppermute | solution.py:12
  375.0 11.4 %collective-permute-start.15 = (bf16[8,1536]{1,0:T(8,128)(2,1)S(1)}, bf16[8,1536]{1,0:T(8,128)(2,1)S(1)}, u32[]{:S(2)}, u32[]{:S(2)}) collective-permute-start(bf16[8,1536]{1,0:T(8,128)(2,1)S(1)} %reshape.246), channel_id=1, source_target_pairs={{1,0},{2,1},{3,2},{4,3},{5,4},{6,5},{7,6},{8,7},{9,8},{10,9},{11,1... | collective-permute-start | bytes 73736 | tf_op jit(solution)/shard_map/ppermute | solution.py:12
  376.4 10.1 collective-permute-start.14
  381.0 5.7 collective-permute-start.7
  382.4 4.9 collective-permute-start.6
  431.8 27.2 %copy-start.116 = (pred[4]{0:T(512)(128)(4,1)S(1)}, pred[4]{0:T(512)(128)(4,1)}, u32[]{:S(2)}) copy-start(pred[4]{0:T(512)(128)(4,1)} %get-tuple-element.455) | copy-start | bytes 16
  431.8 28.0 %copy-start.114 = (pred[4]{0:T(512)(128)(4,1)S(1)}, pred[4]{0:T(512)(128)(4,1)}, u32[]{:S(2)}) copy-start(pred[4]{0:T(512)(128)(4,1)} %get-tuple-element.164) | copy-start | bytes 16
  431.8 28.8 %copy-start.112 = (pred[4]{0:T(512)(128)(4,1)S(1)}, pred[4]{0:T(512)(128)(4,1)}, u32[]{:S(2)}) copy-start(pred[4]{0:T(512)(128)(4,1)} %get-tuple-element.454) | copy-start | bytes 16
  431.8 29.5 %copy-start.98 = (pred[4]{0:T(512)(128)(4,1)S(1)}, pred[4]{0:T(512)(128)(4,1)}, u32[]{:S(2)}) copy-start(pred[4]{0:T(512)(128)(4,1)} %get-tuple-element.465) | copy-start | bytes 16
  431.8 30.4 %copy-start.96 = (pred[4]{0:T(512)(128)(4,1)S(1)}, pred[4]{0:T(512)(128)(4,1)}, u32[]{:S(2)}) copy-start(pred[4]{0:T(512)(128)(4,1)} %get-tuple-element.468) | copy-start | bytes 16
  433.2 29.8 %copy-start.94 = (pred[4]{0:T(512)(128)(4,1)S(1)}, pred[4]{0:T(512)(128)(4,1)}, u32[]{:S(2)}) copy-start(pred[4]{0:T(512)(128)(4,1)} %get-tuple-element.467) | copy-start | bytes 16
  433.2 30.7 %copy-start.110 = (pred[4]{0:T(512)(128)(4,1)S(1)}, pred[4]{0:T(512)(128)(4,1)}, u32[]{:S(2)}) copy-start(pred[4]{0:T(512)(128)(4,1)} %get-tuple-element.449) | copy-start | bytes 16
  433.2 31.5 %copy-start.108 = (pred[4]{0:T(512)(128)(4,1)S(1)}, pred[4]{0:T(512)(128)(4,1)}, u32[]{:S(2)}) copy-start(pred[4]{0:T(512)(128)(4,1)} %get-tuple-element.152) | copy-start | bytes 16
  433.2 32.2 %copy-start.106 = (pred[4]{0:T(512)(128)(4,1)S(1)}, pred[4]{0:T(512)(128)(4,1)}, u32[]{:S(2)}) copy-start(pred[4]{0:T(512)(128)(4,1)} %get-tuple-element.448) | copy-start | bytes 16
  433.2 33.0 %copy-start.91 = (pred[4]{0:T(512)(128)(4,1)S(1)}, pred[4]{0:T(512)(128)(4,1)}, u32[]{:S(2)}) copy-start(pred[4]{0:T(512)(128)(4,1)} %get-tuple-element.470) | copy-start | bytes 16
  434.6 32.4 %copy-start.88 = (pred[4]{0:T(512)(128)(4,1)S(1)}, pred[4]{0:T(512)(128)(4,1)}, u32[]{:S(2)}) copy-start(pred[4]{0:T(512)(128)(4,1)} %get-tuple-element.473) | copy-start | bytes 16
  434.6 32.6 %copy-start.86 = (pred[4]{0:T(512)(128)(4,1)S(1)}, pred[4]{0:T(512)(128)(4,1)}, u32[]{:S(2)}) copy-start(pred[4]{0:T(512)(128)(4,1)} %get-tuple-element.472) | copy-start | bytes 16
  487.3 19.4 %copy-start.2 = (bf16[27,96,96]{2,1,0:T(8,128)(2,1)S(1)}, bf16[27,96,96]{2,1,0:T(8,128)(2,1)}, u32[]{:S(2)}) copy-start(bf16[27,96,96]{2,1,0:T(8,128)(2,1)} %rev.8) | copy-start | bytes 1492996
  506.8 14.2 %copy-start.118 = (pred[4]{0:T(512)(128)(4,1)S(1)}, pred[4]{0:T(512)(128)(4,1)}, u32[]{:S(2)}) copy-start(pred[4]{0:T(512)(128)(4,1)} %get-tuple-element.430) | copy-start | bytes 16
  506.8 15.5 %copy-start.14 = (bf16[4,4,1,4,96]{4,3,2,1,0:T(4,128)(2,1)S(1)}, bf16[4,4,1,4,96]{4,3,2,1,0:T(4,128)(2,1)}, u32[]{:S(2)}) copy-start(bf16[4,4,1,4,96]{4,3,2,1,0:T(4,128)(2,1)} %copy-done.13) | copy-start | bytes 36868
  506.8 15.5 %copy-start.16 = (bf16[4,4,1,4,96]{4,3,2,1,0:T(4,128)(2,1)S(1)}, bf16[4,4,1,4,96]{4,3,2,1,0:T(4,128)(2,1)}, u32[]{:S(2)}) copy-start(bf16[4,4,1,4,96]{4,3,2,1,0:T(4,128)(2,1)} %copy-done.15) | copy-start | bytes 36868
  506.9 15.5 %copy-start.38 = (bf16[4,4,1,1,96]{4,3,2,1,0:T(2,128)(2,1)S(1)}, bf16[4,4,1,1,96]{4,3,2,1,0:T(2,128)(2,1)}, u32[]{:S(2)}) copy-start(bf16[4,4,1,1,96]{4,3,2,1,0:T(2,128)(2,1)} %copy-done.37) | copy-start | bytes 9220
  506.9 15.5 %copy-start.40 = (bf16[4,4,1,1,96]{4,3,2,1,0:T(2,128)(2,1)S(1)}, bf16[4,4,1,1,96]{4,3,2,1,0:T(2,128)(2,1)}, u32[]{:S(2)}) copy-start(bf16[4,4,1,1,96]{4,3,2,1,0:T(2,128)(2,1)} %copy-done.39) | copy-start | bytes 9220
  506.9 15.5 %copy-start.42 = (bf16[4,4,1,1,96]{4,3,2,1,0:T(2,128)(2,1)S(1)}, bf16[4,4,1,1,96]{4,3,2,1,0:T(2,128)(2,1)}, u32[]{:S(2)}) copy-start(bf16[4,4,1,1,96]{4,3,2,1,0:T(2,128)(2,1)} %copy-done.41) | copy-start | bytes 9220
  506.9 15.5 %copy-start.44 = (bf16[4,4,1,1,96]{4,3,2,1,0:T(2,128)(2,1)S(1)}, bf16[4,4,1,1,96]{4,3,2,1,0:T(2,128)(2,1)}, u32[]{:S(2)}) copy-start(bf16[4,4,1,1,96]{4,3,2,1,0:T(2,128)(2,1)} %copy-done.43) | copy-start | bytes 9220
  (80 other events, 424.2 us)
Sparse Core Ops, SparseCore 0:
  543.7 485.6 all-reduce.23
where the time goes:
time: 1050 us; the launch traced here: 1040 us
  waiting for transfers between devices  485 us (46%)
  local copies, waits for them, and re-layouts  253 us (24%)
  blocking collectives  111 us (11%)
  other arithmetic  97.4 us (9%)
  starting transfers between devices  59.5 us (6%)
  between operations  29.9 us (3%)
    psum x1, waiting for transfers between devices, body(): lax.psum((grad_one_local, grad_two_local, gain_local, bias_local), ('gx',...  484 us
    gather x108, local copies, waits for them, and re-layouts, assemble(): whole_bricks = jnp.take(ext_flat, rows_index, axis=0)  140 us
    psum x1, blocking collectives, body(): lax.psum((grad_one_local, grad_two_local, gain_local, bias_local), ('gx',...  111 us
    ppermute x16, starting transfers between devices, passed_along(): return lax.ppermute(block, axis, route)  59.4 us
    select_n x56, other arithmetic, assemble(): whole_bricks = jnp.take(ext_flat, rows_index, axis=0)  59.2 us
    another operation x120, local copies, waits for them, and re-layouts, plane_windows(): return jnp.stack(windows, axis=0)  54.6 us
    unnamed x362, local copies, waits for them, and re-layouts  30.7 us
  transfers between devices with their start and end apart: 17, of which 2 were waited for; matrix products, arithmetic and copies ran while one was open for 3% of the time, Pallas kernels for 0%

commit v1 on v0

v1 whole, which is shorter than its diff:
```python
import functools
import math

import jax
import jax.numpy as jnp
from jax import lax
from jax.experimental import pallas as pl
from jax.experimental.pallas import tpu as pltpu
from jax.sharding import PartitionSpec as P

C = 96
LANES = 128
SIDE = 8
TAPS = 27
SPAN = TAPS * LANES
OWN = 512
RIM = 800
ROWS = 4096
F32 = jnp.float32
BF16 = jnp.bfloat16

VMEM_SPEC = pl.BlockSpec(memory_space=pltpu.VMEM)
SMEM_SPEC = pl.BlockSpec(memory_space=pltpu.SMEM)


def call(kernel, out_shape, specs, scratch=(), flops=0, moved=0, name=None, room=16):
    return pl.pallas_call(
        kernel,
        out_shape=out_shape,
        in_specs=specs,
        out_specs=jax.tree.map(lambda _: VMEM_SPEC, out_shape),
        scratch_shapes=list(scratch),
        cost_estimate=pl.CostEstimate(flops=flops, bytes_accessed=moved, transcendentals=0),
        name=name,
        compiler_params=pltpu.CompilerParams(vmem_limit_bytes=room << 20),
    )


def sublane_low(shape):
    return lax.broadcasted_iota(jnp.int32, shape, len(shape) - 2) < 4


def rotated(value, shift):
    flat = value.reshape((-1,) + value.shape[-2:])
    return pltpu.roll(flat, shift, 1).reshape(value.shape)


def grid_kernel(slots, features, cotangent, grid, low, high):
    count = features.shape[0]
    for field, source in enumerate((features, cotangent)):
        for i in range(2):
            for j in range(2):
                tiles, marks = [], []
                for k in range(2):
                    slot = slots[(i * 2 + j) * 2 + k]
                    filled = (slot < count).astype(F32)
                    brick = source[jnp.minimum(slot, count - 1)].astype(F32) * filled
                    tiles.append(brick.reshape(8, 8, C))
                    marks.append(filled)
                first, second = tiles
                is_low = sublane_low(first.shape)
                even = jnp.where(is_low, first, rotated(second, 4))
                odd = jnp.where(is_low, rotated(first, 4), second)
                joined = jnp.stack(
                    [even.reshape(4, 2, 8, C), odd.reshape(4, 2, 8, C)], axis=2
                ).reshape(4, 4, 8, C)
                at_x, at_y = slice(4 * i, 4 * i + 4), slice(4 * j, 4 * j + 4)
                grid[field, at_x, at_y, :, 0:C] = joined
                rest = (4, 4, 8, LANES - C)
                if field == 0:
                    mark = jnp.where(sublane_low(rest), marks[0], marks[1])
                else:
                    mark = jnp.zeros(rest, F32)
                grid[field, at_x, at_y, :, C:LANES] = mark
    for field in range(2):
        rows = slice(field * 128, field * 128 + 128)
        low[rows] = grid[field, 0:2].reshape(128, LANES).astype(BF16)
        high[rows] = grid[field, 6:8].reshape(128, LANES).astype(BF16)


def opened(message, lead):
    return message.astype(F32).reshape(lead + (SIDE, LANES))


def rim_kernel(grid, below, above, low, high):
    lower = opened(below[...], (2, 2, SIDE))
    upper = opened(above[...], (2, 2, SIDE))
    for message, at in ((low, 0), (high, SIDE - 2)):
        for field in range(2):
            base = field * 192
            message[base : base + 32] = (
                lower[field, :, at : at + 2].reshape(32, LANES).astype(BF16)
            )
            message[base + 32 : base + 160] = (
                grid[field, :, at : at + 2].reshape(128, LANES).astype(BF16)
            )
            message[base + 160 : base + 192] = (
                upper[field, :, at : at + 2].reshape(32, LANES).astype(BF16)
            )


def with_neighbours(value):
    spot = lax.broadcasted_iota(jnp.int32, value.shape, value.ndim - 2)
    before = jnp.where(spot == 0, 0.0, rotated(value, 1))
    after = jnp.where(spot == SIDE - 1, 0.0, rotated(value, SIDE - 1))
    return jnp.concatenate([before, value, after], axis=value.ndim - 1)


def fill_windows(windows, stacked, start, extent):
    rows = extent * extent * SIDE
    for wx in range(3):
        for wy in range(3):
            at = (wx * 3 + wy) * 3 * LANES
            piece = stacked[
                start + wx : start + wx + extent, start + wy : start + wy + extent
            ]
            windows[0:rows, at : at + 3 * LANES] = piece.reshape(rows, 3 * LANES).astype(BF16)


def spread(kernel, rows_ref):
    rows_ref[...] = jnp.zeros_like(rows_ref)
    for tap in range(TAPS):
        rows_ref[tap * LANES : tap * LANES + C, 0:C] = kernel[tap]


def spread_flipped(kernel, columns_ref):
    columns_ref[...] = jnp.zeros_like(columns_ref)
    for tap in range(TAPS):
        columns_ref[0:C, tap * LANES : tap * LANES + C] = kernel[TAPS - 1 - tap]


def plain_dot(left, right):
    return jnp.dot(left, right, preferred_element_type=F32)


def turned_dot(left, right):
    return lax.dot_general(left, right, (((1,), (1,)), ((), ())), preferred_element_type=F32)


def rounded(value):
    return value.astype(BF16).astype(F32)


def gradient_kernel(
    grid, below, above, left, right, weight_one, weight_two, gain_bias,
    result, inner,
    field_ref, stack_ref, windows, rows_ref, columns_ref, terms_one, terms_two, packed,
):
    lower = opened(below[...], (2, 2, SIDE))
    upper = opened(above[...], (2, 2, SIDE))
    to_left = opened(left[...], (2, SIDE + 4, 2))
    to_right = opened(right[...], (2, SIDE + 4, 2))

    def load_field(field):
        field_ref[2 : SIDE + 2, 2 : SIDE + 2] = grid[field]
        field_ref[0:2, 2 : SIDE + 2] = lower[field]
        field_ref[SIDE + 2 : SIDE + 4, 2 : SIDE + 2] = upper[field]
        field_ref[:, 0:2] = to_left[field]
        field_ref[:, SIDE + 2 : SIDE + 4] = to_right[field]

    gain, bias = gain_bias[0:1], gain_bias[1:2]
    spread(weight_one, rows_ref)
    spread_flipped(weight_two, columns_ref)
    load_field(0)
    mark = field_ref[1 : SIDE + 3, 1 : SIDE + 3].reshape(RIM, LANES)[:, C : C + 1]
    stack_ref[...] = with_neighbours(field_ref[...])
    fill_windows(windows, stack_ref, 0, SIDE + 2)
    first_conv = plain_dot(windows[...], rows_ref[...]) * mark
    pre = first_conv * gain + bias
    gate = 1.0 / (1.0 + jnp.exp(-pre))
    hidden = rounded(pre * gate * mark)
    slope = gate * (1.0 + pre * (1.0 - gate)) * mark
    inner[0:RIM] = hidden.astype(BF16)

    load_field(1)
    stack_ref[...] = with_neighbours(field_ref[...])
    fill_windows(windows, stack_ref, 0, SIDE + 2)
    back_hidden = turned_dot(windows[...], columns_ref[...])
    back_pre = back_hidden * slope
    back_conv = rounded(back_pre * gain)
    inner[RIM : 2 * RIM] = back_conv.astype(BF16)

    def own(value):
        lead = value.reshape(SIDE + 2, SIDE + 2, SIDE, LANES)
        return lead[1 : SIDE + 1, 1 : SIDE + 1].reshape(OWN, LANES)

    own_pre = own(back_pre)
    gain_term = jnp.sum(own_pre * own(first_conv), axis=0, keepdims=True)
    bias_term = jnp.sum(own_pre, axis=0, keepdims=True)

    fill_windows(windows, stack_ref, 1, SIDE)
    hidden_turned = own(hidden).T.astype(BF16)
    terms_two[...] = plain_dot(hidden_turned, windows[0:OWN])

    lead = back_conv.reshape(SIDE + 2, SIDE + 2, SIDE, LANES)
    stack_ref[0 : SIDE + 2, 0 : SIDE + 2] = with_neighbours(lead)
    fill_windows(windows, stack_ref, 0, SIDE)
    features_turned = grid[0].reshape(OWN, LANES).T.astype(BF16)
    terms_one[...] = plain_dot(features_turned, windows[0:OWN])

    def term(index):
        source = terms_one if index < TAPS else terms_two
        at = (TAPS - 1 - index % TAPS) * LANES
        return source[0:C, at : at + LANES]

    lane = lax.broadcasted_iota(jnp.int32, (C, LANES), 1)
    for group in range(13):
        split = term(4 * group + 3)
        for part in range(3):
            row = (3 * group + part) * C
            moved = pltpu.roll(split, C - 32 * part, 1)
            packed[row : row + C] = jnp.where(lane < C, term(4 * group + part), moved)
    packed[39 * C : 40 * C] = term(52)
    packed[40 * C : 41 * C] = term(53)
    packed[41 * C : ROWS] = jnp.zeros((ROWS - 41 * C, LANES), F32)
    packed[41 * C : 41 * C + 1] = gain_term
    packed[41 * C + 1 : 41 * C + 2] = bias_term
    result[...] = packed[...].astype(BF16)


def output_kernel(
    slots, grid, inner, weight_one, weight_two, out, grad,
    stack_ref, windows, rows_ref, columns_ref,
):
    count = out.shape[0]
    out[...] = jnp.zeros_like(out)
    grad[...] = jnp.zeros_like(grad)
    spread(weight_two, rows_ref)
    spread_flipped(weight_one, columns_ref)
    for field, target in enumerate((out, grad)):
        lead = inner[field * RIM : field * RIM + RIM].astype(F32)
        stack_ref[...] = with_neighbours(lead.reshape(SIDE + 2, SIDE + 2, SIDE, LANES))
        fill_windows(windows, stack_ref, 0, SIDE)
        if field == 0:
            total = plain_dot(windows[...], rows_ref[...])
        else:
            total = turned_dot(windows[...], columns_ref[...])
        dense = total.reshape(SIDE, SIDE, SIDE, LANES) + grid[field]
        for i in range(2):
            for j in range(2):
                column = dense[4 * i : 4 * i + 4, 4 * j : 4 * j + 4].reshape(4, 2, 2, 8, LANES)
                even = column[:, :, 0].reshape(8, 8, LANES)
                odd = column[:, :, 1].reshape(8, 8, LANES)
                is_low = sublane_low(even.shape)
                tiles = (
                    jnp.where(is_low, even, rotated(odd, 4)),
                    jnp.where(is_low, rotated(even, 4), odd),
                )
                for k in range(2):
                    slot = slots[(i * 2 + j) * 2 + k]
                    brick = tiles[k].reshape(64, LANES)[:, 0:C].astype(BF16)

                    @pl.when(slot < count)
                    def _():
                        target[slot] = brick


def finish_kernel(scale, total, grad_one, grad_two, grad_gain, grad_bias):
    lane = lax.broadcasted_iota(jnp.int32, (C, LANES), 1)

    def put(index, value):
        target = grad_one if index < TAPS else grad_two
        target[index % TAPS] = value[:, 0:C] * scale

    for group in range(13):
        parts = [total[(3 * group + part) * C : (3 * group + part + 1) * C] for part in range(3)]
        for part in range(3):
            put(4 * group + part, parts[part])
        moved = [pltpu.roll(parts[part], 32 * part + 32, 1) for part in range(3)]
        put(4 * group + 3, jnp.where(lane < 32, moved[0], jnp.where(lane < 64, moved[1], moved[2])))
    put(52, total[39 * C : 40 * C])
    put(53, total[40 * C : 41 * C])
    grad_gain[...] = total[41 * C : 41 * C + 1, 0:C] * scale
    grad_bias[...] = total[41 * C + 1 : 41 * C + 2, 0:C] * scale


def shape(dims, dtype):
    return jax.ShapeDtypeStruct(dims, dtype)


def dense_parts(features, cotangent, slots):
    return call(
        grid_kernel,
        (shape((2, SIDE, SIDE, SIDE, LANES), F32), shape((256, LANES), BF16), shape((256, LANES), BF16)),
        [SMEM_SPEC, VMEM_SPEC, VMEM_SPEC],
        moved=2_000_000,
        name="dense_grid",
    )(slots, features, cotangent)


def rims(grid, below, above):
    return call(
        rim_kernel,
        (shape((384, LANES), BF16), shape((384, LANES), BF16)),
        [VMEM_SPEC] * 3,
        moved=1_500_000,
        name="rims",
    )(grid, below, above)


def gradients(grid, halos, weight_one, weight_two, gain_bias):
    return call(
        gradient_kernel,
        (shape((ROWS, LANES), BF16), shape((2 * RIM, LANES), BF16)),
        [VMEM_SPEC] * 8,
        scratch=[
            pltpu.VMEM((SIDE + 4, SIDE + 4, SIDE, LANES), F32),
            pltpu.VMEM((SIDE + 4, SIDE + 4, SIDE, 3 * LANES), F32),
            pltpu.VMEM((RIM, SPAN), BF16),
            pltpu.VMEM((SPAN, LANES), BF16),
            pltpu.VMEM((LANES, SPAN), BF16),
            pltpu.VMEM((LANES, SPAN), F32),
            pltpu.VMEM((LANES, SPAN), F32),
            pltpu.VMEM((ROWS, LANES), F32),
        ],
        flops=2_400_000_000,
        moved=8_000_000,
        name="gradients",
        room=36,
    )(grid, *halos, weight_one, weight_two, gain_bias)


def outputs(slots, grid, inner, weight_one, weight_two):
    result = shape((4, 64, C), BF16)
    return call(
        output_kernel,
        (result, result),
        [SMEM_SPEC] + [VMEM_SPEC] * 4,
        scratch=[
            pltpu.VMEM((SIDE + 2, SIDE + 2, SIDE, 3 * LANES), F32),
            pltpu.VMEM((OWN, SPAN), BF16),
            pltpu.VMEM((SPAN, LANES), BF16),
            pltpu.VMEM((LANES, SPAN), BF16),
        ],
        flops=900_000_000,
        moved=4_000_000,
        name="outputs",
        room=24,
    )(slots, grid, inner, weight_one, weight_two)


def finish(total, scale):
    grads = shape((TAPS, C, C), F32)
    line = shape((1, C), F32)
    return call(
        functools.partial(finish_kernel, scale),
        (grads, grads, line, line),
        [VMEM_SPEC],
        moved=4_000_000,
        name="finish",
    )(total)


SIZES = dict(y=4, zh=4, core=2, zl=4, x=4)
PLANE = ("core", "y", "x")
LINE = ("zh", "zl")


def reduce_all(packed):
    plane, line = lax.axis_size(PLANE), lax.axis_size(LINE)
    rows = ROWS // plane
    parts = packed.reshape(plane, rows, LANES)
    parts = lax.all_to_all(parts, PLANE, 0, 0)
    chunk = jnp.sum(parts.astype(F32), axis=0)
    pieces = lax.all_to_all(chunk.reshape(line, rows // line, LANES), LINE, 0, 0)
    piece = jnp.sum(pieces, axis=0)
    chunk = lax.all_to_all(jnp.broadcast_to(piece, pieces.shape), LINE, 0, 0)
    chunk = chunk.reshape(rows, LANES)
    total = lax.all_to_all(jnp.broadcast_to(chunk, parts.shape), PLANE, 0, 0)
    return total.reshape(ROWS, LANES)


GX = ("y", "zh", "core")
GY = ("zl", "x")


def passed_along(block, axis, distance):
    devices = range(lax.axis_size(axis))
    route = [(i - distance, i) for i in devices if i - distance in devices]
    return lax.ppermute(block, axis, route)


def body(features, cotangent, brick_slot, weight_one, weight_two, gain, bias):
    slots = brick_slot.reshape(-1)
    source = features.reshape(4, 64, C)
    upstream = cotangent.reshape(4, 64, C)
    padded = jnp.pad(jnp.stack([gain, bias]), ((0, 0), (0, LANES - C)))
    grid, low, high = dense_parts(source, upstream, slots)
    below = passed_along(high, GX, 1)
    above = passed_along(low, GX, -1)
    low, high = rims(grid, below, above)
    left = passed_along(high, GY, 1)
    right = passed_along(low, GY, -1)
    packed, inner = gradients(grid, (below, above, left, right), weight_one, weight_two, padded)
    out, grad = outputs(slots, grid, inner, weight_one, weight_two)
    total = reduce_all(packed)
    scale = 1.0 / math.sqrt(lax.axis_size(GX) * lax.axis_size(GY) * 256)
    grad_one, grad_two, grad_gain, grad_bias = finish(total, scale)
    return (
        out.reshape(features.shape),
        grad.reshape(features.shape),
        grad_one,
        grad_two,
        grad_gain.reshape(gain.shape),
        grad_bias.reshape(bias.shape),
    )


def solution(mesh):
    fine = jax.sharding.Mesh(mesh.devices.reshape(tuple(SIZES.values())), tuple(SIZES))
    slabs = P(GX, GY, None, None)
    in_specs = (slabs, slabs, P(GX, GY, None, None, None), P(), P(), P(), P())
    out_specs = (slabs, slabs, P(), P(), P(), P())
    return jax.shard_map(body, mesh=fine, in_specs=in_specs, out_specs=out_specs, check_vma=False)
```

time: 1050 us -> 143 us (0.14)
  waiting for transfers between devices: 485 us -> 30.7 us
  local copies, waits for them, and re-layouts: 253 us -> 9.98 us
  other arithmetic: 97.4 us -> 0.85 us
  blocking collectives: 111 us -> 62.3 us
  starting transfers between devices: 59.5 us -> 24.6 us
  between operations: 29.9 us -> 0.75 us
  Pallas kernels: 0 us -> 13 us
    psum x1 -> x0, waiting for transfers between devices: 484 us -> none  [body(): lax.psum((grad_one_local, grad_two_local, gain_local, bias_local), ('gx',...]
    gather x133 -> x0, local copies, waits for them, and re-layouts: 143 us -> none  [the longest x108 140 us: assemble(): whole_bricks = jnp.take(ext_flat, rows_index, axis=0)]
    psum x1 -> x0, blocking collectives: 111 us -> none  [body(): lax.psum((grad_one_local, grad_two_local, gain_local, bias_local), ('gx',...]
    all_to_all x0 -> x3, blocking collectives: none -> 62.3 us  [the longest x1 25.7 us: reduce_all(): parts = lax.all_to_all(parts, PLANE, 0, 0)]
    select_n x60 -> x0, other arithmetic: 59.5 us -> none  [the longest x56 59.2 us: assemble(): whole_bricks = jnp.take(ext_flat, rows_index, axis=0)]
    another operation x141 -> x0, local copies, waits for them, and re-layouts: 57.2 us -> none  [the longest x120 54.6 us: plane_windows(): return jnp.stack(windows, axis=0)]
    ppermute x16 -> x4, starting transfers between devices: 59.4 us -> 16.5 us  [passed_along(): return lax.ppermute(block, axis, route)]
    unnamed x362 -> x12, local copies, waits for them, and re-layouts: 30.7 us -> 4.28 us
  transfers between devices with their start and end apart: 17 -> 5, of which waited for: 2 -> 3; matrix products, arithmetic and copies ran while one was open for 3% -> 2% of each run, Pallas kernels for 0% -> 3%
where the time goes in v1:
time: 143 us; the launch traced here: 142 us
  blocking collectives  62.3 us (44%)
  waiting for transfers between devices  30.7 us (21%)
  starting transfers between devices  24.6 us (17%)
  Pallas kernels  13 us (9%)
  local copies, waits for them, and re-layouts  9.98 us (7%)
    all_to_all x1, blocking collectives, reduce_all(): parts = lax.all_to_all(parts, PLANE, 0, 0)  25.7 us
    all_to_all x1, blocking collectives, reduce_all(): lax.all_to_all(chunk.reshape(line, rows // line, LANES), LINE, 0, 0)  22.2 us
    all_to_all x1, waiting for transfers between devices, reduce_all(): total = lax.all_to_all(jnp.broadcast_to(chunk, parts.shape), PLANE, 0, 0)  19.8 us
    ppermute x4, starting transfers between devices, passed_along(): return lax.ppermute(block, axis, route)  16.5 us
    all_to_all x1, blocking collectives, reduce_all(): chunk = lax.all_to_all(jnp.broadcast_to(piece, pieces.shape), LINE, 0, 0)  14.4 us
    ppermute x4, waiting for transfers between devices, passed_along(): return lax.ppermute(block, axis, route)  10.9 us
    all_to_all x1, starting transfers between devices, reduce_all(): total = lax.all_to_all(jnp.broadcast_to(chunk, parts.shape), PLANE, 0, 0)  8.07 us
    pallas_call x1, Pallas kernels, gradients(): call(gradient_kernel, (shape((ROWS, LANES), BF16), shape((2 * RIM, LANES)...  5.57 us
  transfers between devices with their start and end apart: 5, of which 3 were waited for; matrix products, arithmetic and copies ran while one was open for 2% of the time, Pallas kernels for 3%

profile of v1, /device:TPU:1, one launch (start us, length us, event | category | flops | bytes accessed | tf_op | source)
XLA Modules:
  0.0 142.2 jit_solution(16601055184434653326)
XLA Ops:
  0.6 0.8 reshape.45.slots
  1.4 0.9 reshape.46.features
  2.3 0.9 reshape.47.cotangent
  3.2 0.6 dense_grid.1
  3.9 10.2 %collective-permute-start = (bf16[256,128]{1,0:T(8,128)(2,1)S(1)}, bf16[256,128]{1,0:T(8,128)(2,1)S(1)}, u32[]{:S(2)}, u32[]{:S(2)}) collective-permute-start(bf16[256,128]{1,0:T(8,128)(2,1)S(1)} %get-tuple-element.20), channel_id=1, source_target_pairs={{0,16},{16,32},{32,48},{48,64},{64,80},{80,96},{96,112},{112,128},... | collective-permute-start | bytes 196616 | tf_op jit(solution)/shard_map/ppermute | solution.py:380
  14.1 1.9 %collective-permute-start.1 = (bf16[256,128]{1,0:T(8,128)(2,1)S(1)}, bf16[256,128]{1,0:T(8,128)(2,1)S(1)}, u32[]{:S(2)}, u32[]{:S(2)}) collective-permute-start(bf16[256,128]{1,0:T(8,128)(2,1)S(1)} %get-tuple-element.21), channel_id=1, source_target_pairs={{16,0},{32,16},{48,32},{64,48},{80,64},{96,80},{112,96},{128,112},... | collective-permute-start | bytes 196616 | tf_op jit(solution)/shard_map/ppermute | solution.py:380
  16.0 0.0 collective-permute-done.below
  16.0 7.6 %collective-permute-done.1.above = bf16[256,128]{1,0:T(8,128)(2,1)S(1)} collective-permute-done((bf16[256,128]{1,0:T(8,128)(2,1)S(1)}, bf16[256,128]{1,0:T(8,128)(2,1)S(1)}, u32[]{:S(2)}, u32[]{:S(2)}) %collective-permute-start.1) | collective-permute-done | bytes 65568 | tf_op jit(solution)/shard_map/ppermute | solution.py:380
  23.6 3.1 %collective-permute-start.2 = (bf16[384,128]{1,0:T(8,128)(2,1)S(1)}, bf16[384,128]{1,0:T(8,128)(2,1)S(1)}, u32[]{:S(2)}, u32[]{:S(2)}) collective-permute-start(bf16[384,128]{1,0:T(8,128)(2,1)S(1)} %get-tuple-element.22), channel_id=1, source_target_pairs={{0,1},{1,2},{2,3},{3,4},{4,5},{5,6},{6,7},{7,8},{8,9},{9,10},{10,1... | collective-permute-start | bytes 294920 | tf_op jit(solution)/shard_map/ppermute | solution.py:380
  26.7 1.3 collective-permute-start.3
  28.0 0.7 select_maximum_fusion.gain_bias
  28.7 0.0 collective-permute-done.2.left
  28.7 3.4 %collective-permute-done.3.right = bf16[384,128]{1,0:T(8,128)(2,1)S(1)} collective-permute-done((bf16[384,128]{1,0:T(8,128)(2,1)S(1)}, bf16[384,128]{1,0:T(8,128)(2,1)S(1)}, u32[]{:S(2)}, u32[]{:S(2)}) %collective-permute-start.3) | collective-permute-done | bytes 98336 | tf_op jit(solution)/shard_map/ppermute | solution.py:380
  32.1 0.0 copy-start
  32.1 1.1 copy-done
  33.2 0.0 copy-start.2
  33.2 1.1 copy-done.2
  34.3 5.6 %gradients.1 = (bf16[4096,128]{1,0:T(8,128)(2,1)S(1)}, bf16[1600,128]{1,0:T(8,128)(2,1)S(1)}) custom-call(f32[2,8,8,8,128]{4,3,2,1,0:T(8,128)S(1)} %get-tuple-element.19.grid, bf16[256,128]{1,0:T(8,128)(2,1)S(1)} %collective-permute-done.below, bf16[256,128]{1,0:T(8,128)(2,1)S(1)} %collective-permute-done.1.above, ...), custom_call_target="tpu_custom_call" | custom-call | flops 2400000000 | bytes 8000000 | tf_op jit(solution)/shard_map/gradients/pallas_call | solution.py:302
  39.8 0.0 copy-start.4
  39.9 25.7 %all_to_all.20 = bf16[32,128,128]{2,1,0:T(8,128)(2,1)S(1)} all-to-all(bf16[32,128,128]{2,1,0:T(8,128)(2,1)S(1)} %bitcast.9), channel_id=1, replica_groups=mesh['y'=4,'zh'=4,'core'=2,'zl'=4,'x'=4] {'core','y','x'}, dimensions={0} | all-to-all | bytes 2097152 | tf_op jit(solution)/shard_map/all_to_all | solution.py:363
  65.6 0.0 copy-done.4
  65.6 0.2 convert_reduce_fusion
  65.7 22.2 %all_to_all.21 = f32[16,8,128]{2,1,0:T(8,128)S(1)} all-to-all(f32[16,8,128]{2,1,0:T(8,128)S(1)} %bitcast.10), channel_id=1, replica_groups=mesh['y'=4,'zh'=4,'core'=2,'zl'=4,'x'=4] {'zh','zl'}, dimensions={0} | all-to-all | bytes 131072 | tf_op jit(solution)/shard_map/all_to_all | solution.py:365
  87.9 14.4 %all_to_all.22 = f32[16,8,128]{2,1,0:T(8,128)S(1)} all-to-all(f32[16,8,128]{2,1,0:T(8,128)S(1)} %broadcast_in_dim.6), channel_id=1, replica_groups=mesh['y'=4,'zh'=4,'core'=2,'zl'=4,'x'=4] {'zh','zl'}, dimensions={0} | all-to-all | bytes 131072 | tf_op jit(solution)/shard_map/all_to_all | solution.py:367
  102.3 1.6 %broadcast_in_dim.7 = f32[32,128,128]{2,1,0:T(8,128)} broadcast(f32[128,128]{1,0:T(8,128)S(1)} %bitcast.11), dimensions={1,2} | broadcast | bytes 2162688 | tf_op jit(solution)/shard_map/broadcast_in_dim | solution.py:369
  103.9 0.0 copy-start.1
  103.9 8.1 %all-to-all-start.3 = ((f32[32,128,128]{2,1,0:T(8,128)}), f32[32,128,128]{2,1,0:T(8,128)S(1)}, u32[]{:S(2)}, u32[]{:S(2)}) async-start(f32[32,128,128]{2,1,0:T(8,128)} %broadcast_in_dim.7), calls=%async_computation.3 | async-start | bytes 4194304 | tf_op jit(solution)/shard_map/all_to_all | solution.py:369
  112.0 0.0 copy-done.1
  112.0 0.0 copy-start.3
  112.0 1.1 copy-done.3
  113.1 0.0 copy-start.5
  113.1 1.0 copy-done.5
  114.1 4.9 %outputs.1 = (bf16[4,64,96]{2,1,0:T(8,128)(2,1)S(1)}, bf16[4,64,96]{2,1,0:T(8,128)(2,1)S(1)}) custom-call(s32[8]{0:T(128)S(1)} %reshape.45.slots, f32[2,8,8,8,128]{4,3,2,1,0:T(8,128)S(1)} %get-tuple-element.19.grid, bf16[1600,128]{1,0:T(8,128)(2,1)S(1)} %copy-done.5, bf16[27,96,96]{2,1,0:T(8,128)(2,1)S(1)} %copy-done.1, bf16[27,96,96]{2,1,0:T(8,128)(2,1)S(1)} %copy-done.3), custom_call_target="tpu_custom_call" | custom-call | flops 900000000 | bytes 4000000 | tf_op jit(solution)/shard_map/outputs/pallas_call | solution.py:325
  119.0 0.8 reshape.48
  119.8 0.8 reshape.49
  120.6 19.8 %all-to-all-done.3 = f32[32,128,128]{2,1,0:T(8,128)S(1)} async-done(((f32[32,128,128]{2,1,0:T(8,128)}), f32[32,128,128]{2,1,0:T(8,128)S(1)}, u32[]{:S(2)}, u32[]{:S(2)}) %all-to-all-start.3) | async-done | bytes 2097184 | tf_op jit(solution)/shard_map/all_to_all | solution.py:369
  140.4 1.8 %finish.1 = (f32[27,96,96]{2,1,0:T(8,128)}, f32[27,96,96]{2,1,0:T(8,128)}, f32[1,96]{1,0:T(1,128)}, f32[1,96]{1,0:T(1,128)}) custom-call(f32[4096,128]{1,0:T(8,128)S(1)} %bitcast.8), custom_call_target="tpu_custom_call" | custom-call | bytes 4000000 | tf_op jit(solution)/shard_map/finish/pallas_call | solution.py:345
  (3 shorter events, 0.1 us)
Async XLA Ops:
  3.9 12.1 %collective-permute-start = (bf16[256,128]{1,0:T(8,128)(2,1)S(1)}, bf16[256,128]{1,0:T(8,128)(2,1)S(1)}, u32[]{:S(2)}, u32[]{:S(2)}) collective-permute-start(bf16[256,128]{1,0:T(8,128)(2,1)S(1)} %get-tuple-element.20), channel_id=1, source_target_pairs={{0,16},{16,32},{32,48},{48,64},{64,80},{80,96},{96,112},{112,128},... | collective-permute-start | bytes 196616 | tf_op jit(solution)/shard_map/ppermute | solution.py:380
  14.1 9.5 %collective-permute-start.1 = (bf16[256,128]{1,0:T(8,128)(2,1)S(1)}, bf16[256,128]{1,0:T(8,128)(2,1)S(1)}, u32[]{:S(2)}, u32[]{:S(2)}) collective-permute-start(bf16[256,128]{1,0:T(8,128)(2,1)S(1)} %get-tuple-element.21), channel_id=1, source_target_pairs={{16,0},{32,16},{48,32},{64,48},{80,64},{96,80},{112,96},{128,112},... | collective-permute-start | bytes 196616 | tf_op jit(solution)/shard_map/ppermute | solution.py:380
  23.6 5.1 %collective-permute-start.2 = (bf16[384,128]{1,0:T(8,128)(2,1)S(1)}, bf16[384,128]{1,0:T(8,128)(2,1)S(1)}, u32[]{:S(2)}, u32[]{:S(2)}) collective-permute-start(bf16[384,128]{1,0:T(8,128)(2,1)S(1)} %get-tuple-element.22), channel_id=1, source_target_pairs={{0,1},{1,2},{2,3},{3,4},{4,5},{5,6},{6,7},{7,8},{8,9},{9,10},{10,1... | collective-permute-start | bytes 294920 | tf_op jit(solution)/shard_map/ppermute | solution.py:380
  26.7 5.4 %collective-permute-start.3 = (bf16[384,128]{1,0:T(8,128)(2,1)S(1)}, bf16[384,128]{1,0:T(8,128)(2,1)S(1)}, u32[]{:S(2)}, u32[]{:S(2)}) collective-permute-start(bf16[384,128]{1,0:T(8,128)(2,1)S(1)} %get-tuple-element.23), channel_id=1, source_target_pairs={{1,0},{2,1},{3,2},{4,3},{5,4},{6,5},{7,6},{8,7},{9,8},{10,9},{11,1... | collective-permute-start | bytes 294920 | tf_op jit(solution)/shard_map/ppermute | solution.py:380
  32.1 1.1 copy-start
  33.2 1.1 copy-start.2
  39.8 25.7 %copy-start.4 = (bf16[1600,128]{1,0:T(8,128)(2,1)}, bf16[1600,128]{1,0:T(8,128)(2,1)S(1)}, u32[]{:S(2)}) copy-start(bf16[1600,128]{1,0:T(8,128)(2,1)S(1)} %get-tuple-element.24.inner) | copy-start | bytes 1228804
  103.9 8.1 %copy-start.1 = (bf16[27,96,96]{2,1,0:T(8,128)(2,1)S(1)}, bf16[27,96,96]{2,1,0:T(8,128)(2,1)}, u32[]{:S(2)}) copy-start(bf16[27,96,96]{2,1,0:T(8,128)(2,1)} %weight_one.3) | copy-start | bytes 1492996
  103.9 36.5 %all-to-all-start.3 = ((f32[32,128,128]{2,1,0:T(8,128)}), f32[32,128,128]{2,1,0:T(8,128)S(1)}, u32[]{:S(2)}, u32[]{:S(2)}) async-start(f32[32,128,128]{2,1,0:T(8,128)} %broadcast_in_dim.7), calls=%async_computation.3 | async-start | bytes 4194304 | tf_op jit(solution)/shard_map/all_to_all | solution.py:369
  112.0 1.1 copy-start.3
  113.1 1.0 copy-start.5

commit v2 on v1

--- a/solution.py
+++ b/solution.py
@@ -52,7 +52,7 @@
             for j in range(2):
                 tiles, marks = [], []
                 for k in range(2):
-                    slot = slots[(i * 2 + j) * 2 + k]
+                    slot = slots[0, 0, i, j, k]
                     filled = (slot < count).astype(F32)
                     brick = source[jnp.minimum(slot, count - 1)].astype(F32) * filled
                     tiles.append(brick.reshape(8, 8, C))
@@ -129,6 +129,18 @@
         columns_ref[0:C, tap * LANES : tap * LANES + C] = kernel[TAPS - 1 - tap]
 
 
+def prepare_kernel(
+    weight_one, weight_two, gain, bias, rows_one, columns_two, rows_two, columns_one, gain_bias
+):
+    spread(weight_one, rows_one)
+    spread(weight_two, rows_two)
+    spread_flipped(weight_one, columns_one)
+    spread_flipped(weight_two, columns_two)
+    gain_bias[...] = jnp.zeros_like(gain_bias)
+    gain_bias[0:1, 0:C] = gain[...]
+    gain_bias[1:2, 0:C] = bias[...]
+
+
 def plain_dot(left, right):
     return jnp.dot(left, right, preferred_element_type=F32)
 
@@ -142,9 +154,9 @@
 
 
 def gradient_kernel(
-    grid, below, above, left, right, weight_one, weight_two, gain_bias,
+    grid, below, above, left, right, rows_ref, columns_ref, gain_bias,
     result, inner,
-    field_ref, stack_ref, windows, rows_ref, columns_ref, terms_one, terms_two, packed,
+    field_ref, stack_ref, windows, terms_one, terms_two, packed,
 ):
     lower = opened(below[...], (2, 2, SIDE))
     upper = opened(above[...], (2, 2, SIDE))
@@ -159,8 +171,6 @@
         field_ref[:, SIDE + 2 : SIDE + 4] = to_right[field]
 
     gain, bias = gain_bias[0:1], gain_bias[1:2]
-    spread(weight_one, rows_ref)
-    spread_flipped(weight_two, columns_ref)
     load_field(0)
     mark = field_ref[1 : SIDE + 3, 1 : SIDE + 3].reshape(RIM, LANES)[:, C : C + 1]
     stack_ref[...] = with_neighbours(field_ref[...])
@@ -213,20 +223,20 @@
     packed[39 * C : 40 * C] = term(52)
     packed[40 * C : 41 * C] = term(53)
     packed[41 * C : ROWS] = jnp.zeros((ROWS - 41 * C, LANES), F32)
-    packed[41 * C : 41 * C + 1] = gain_term
-    packed[41 * C + 1 : 41 * C + 2] = bias_term
+    for spot, value in enumerate((gain_term, bias_term)):
+        base = 41 * C + 2 * spot
+        packed[base : base + 1] = rounded(value)
+        packed[base + 1 : base + 2] = value - rounded(value)
     result[...] = packed[...].astype(BF16)
 
 
 def output_kernel(
-    slots, grid, inner, weight_one, weight_two, out, grad,
-    stack_ref, windows, rows_ref, columns_ref,
+    slots, grid, inner, rows_ref, columns_ref, out, grad,
+    stack_ref, windows,
 ):
     count = out.shape[0]
     out[...] = jnp.zeros_like(out)
     grad[...] = jnp.zeros_like(grad)
-    spread(weight_two, rows_ref)
-    spread_flipped(weight_one, columns_ref)
     for field, target in enumerate((out, grad)):
         lead = inner[field * RIM : field * RIM + RIM].astype(F32)
         stack_ref[...] = with_neighbours(lead.reshape(SIDE + 2, SIDE + 2, SIDE, LANES))
@@ -247,7 +257,7 @@
                     jnp.where(is_low, rotated(even, 4), odd),
                 )
                 for k in range(2):
-                    slot = slots[(i * 2 + j) * 2 + k]
+                    slot = slots[0, 0, i, j, k]
                     brick = tiles[k].reshape(64, LANES)[:, 0:C].astype(BF16)
 
                     @pl.when(slot < count)
@@ -255,7 +265,11 @@
                         target[slot] = brick
 
 
-def finish_kernel(scale, total, grad_one, grad_two, grad_gain, grad_bias):
+def finish_kernel(scale, side, mine, other, grad_one, grad_two, grad_gain, grad_bias, total):
+    half = ROWS // 2
+    at = pl.multiple_of(side[0] * half, half)
+    total[pl.ds(at, half)] = mine[...]
+    total[pl.ds(half - at, half)] = other[...]
     lane = lax.broadcasted_iota(jnp.int32, (C, LANES), 1)
 
     def put(index, value):
@@ -270,8 +284,9 @@
         put(4 * group + 3, jnp.where(lane < 32, moved[0], jnp.where(lane < 64, moved[1], moved[2])))
     put(52, total[39 * C : 40 * C])
     put(53, total[40 * C : 41 * C])
-    grad_gain[...] = total[41 * C : 41 * C + 1, 0:C] * scale
-    grad_bias[...] = total[41 * C + 1 : 41 * C + 2, 0:C] * scale
+    for spot, target in enumerate((grad_gain, grad_bias)):
+        base = 41 * C + 2 * spot
+        target[...] = (total[base : base + 1, 0:C] + total[base + 1 : base + 2, 0:C]) * scale
 
 
 def shape(dims, dtype):
@@ -298,7 +313,7 @@
     )(grid, below, above)
 
 
-def gradients(grid, halos, weight_one, weight_two, gain_bias):
+def gradients(grid, halos, rows, columns, gain_bias):
     return call(
         gradient_kernel,
         (shape((ROWS, LANES), BF16), shape((2 * RIM, LANES), BF16)),
@@ -307,8 +322,6 @@
             pltpu.VMEM((SIDE + 4, SIDE + 4, SIDE, LANES), F32),
             pltpu.VMEM((SIDE + 4, SIDE + 4, SIDE, 3 * LANES), F32),
             pltpu.VMEM((RIM, SPAN), BF16),
-            pltpu.VMEM((SPAN, LANES), BF16),
-            pltpu.VMEM((LANES, SPAN), BF16),
             pltpu.VMEM((LANES, SPAN), F32),
             pltpu.VMEM((LANES, SPAN), F32),
             pltpu.VMEM((ROWS, LANES), F32),
@@ -317,10 +330,10 @@
         moved=8_000_000,
         name="gradients",
         room=36,
-    )(grid, *halos, weight_one, weight_two, gain_bias)
-
-
-def outputs(slots, grid, inner, weight_one, weight_two):
+    )(grid, *halos, rows, columns, gain_bias)
+
+
+def outputs(slots, grid, inner, rows, columns):
     result = shape((4, 64, C), BF16)
     return call(
         output_kernel,
@@ -329,49 +342,59 @@
         scratch=[
             pltpu.VMEM((SIDE + 2, SIDE + 2, SIDE, 3 * LANES), F32),
             pltpu.VMEM((OWN, SPAN), BF16),
-            pltpu.VMEM((SPAN, LANES), BF16),
-            pltpu.VMEM((LANES, SPAN), BF16),
         ],
         flops=900_000_000,
         moved=4_000_000,
         name="outputs",
         room=24,
-    )(slots, grid, inner, weight_one, weight_two)
-
-
-def finish(total, scale):
+    )(slots, grid, inner, rows, columns)
+
+
+def finish(side, mine, other, scale):
     grads = shape((TAPS, C, C), F32)
     line = shape((1, C), F32)
     return call(
         functools.partial(finish_kernel, scale),
         (grads, grads, line, line),
-        [VMEM_SPEC],
+        [SMEM_SPEC, VMEM_SPEC, VMEM_SPEC],
+        scratch=[pltpu.VMEM((ROWS, LANES), F32)],
         moved=4_000_000,
         name="finish",
-    )(total)
-
-
-SIZES = dict(y=4, zh=4, core=2, zl=4, x=4)
-PLANE = ("core", "y", "x")
+    )(side, mine, other)
+
+
+def prepare(weight_one, weight_two, gain, bias):
+    rows, columns = shape((SPAN, LANES), BF16), shape((LANES, SPAN), BF16)
+    return call(
+        prepare_kernel,
+        (rows, columns, rows, columns, shape((2, LANES), F32)),
+        [VMEM_SPEC] * 4,
+        moved=6_000_000,
+        name="prepare",
+    )(weight_one, weight_two, gain.reshape(1, C), bias.reshape(1, C))
+
+
+SIZES = dict(y=4, zh=4, core=2, zl=2, zp=2, x=4)
+PLANE = ("y", "x", "zp")
 LINE = ("zh", "zl")
 
 
+def spread_out(block, axes):
+    copies = jnp.broadcast_to(block, (lax.axis_size(axes),) + block.shape)
+    return lax.all_to_all(copies, axes, 0, 0)
+
+
 def reduce_all(packed):
-    plane, line = lax.axis_size(PLANE), lax.axis_size(LINE)
-    rows = ROWS // plane
-    parts = packed.reshape(plane, rows, LANES)
-    parts = lax.all_to_all(parts, PLANE, 0, 0)
+    group = ("core",) + PLANE
+    rows = ROWS // lax.axis_size(group)
+    parts = lax.all_to_all(packed.reshape(-1, rows, LANES), group, 0, 0)
     chunk = jnp.sum(parts.astype(F32), axis=0)
-    pieces = lax.all_to_all(chunk.reshape(line, rows // line, LANES), LINE, 0, 0)
-    piece = jnp.sum(pieces, axis=0)
-    chunk = lax.all_to_all(jnp.broadcast_to(piece, pieces.shape), LINE, 0, 0)
-    chunk = chunk.reshape(rows, LANES)
-    total = lax.all_to_all(jnp.broadcast_to(chunk, parts.shape), PLANE, 0, 0)
-    return total.reshape(ROWS, LANES)
+    chunk = jnp.sum(spread_out(chunk, LINE), axis=0)
+    return spread_out(chunk, PLANE).reshape(ROWS // 2, LANES)
 
 
 GX = ("y", "zh", "core")
-GY = ("zl", "x")
+GY = ("zl", "zp", "x")
 
 
 def passed_along(block, axis, distance):
@@ -381,24 +404,25 @@
 
 
 def body(features, cotangent, brick_slot, weight_one, weight_two, gain, bias):
-    slots = brick_slot.reshape(-1)
     source = features.reshape(4, 64, C)
     upstream = cotangent.reshape(4, 64, C)
-    padded = jnp.pad(jnp.stack([gain, bias]), ((0, 0), (0, LANES - C)))
-    grid, low, high = dense_parts(source, upstream, slots)
+    rows_one, columns_two, rows_two, columns_one, gain_bias = prepare(weight_one, weight_two, gain, bias)
+    grid, low, high = dense_parts(source, upstream, brick_slot)
     below = passed_along(high, GX, 1)
     above = passed_along(low, GX, -1)
     low, high = rims(grid, below, above)
     left = passed_along(high, GY, 1)
     right = passed_along(low, GY, -1)
-    packed, inner = gradients(grid, (below, above, left, right), weight_one, weight_two, padded)
-    out, grad = outputs(slots, grid, inner, weight_one, weight_two)
-    total = reduce_all(packed)
+    packed, inner = gradients(grid, (below, above, left, right), rows_one, columns_two, gain_bias)
+    out, grad = outputs(brick_slot, grid, inner, rows_two, columns_one)
+    out, grad = out.reshape(features.shape), grad.reshape(features.shape)
+    mine, out, grad = lax.optimization_barrier((reduce_all(packed), out, grad))
+    other = lax.ppermute(mine, "core", [(0, 1), (1, 0)])
     scale = 1.0 / math.sqrt(lax.axis_size(GX) * lax.axis_size(GY) * 256)
-    grad_one, grad_two, grad_gain, grad_bias = finish(total, scale)
+    grad_one, grad_two, grad_gain, grad_bias = finish(lax.axis_index("core").reshape(1), mine, other, scale)
     return (
-        out.reshape(features.shape),
-        grad.reshape(features.shape),
+        out,
+        grad,
         grad_one,
         grad_two,
         grad_gain.reshape(gain.shape),

time: 143 us -> 126 us (0.88)
  waiting for transfers between devices: 30.7 us -> 19.5 us
  blocking collectives: 62.3 us -> 54.1 us
  starting transfers between devices: 24.6 us -> 29.1 us
    all_to_all x1, waiting for transfers between devices: 19.8 us -> 8.87 us  [spread_out(): return lax.all_to_all(copies, axes, 0, 0)]
    all_to_all x3 -> x2, blocking collectives: 62.3 us -> 54.1 us  [the longest x1 28 us: reduce_all(): parts = lax.all_to_all(packed.reshape(-1, rows, LANES), group, 0, 0)]
    ppermute x0 -> x1, starting transfers between devices: none -> 4.74 us  [body(): other = lax.ppermute(mine, 'core', [(0, 1), (1, 0)])]
    ppermute x4, waiting for transfers between devices: 10.9 us -> 8.4 us  [passed_along(): return lax.ppermute(block, axis, route)]
    ppermute x0 -> x1, waiting for transfers between devices: none -> 2.26 us  [body(): other = lax.ppermute(mine, 'core', [(0, 1), (1, 0)])]
    unnamed x12 -> x16, local copies, waits for them, and re-layouts: 4.28 us -> 4.09 us
  transfers between devices with their start and end apart: 5 -> 6, of which waited for: 3 -> 4; matrix products, arithmetic and copies ran while one was open for 2% -> 1% of each run, Pallas kernels for 3% -> 4%
where the time goes in v2:
time: 126 us; the launch traced here: 125 us
  blocking collectives  54.1 us (43%)
  starting transfers between devices  29.1 us (23%)
  waiting for transfers between devices  19.5 us (15%)
  Pallas kernels  13.1 us (10%)
  local copies, waits for them, and re-layouts  8.62 us (7%)
    all_to_all x1, blocking collectives, reduce_all(): parts = lax.all_to_all(packed.reshape(-1, rows, LANES), group, 0, 0)  28 us
    all_to_all x1, blocking collectives, spread_out(): return lax.all_to_all(copies, axes, 0, 0)  26.1 us
    ppermute x4, starting transfers between devices, passed_along(): return lax.ppermute(block, axis, route)  16.5 us
    all_to_all x1, waiting for transfers between devices, spread_out(): return lax.all_to_all(copies, axes, 0, 0)  8.87 us
    ppermute x4, waiting for transfers between devices, passed_along(): return lax.ppermute(block, axis, route)  8.4 us
    all_to_all x1, starting transfers between devices, spread_out(): return lax.all_to_all(copies, axes, 0, 0)  7.79 us
    pallas_call x1, Pallas kernels, gradients(): call(gradient_kernel, (shape((ROWS, LANES), BF16), shape((2 * RIM, LANES)...  5.11 us
    ppermute x1, starting transfers between devices, body(): other = lax.ppermute(mine, 'core', [(0, 1), (1, 0)])  4.74 us
  transfers between devices with their start and end apart: 6, of which 4 were waited for; matrix products, arithmetic and copies ran while one was open for 1% of the time, Pallas kernels for 4%

profile of v2, /device:TPU:1, one launch (start us, length us, event | category | flops | bytes accessed | tf_op | source)
XLA Modules:
  0.0 125.4 jit_solution(11874388158977507227)
XLA Ops:
  0.6 0.0 copy-start
  0.6 1.0 reshape.45.features
  1.6 0.9 reshape.46.cotangent
  2.5 0.0 copy-start.2
  2.5 0.7 copy-done.2
  3.2 0.7 dense_grid.1
  3.9 10.2 %collective-permute-start = (bf16[256,128]{1,0:T(8,128)(2,1)S(1)}, bf16[256,128]{1,0:T(8,128)(2,1)S(1)}, u32[]{:S(2)}, u32[]{:S(2)}) collective-permute-start(bf16[256,128]{1,0:T(8,128)(2,1)S(1)} %get-tuple-element.28), channel_id=1, source_target_pairs={{0,16},{16,32},{32,48},{48,64},{64,80},{80,96},{96,112},{112,128},... | collective-permute-start | bytes 196616 | tf_op jit(solution)/shard_map/ppermute | solution.py:403
  14.1 1.9 %collective-permute-start.1 = (bf16[256,128]{1,0:T(8,128)(2,1)S(1)}, bf16[256,128]{1,0:T(8,128)(2,1)S(1)}, u32[]{:S(2)}, u32[]{:S(2)}) collective-permute-start(bf16[256,128]{1,0:T(8,128)(2,1)S(1)} %get-tuple-element.29), channel_id=1, source_target_pairs={{16,0},{32,16},{48,32},{64,48},{80,64},{96,80},{112,96},{128,112},... | collective-permute-start | bytes 196616 | tf_op jit(solution)/shard_map/ppermute | solution.py:403
  16.0 0.0 collective-permute-done.below
  16.0 7.6 %collective-permute-done.1.above = bf16[256,128]{1,0:T(8,128)(2,1)S(1)} collective-permute-done((bf16[256,128]{1,0:T(8,128)(2,1)S(1)}, bf16[256,128]{1,0:T(8,128)(2,1)S(1)}, u32[]{:S(2)}, u32[]{:S(2)}) %collective-permute-start.1) | collective-permute-done | bytes 65568 | tf_op jit(solution)/shard_map/ppermute | solution.py:403
  23.6 3.1 %collective-permute-start.2 = (bf16[384,128]{1,0:T(8,128)(2,1)S(1)}, bf16[384,128]{1,0:T(8,128)(2,1)S(1)}, u32[]{:S(2)}, u32[]{:S(2)}) collective-permute-start(bf16[384,128]{1,0:T(8,128)(2,1)S(1)} %get-tuple-element.30), channel_id=1, source_target_pairs={{0,1},{1,2},{2,3},{3,4},{4,5},{5,6},{6,7},{7,8},{8,9},{9,10},{10,1... | collective-permute-start | bytes 294920 | tf_op jit(solution)/shard_map/ppermute | solution.py:403
  26.7 1.3 %collective-permute-start.3 = (bf16[384,128]{1,0:T(8,128)(2,1)S(1)}, bf16[384,128]{1,0:T(8,128)(2,1)S(1)}, u32[]{:S(2)}, u32[]{:S(2)}) collective-permute-start(bf16[384,128]{1,0:T(8,128)(2,1)S(1)} %get-tuple-element.31), channel_id=1, source_target_pairs={{1,0},{2,1},{3,2},{4,3},{5,4},{6,5},{7,6},{8,7},{9,8},{10,9},{11,1... | collective-permute-start | bytes 294920 | tf_op jit(solution)/shard_map/ppermute | solution.py:403
  28.0 0.0 copy-done
  28.0 0.0 copy-start.1
  28.1 1.1 copy-done.1
  29.1 0.0 copy-start.4
  29.1 0.7 copy-done.4
  29.8 0.0 copy-start.5
  29.8 0.7 copy-done.5
  30.5 0.8 prepare.1
  31.2 0.0 collective-permute-done.2.left
  31.3 0.8 collective-permute-done.3.right
  32.1 5.1 %gradients.1 = (bf16[4096,128]{1,0:T(8,128)(2,1)S(1)}, bf16[1600,128]{1,0:T(8,128)(2,1)S(1)}) custom-call(f32[2,8,8,8,128]{4,3,2,1,0:T(8,128)S(1)} %get-tuple-element.27.grid, bf16[256,128]{1,0:T(8,128)(2,1)S(1)} %collective-permute-done.below, bf16[256,128]{1,0:T(8,128)(2,1)S(1)} %collective-permute-done.1.above, ...), custom_call_target="tpu_custom_call" | custom-call | flops 2400000000 | bytes 8000000 | tf_op jit(solution)/shard_map/gradients/pallas_call | solution.py:317
  37.2 0.0 copy-start.6
  37.2 28.0 %all_to_all.15 = bf16[64,64,128]{2,1,0:T(8,128)(2,1)S(1)} all-to-all(bf16[64,64,128]{2,1,0:T(8,128)(2,1)S(1)} %bitcast.9), channel_id=1, replica_groups=mesh['y'=4,'zh'=4,'core'=2,'zl'=2,'zp'=2,'x'=4] {'core','y','x','zp'}, dimensions={0} | all-to-all | bytes 2097152 | tf_op jit(solution)/shard_map/all_to_all | solution.py:390
  65.2 0.2 convert_reduce_fusion
  65.4 0.0 copy-done.6
  65.4 26.1 %all_to_all.16 = f32[8,64,128]{2,1,0:T(8,128)S(1)} all-to-all(f32[8,64,128]{2,1,0:T(8,128)S(1)} %broadcast_in_dim.6), channel_id=1, replica_groups=mesh['y'=4,'zh'=4,'core'=2,'zl'=2,'zp'=2,'x'=4] {'zh','zl'}, dimensions={0} | all-to-all | bytes 524288 | tf_op jit(solution)/shard_map/all_to_all | solution.py:384
  91.6 0.0 copy-start.3
  91.6 1.1 broadcast_in_dim.7
  92.7 7.8 %all-to-all-start.2 = ((f32[32,64,128]{2,1,0:T(8,128)}), f32[32,64,128]{2,1,0:T(8,128)S(1)}, u32[]{:S(2)}, u32[]{:S(2)}) async-start(f32[32,64,128]{2,1,0:T(8,128)} %broadcast_in_dim.7), calls=%async_computation.2 | async-start | bytes 2097152 | tf_op jit(solution)/shard_map/all_to_all | solution.py:384
  100.5 0.0 copy-done.3
  100.5 0.0 copy-start.7
  100.5 1.0 copy-done.7
  101.5 4.5 %outputs.1 = (bf16[4,64,96]{2,1,0:T(8,128)(2,1)S(1)}, bf16[4,64,96]{2,1,0:T(8,128)(2,1)S(1)}) custom-call(s32[1,1,2,2,2]{4,3,2,1,0:T(2,128)S(1)} %copy-done.3, f32[2,8,8,8,128]{4,3,2,1,0:T(8,128)S(1)} %get-tuple-element.27.grid, bf16[1600,128]{1,0:T(8,128)(2,1)S(1)} %copy-done.7, bf16[3456,128]{1,0:T(8,128)(2,1)S(1)} %get-tuple-element.37.rows_ref, ...), custom_call_target="tpu_custom_call" | custom-call | flops 900000000 | bytes 4000000 | tf_op jit(solution)/shard_map/outputs/pallas_call | solution.py:338
  106.0 0.8 reshape.51
  106.8 0.8 reshape.52
  107.6 8.9 %all-to-all-done.2 = f32[32,64,128]{2,1,0:T(8,128)S(1)} async-done(((f32[32,64,128]{2,1,0:T(8,128)}), f32[32,64,128]{2,1,0:T(8,128)S(1)}, u32[]{:S(2)}, u32[]{:S(2)}) %all-to-all-start.2) | async-done | bytes 1048608 | tf_op jit(solution)/shard_map/all_to_all | solution.py:384
  116.4 4.7 %collective-permute-start.4 = (f32[2048,128]{1,0:T(8,128)S(1)}, f32[2048,128]{1,0:T(8,128)S(1)}, u32[]{:S(2)}, u32[]{:S(2)}) collective-permute-start(f32[2048,128]{1,0:T(8,128)S(1)} %bitcast.7), channel_id=1, source_target_pairs={{0,16},{16,0},{1,17},{17,1},{2,18},{18,2},{3,19},{19,3},{4,20},{20... | collective-permute-start | bytes 3145736 | tf_op jit(solution)/shard_map/ppermute | solution.py:420
  121.2 2.3 %collective-permute-done.4.other = f32[2048,128]{1,0:T(8,128)S(1)} collective-permute-done((f32[2048,128]{1,0:T(8,128)S(1)}, f32[2048,128]{1,0:T(8,128)S(1)}, u32[]{:S(2)}, u32[]{:S(2)}) %collective-permute-start.4) | collective-permute-done | bytes 1048608 | tf_op jit(solution)/shard_map/ppermute | solution.py:420
  123.5 1.9 %finish.1 = (f32[27,96,96]{2,1,0:T(8,128)}, f32[27,96,96]{2,1,0:T(8,128)}, f32[1,96]{1,0:T(1,128)}, f32[1,96]{1,0:T(1,128)}) custom-call(s32[1]{0:T(128)} %bitcast.4.side, f32[2048,128]{1,0:T(8,128)S(1)} %bitcast.8, f32[2048,128]{1,0:T(8,128)S(1)} %collective-permute-done.4.other), custom_call_target="tpu_custom_call" | custom-call | bytes 4000000 | tf_op jit(solution)/shard_map/finish/pallas_call | solution.py:356
  (3 shorter events, 0.1 us)
Async XLA Ops:
  0.6 27.4 %copy-start = (bf16[27,96,96]{2,1,0:T(8,128)(2,1)S(1)}, bf16[27,96,96]{2,1,0:T(8,128)(2,1)}, u32[]{:S(2)}) copy-start(bf16[27,96,96]{2,1,0:T(8,128)(2,1)} %weight_one.1) | copy-start | bytes 1492996
  2.5 0.7 copy-start.2
  3.9 12.1 %collective-permute-start = (bf16[256,128]{1,0:T(8,128)(2,1)S(1)}, bf16[256,128]{1,0:T(8,128)(2,1)S(1)}, u32[]{:S(2)}, u32[]{:S(2)}) collective-permute-start(bf16[256,128]{1,0:T(8,128)(2,1)S(1)} %get-tuple-element.28), channel_id=1, source_target_pairs={{0,16},{16,32},{32,48},{48,64},{64,80},{80,96},{96,112},{112,128},... | collective-permute-start | bytes 196616 | tf_op jit(solution)/shard_map/ppermute | solution.py:403
  14.1 9.5 %collective-permute-start.1 = (bf16[256,128]{1,0:T(8,128)(2,1)S(1)}, bf16[256,128]{1,0:T(8,128)(2,1)S(1)}, u32[]{:S(2)}, u32[]{:S(2)}) collective-permute-start(bf16[256,128]{1,0:T(8,128)(2,1)S(1)} %get-tuple-element.29), channel_id=1, source_target_pairs={{16,0},{32,16},{48,32},{64,48},{80,64},{96,80},{112,96},{128,112},... | collective-permute-start | bytes 196616 | tf_op jit(solution)/shard_map/ppermute | solution.py:403
  23.6 7.6 %collective-permute-start.2 = (bf16[384,128]{1,0:T(8,128)(2,1)S(1)}, bf16[384,128]{1,0:T(8,128)(2,1)S(1)}, u32[]{:S(2)}, u32[]{:S(2)}) collective-permute-start(bf16[384,128]{1,0:T(8,128)(2,1)S(1)} %get-tuple-element.30), channel_id=1, source_target_pairs={{0,1},{1,2},{2,3},{3,4},{4,5},{5,6},{6,7},{7,8},{8,9},{9,10},{10,1... | collective-permute-start | bytes 294920 | tf_op jit(solution)/shard_map/ppermute | solution.py:403
  26.7 5.4 %collective-permute-start.3 = (bf16[384,128]{1,0:T(8,128)(2,1)S(1)}, bf16[384,128]{1,0:T(8,128)(2,1)S(1)}, u32[]{:S(2)}, u32[]{:S(2)}) collective-permute-start(bf16[384,128]{1,0:T(8,128)(2,1)S(1)} %get-tuple-element.31), channel_id=1, source_target_pairs={{1,0},{2,1},{3,2},{4,3},{5,4},{6,5},{7,6},{8,7},{9,8},{10,9},{11,1... | collective-permute-start | bytes 294920 | tf_op jit(solution)/shard_map/ppermute | solution.py:403
  28.0 1.1 copy-start.1
  29.1 0.7 copy-start.4
  29.8 0.7 copy-start.5
  37.2 28.1 %copy-start.6 = (bf16[1600,128]{1,0:T(8,128)(2,1)}, bf16[1600,128]{1,0:T(8,128)(2,1)S(1)}, u32[]{:S(2)}) copy-start(bf16[1600,128]{1,0:T(8,128)(2,1)S(1)} %get-tuple-element.36.inner) | copy-start | bytes 1228804
  91.6 8.9 %copy-start.3 = (s32[1,1,2,2,2]{4,3,2,1,0:T(2,128)S(1)}, s32[1,1,2,2,2]{4,3,2,1,0:T(2,128)}, u32[]{:S(2)}) copy-start(s32[1,1,2,2,2]{4,3,2,1,0:T(2,128)} %slots.3) | copy-start | bytes 100
  92.7 23.8 %all-to-all-start.2 = ((f32[32,64,128]{2,1,0:T(8,128)}), f32[32,64,128]{2,1,0:T(8,128)S(1)}, u32[]{:S(2)}, u32[]{:S(2)}) async-start(f32[32,64,128]{2,1,0:T(8,128)} %broadcast_in_dim.7), calls=%async_computation.2 | async-start | bytes 2097152 | tf_op jit(solution)/shard_map/all_to_all | solution.py:384
  100.5 1.0 copy-start.7
  116.4 7.0 %collective-permute-start.4 = (f32[2048,128]{1,0:T(8,128)S(1)}, f32[2048,128]{1,0:T(8,128)S(1)}, u32[]{:S(2)}, u32[]{:S(2)}) collective-permute-start(f32[2048,128]{1,0:T(8,128)S(1)} %bitcast.7), channel_id=1, source_target_pairs={{0,16},{16,0},{1,17},{17,1},{2,18},{18,2},{3,19},{19,3},{4,20},{20... | collective-permute-start | bytes 3145736 | tf_op jit(solution)/shard_map/ppermute | solution.py:420

commit v3 on v2

--- a/solution.py
+++ b/solution.py
@@ -265,11 +265,8 @@
                         target[slot] = brick
 
 
-def finish_kernel(scale, side, mine, other, grad_one, grad_two, grad_gain, grad_bias, total):
-    half = ROWS // 2
-    at = pl.multiple_of(side[0] * half, half)
-    total[pl.ds(at, half)] = mine[...]
-    total[pl.ds(half - at, half)] = other[...]
+def finish_kernel(scale, parts, grad_one, grad_two, grad_gain, grad_bias, total):
+    total[...] = parts[...].astype(F32)
     lane = lax.broadcasted_iota(jnp.int32, (C, LANES), 1)
 
     def put(index, value):
@@ -350,17 +347,17 @@
     )(slots, grid, inner, rows, columns)
 
 
-def finish(side, mine, other, scale):
+def finish(total, scale):
     grads = shape((TAPS, C, C), F32)
     line = shape((1, C), F32)
     return call(
         functools.partial(finish_kernel, scale),
         (grads, grads, line, line),
-        [SMEM_SPEC, VMEM_SPEC, VMEM_SPEC],
+        [VMEM_SPEC],
         scratch=[pltpu.VMEM((ROWS, LANES), F32)],
         moved=4_000_000,
         name="finish",
-    )(side, mine, other)
+    )(total)
 
 
 def prepare(weight_one, weight_two, gain, bias):
@@ -375,7 +372,7 @@
 
 
 SIZES = dict(y=4, zh=4, core=2, zl=2, zp=2, x=4)
-PLANE = ("y", "x", "zp")
+PLANE = ("core", "y", "x", "zp")
 LINE = ("zh", "zl")
 
 
@@ -385,12 +382,11 @@
 
 
 def reduce_all(packed):
-    group = ("core",) + PLANE
-    rows = ROWS // lax.axis_size(group)
-    parts = lax.all_to_all(packed.reshape(-1, rows, LANES), group, 0, 0)
+    rows = ROWS // lax.axis_size(PLANE)
+    parts = lax.all_to_all(packed.reshape(-1, rows, LANES), PLANE, 0, 0)
     chunk = jnp.sum(parts.astype(F32), axis=0)
     chunk = jnp.sum(spread_out(chunk, LINE), axis=0)
-    return spread_out(chunk, PLANE).reshape(ROWS // 2, LANES)
+    return spread_out(chunk.astype(BF16), PLANE).reshape(ROWS, LANES)
 
 
 GX = ("y", "zh", "core")
@@ -406,20 +402,22 @@
 def body(features, cotangent, brick_slot, weight_one, weight_two, gain, bias):
     source = features.reshape(4, 64, C)
     upstream = cotangent.reshape(4, 64, C)
-    rows_one, columns_two, rows_two, columns_one, gain_bias = prepare(weight_one, weight_two, gain, bias)
     grid, low, high = dense_parts(source, upstream, brick_slot)
+    low, high, *parameters = lax.optimization_barrier((low, high, weight_one, weight_two, gain, bias))
     below = passed_along(high, GX, 1)
     above = passed_along(low, GX, -1)
+    prepared = prepare(*parameters)
+    below, above, prepared = lax.optimization_barrier((below, above, prepared))
+    rows_one, columns_two, rows_two, columns_one, gain_bias = prepared
     low, high = rims(grid, below, above)
     left = passed_along(high, GY, 1)
     right = passed_along(low, GY, -1)
     packed, inner = gradients(grid, (below, above, left, right), rows_one, columns_two, gain_bias)
     out, grad = outputs(brick_slot, grid, inner, rows_two, columns_one)
     out, grad = out.reshape(features.shape), grad.reshape(features.shape)
-    mine, out, grad = lax.optimization_barrier((reduce_all(packed), out, grad))
-    other = lax.ppermute(mine, "core", [(0, 1), (1, 0)])
+    total = reduce_all(packed)
     scale = 1.0 / math.sqrt(lax.axis_size(GX) * lax.axis_size(GY) * 256)
-    grad_one, grad_two, grad_gain, grad_bias = finish(lax.axis_index("core").reshape(1), mine, other, scale)
+    grad_one, grad_two, grad_gain, grad_bias = finish(total, scale)
     return (
         out,
         grad,

time: 126 us -> 124 us (0.984)
  starting transfers between devices: 29.1 us -> 26.5 us
  waiting for transfers between devices: 19.5 us -> 17.1 us
  blocking collectives: 54.1 us -> 55.6 us
    ppermute x1 -> x0, starting transfers between devices: 4.74 us -> none  [body(): other = lax.ppermute(mine, 'core', [(0, 1), (1, 0)])]
    ppermute x1 -> x0, waiting for transfers between devices: 2.26 us -> none  [body(): other = lax.ppermute(mine, 'core', [(0, 1), (1, 0)])]
    all_to_all x1, starting transfers between devices: 7.79 us -> 9.94 us  [spread_out(): return lax.all_to_all(copies, axes, 0, 0)]
    all_to_all x1, blocking collectives: 26.1 us -> 27.4 us  [spread_out(): return lax.all_to_all(copies, axes, 0, 0)]
  transfers between devices with their start and end apart: 6 -> 5, of which waited for: 4 -> 4; matrix products, arithmetic and copies ran while one was open for 1% -> 1% of each run, Pallas kernels for 4% -> 4%
where the time goes in v3:
time: 124 us; the launch traced here: 123 us
  blocking collectives  55.6 us (45%)
  starting transfers between devices  26.5 us (21%)
  waiting for transfers between devices  17.1 us (14%)
  Pallas kernels  12.9 us (10%)
  local copies, waits for them, and re-layouts  9.78 us (8%)
    all_to_all x1, blocking collectives, reduce_all(): parts = lax.all_to_all(packed.reshape(-1, rows, LANES), PLANE, 0, 0)  28.2 us
    all_to_all x1, blocking collectives, spread_out(): return lax.all_to_all(copies, axes, 0, 0)  27.4 us
    ppermute x4, starting transfers between devices, passed_along(): return lax.ppermute(block, axis, route)  16.5 us
    all_to_all x1, starting transfers between devices, spread_out(): return lax.all_to_all(copies, axes, 0, 0)  9.94 us
    all_to_all x1, waiting for transfers between devices, spread_out(): return lax.all_to_all(copies, axes, 0, 0)  9.8 us
    ppermute x4, waiting for transfers between devices, passed_along(): return lax.ppermute(block, axis, route)  7.33 us
    unnamed x16, local copies, waits for them, and re-layouts  5.17 us
    pallas_call x1, Pallas kernels, gradients(): call(gradient_kernel, (shape((ROWS, LANES), BF16), shape((2 * RIM, LANES)...  5.11 us
  transfers between devices with their start and end apart: 5, of which 4 were waited for; matrix products, arithmetic and copies ran while one was open for 1% of the time, Pallas kernels for 4%

profile of v3, /device:TPU:1, one launch (start us, length us, event | category | flops | bytes accessed | tf_op | source)
XLA Modules:
  0.0 122.9 jit_solution(12078203979244597709)
XLA Ops:
  0.6 0.9 reshape.42.features
  1.5 0.9 reshape.43.cotangent
  2.5 0.0 copy-start.2
  2.5 0.7 copy-done.2
  3.1 0.7 dense_grid.1
  3.8 10.2 %collective-permute-start = (bf16[256,128]{1,0:T(8,128)(2,1)S(1)}, bf16[256,128]{1,0:T(8,128)(2,1)S(1)}, u32[]{:S(2)}, u32[]{:S(2)}) collective-permute-start(bf16[256,128]{1,0:T(8,128)(2,1)S(1)} %get-tuple-element.40), channel_id=1, source_target_pairs={{0,16},{16,32},{32,48},{48,64},{64,80},{80,96},{96,112},{112,128},... | collective-permute-start | bytes 196616 | tf_op jit(solution)/shard_map/ppermute | solution.py:399
  14.0 1.9 %collective-permute-start.1 = (bf16[256,128]{1,0:T(8,128)(2,1)S(1)}, bf16[256,128]{1,0:T(8,128)(2,1)S(1)}, u32[]{:S(2)}, u32[]{:S(2)}) collective-permute-start(bf16[256,128]{1,0:T(8,128)(2,1)S(1)} %get-tuple-element.41), channel_id=1, source_target_pairs={{16,0},{32,16},{48,32},{64,48},{80,64},{96,80},{112,96},{128,112},... | collective-permute-start | bytes 196616 | tf_op jit(solution)/shard_map/ppermute | solution.py:399
  15.9 0.0 copy-start
  16.0 1.1 copy-done
  17.0 0.0 copy-start.1
  17.0 1.1 copy-done.1
  18.1 0.0 copy-start.4
  18.1 0.7 copy-done.4
  18.8 0.0 copy-start.5
  18.8 0.7 copy-done.5
  19.4 0.8 prepare.1
  20.2 0.0 collective-permute-done.below
  20.2 3.3 %collective-permute-done.1.above = bf16[256,128]{1,0:T(8,128)(2,1)S(1)} collective-permute-done((bf16[256,128]{1,0:T(8,128)(2,1)S(1)}, bf16[256,128]{1,0:T(8,128)(2,1)S(1)}, u32[]{:S(2)}, u32[]{:S(2)}) %collective-permute-start.1) | collective-permute-done | bytes 65568 | tf_op jit(solution)/shard_map/ppermute | solution.py:399
  23.5 3.1 %collective-permute-start.2 = (bf16[384,128]{1,0:T(8,128)(2,1)S(1)}, bf16[384,128]{1,0:T(8,128)(2,1)S(1)}, u32[]{:S(2)}, u32[]{:S(2)}) collective-permute-start(bf16[384,128]{1,0:T(8,128)(2,1)S(1)} %get-tuple-element.53), channel_id=1, source_target_pairs={{0,1},{1,2},{2,3},{3,4},{4,5},{5,6},{6,7},{7,8},{8,9},{9,10},{10,1... | collective-permute-start | bytes 294920 | tf_op jit(solution)/shard_map/ppermute | solution.py:399
  26.7 1.3 %collective-permute-start.3 = (bf16[384,128]{1,0:T(8,128)(2,1)S(1)}, bf16[384,128]{1,0:T(8,128)(2,1)S(1)}, u32[]{:S(2)}, u32[]{:S(2)}) collective-permute-start(bf16[384,128]{1,0:T(8,128)(2,1)S(1)} %get-tuple-element.54), channel_id=1, source_target_pairs={{1,0},{2,1},{3,2},{4,3},{5,4},{6,5},{7,6},{8,7},{9,8},{10,9},{11,1... | collective-permute-start | bytes 294920 | tf_op jit(solution)/shard_map/ppermute | solution.py:399
  28.0 0.3 collective-permute-done.2.left
  28.3 3.7 %collective-permute-done.3.right = bf16[384,128]{1,0:T(8,128)(2,1)S(1)} collective-permute-done((bf16[384,128]{1,0:T(8,128)(2,1)S(1)}, bf16[384,128]{1,0:T(8,128)(2,1)S(1)}, u32[]{:S(2)}, u32[]{:S(2)}) %collective-permute-start.3) | collective-permute-done | bytes 98336 | tf_op jit(solution)/shard_map/ppermute | solution.py:399
  32.0 5.1 %gradients.1 = (bf16[4096,128]{1,0:T(8,128)(2,1)S(1)}, bf16[1600,128]{1,0:T(8,128)(2,1)S(1)}) custom-call(f32[2,8,8,8,128]{4,3,2,1,0:T(8,128)S(1)} %get-tuple-element.37.grid, bf16[256,128]{1,0:T(8,128)(2,1)S(1)} %collective-permute-done.below, bf16[256,128]{1,0:T(8,128)(2,1)S(1)} %collective-permute-done.1.above, ...), custom_call_target="tpu_custom_call" | custom-call | flops 2400000000 | bytes 8000000 | tf_op jit(solution)/shard_map/gradients/pallas_call | solution.py:314
  37.1 0.0 copy-start.6
  37.2 28.2 %all_to_all.15 = bf16[64,64,128]{2,1,0:T(8,128)(2,1)S(1)} all-to-all(bf16[64,64,128]{2,1,0:T(8,128)(2,1)S(1)} %bitcast.7), channel_id=1, replica_groups=mesh['y'=4,'zh'=4,'core'=2,'zl'=2,'zp'=2,'x'=4] {'core','y','x','zp'}, dimensions={0} | all-to-all | bytes 2097152 | tf_op jit(solution)/shard_map/all_to_all | solution.py:386
  65.3 0.2 convert_reduce_fusion
  65.5 0.0 copy-done.6
  65.5 27.4 %all_to_all.16 = f32[8,64,128]{2,1,0:T(8,128)S(1)} all-to-all(f32[8,64,128]{2,1,0:T(8,128)S(1)} %broadcast_in_dim.6), channel_id=1, replica_groups=mesh['y'=4,'zh'=4,'core'=2,'zl'=2,'zp'=2,'x'=4] {'zh','zl'}, dimensions={0} | all-to-all | bytes 524288 | tf_op jit(solution)/shard_map/all_to_all | solution.py:381
  93.0 0.0 copy-start.3
  93.0 1.2 broadcast_in_dim.7
  94.2 9.9 %all-to-all-start.2 = ((bf16[64,64,128]{2,1,0:T(8,128)(2,1)}), bf16[64,64,128]{2,1,0:T(8,128)(2,1)S(1)}, u32[]{:S(2)}, u32[]{:S(2)}) async-start(bf16[64,64,128]{2,1,0:T(8,128)(2,1)} %broadcast_in_dim.7), calls=%async_computation.2 | async-start | bytes 2097152 | tf_op jit(solution)/shard_map/all_to_all | solution.py:381
  104.2 0.0 copy-done.3
  104.2 0.0 copy-start.7
  104.2 1.0 copy-done.7
  105.2 4.6 %outputs.1 = (bf16[4,64,96]{2,1,0:T(8,128)(2,1)S(1)}, bf16[4,64,96]{2,1,0:T(8,128)(2,1)S(1)}) custom-call(s32[1,1,2,2,2]{4,3,2,1,0:T(2,128)S(1)} %copy-done.3, f32[2,8,8,8,128]{4,3,2,1,0:T(8,128)S(1)} %get-tuple-element.37.grid, bf16[1600,128]{1,0:T(8,128)(2,1)S(1)} %copy-done.7, bf16[3456,128]{1,0:T(8,128)(2,1)S(1)} %get-tuple-element.59.rows_ref, ...), custom_call_target="tpu_custom_call" | custom-call | flops 900000000 | bytes 4000000 | tf_op jit(solution)/shard_map/outputs/pallas_call | solution.py:335
  109.8 0.8 reshape.46
  110.5 0.8 reshape.47
  111.3 9.8 %all-to-all-done.2 = bf16[64,64,128]{2,1,0:T(8,128)(2,1)S(1)} async-done(((bf16[64,64,128]{2,1,0:T(8,128)(2,1)}), bf16[64,64,128]{2,1,0:T(8,128)(2,1)S(1)}, u32[]{:S(2)}, u32[]{:S(2)}) %all-to-all-start.2) | async-done | bytes 1048608 | tf_op jit(solution)/shard_map/all_to_all | solution.py:381
  121.1 1.8 %finish.1 = (f32[27,96,96]{2,1,0:T(8,128)}, f32[27,96,96]{2,1,0:T(8,128)}, f32[1,96]{1,0:T(1,128)}, f32[1,96]{1,0:T(1,128)}) custom-call(bf16[4096,128]{1,0:T(8,128)(2,1)S(1)} %bitcast.6), custom_call_target="tpu_custom_call" | custom-call | bytes 4000000 | tf_op jit(solution)/shard_map/finish/pallas_call | solution.py:353
  (3 shorter events, 0.1 us)
Async XLA Ops:
  2.5 0.7 copy-start.2
  3.8 16.4 %collective-permute-start = (bf16[256,128]{1,0:T(8,128)(2,1)S(1)}, bf16[256,128]{1,0:T(8,128)(2,1)S(1)}, u32[]{:S(2)}, u32[]{:S(2)}) collective-permute-start(bf16[256,128]{1,0:T(8,128)(2,1)S(1)} %get-tuple-element.40), channel_id=1, source_target_pairs={{0,16},{16,32},{32,48},{48,64},{64,80},{80,96},{96,112},{112,128},... | collective-permute-start | bytes 196616 | tf_op jit(solution)/shard_map/ppermute | solution.py:399
  14.0 9.5 %collective-permute-start.1 = (bf16[256,128]{1,0:T(8,128)(2,1)S(1)}, bf16[256,128]{1,0:T(8,128)(2,1)S(1)}, u32[]{:S(2)}, u32[]{:S(2)}) collective-permute-start(bf16[256,128]{1,0:T(8,128)(2,1)S(1)} %get-tuple-element.41), channel_id=1, source_target_pairs={{16,0},{32,16},{48,32},{64,48},{80,64},{96,80},{112,96},{128,112},... | collective-permute-start | bytes 196616 | tf_op jit(solution)/shard_map/ppermute | solution.py:399
  15.9 1.1 copy-start
  17.0 1.1 copy-start.1
  18.1 0.7 copy-start.4
  18.8 0.7 copy-start.5
  23.5 4.7 %collective-permute-start.2 = (bf16[384,128]{1,0:T(8,128)(2,1)S(1)}, bf16[384,128]{1,0:T(8,128)(2,1)S(1)}, u32[]{:S(2)}, u32[]{:S(2)}) collective-permute-start(bf16[384,128]{1,0:T(8,128)(2,1)S(1)} %get-tuple-element.53), channel_id=1, source_target_pairs={{0,1},{1,2},{2,3},{3,4},{4,5},{5,6},{6,7},{7,8},{8,9},{9,10},{10,1... | collective-permute-start | bytes 294920 | tf_op jit(solution)/shard_map/ppermute | solution.py:399
  26.7 5.4 %collective-permute-start.3 = (bf16[384,128]{1,0:T(8,128)(2,1)S(1)}, bf16[384,128]{1,0:T(8,128)(2,1)S(1)}, u32[]{:S(2)}, u32[]{:S(2)}) collective-permute-start(bf16[384,128]{1,0:T(8,128)(2,1)S(1)} %get-tuple-element.54), channel_id=1, source_target_pairs={{1,0},{2,1},{3,2},{4,3},{5,4},{6,5},{7,6},{8,7},{9,8},{10,9},{11,1... | collective-permute-start | bytes 294920 | tf_op jit(solution)/shard_map/ppermute | solution.py:399
  37.1 28.4 %copy-start.6 = (bf16[1600,128]{1,0:T(8,128)(2,1)}, bf16[1600,128]{1,0:T(8,128)(2,1)S(1)}, u32[]{:S(2)}) copy-start(bf16[1600,128]{1,0:T(8,128)(2,1)S(1)} %get-tuple-element.58.inner) | copy-start | bytes 1228804
  93.0 11.2 %copy-start.3 = (s32[1,1,2,2,2]{4,3,2,1,0:T(2,128)S(1)}, s32[1,1,2,2,2]{4,3,2,1,0:T(2,128)}, u32[]{:S(2)}) copy-start(s32[1,1,2,2,2]{4,3,2,1,0:T(2,128)} %slots.3) | copy-start | bytes 100
  94.2 26.9 %all-to-all-start.2 = ((bf16[64,64,128]{2,1,0:T(8,128)(2,1)}), bf16[64,64,128]{2,1,0:T(8,128)(2,1)S(1)}, u32[]{:S(2)}, u32[]{:S(2)}) async-start(bf16[64,64,128]{2,1,0:T(8,128)(2,1)} %broadcast_in_dim.7), calls=%async_computation.2 | async-start | bytes 2097152 | tf_op jit(solution)/shard_map/all_to_all | solution.py:381
  104.2 1.0 copy-start.7

commit v4 on v2

v4 whole, which is shorter than its diff:
```python
import functools
import math

import jax
import jax.numpy as jnp
from jax import lax
from jax.experimental import pallas as pl
from jax.experimental.pallas import tpu as pltpu
from jax.sharding import PartitionSpec as P

C = 96
LANES = 128
SIDE = 8
TAPS = 27
SPAN = TAPS * LANES
OWN = 512
RIM = 800
HALF = 2048
F32 = jnp.float32
BF16 = jnp.bfloat16

VMEM_SPEC = pl.BlockSpec(memory_space=pltpu.VMEM)
SMEM_SPEC = pl.BlockSpec(memory_space=pltpu.SMEM)
HBM_SPEC = pl.BlockSpec(memory_space=pltpu.HBM)


def call(kernel, out_shape, specs, scratch=(), flops=0, moved=0, name=None, room=8):
    return pl.pallas_call(
        kernel,
        out_shape=out_shape,
        in_specs=specs,
        out_specs=jax.tree.map(lambda _: VMEM_SPEC, out_shape),
        scratch_shapes=list(scratch),
        cost_estimate=pl.CostEstimate(flops=flops, bytes_accessed=moved, transcendentals=0),
        name=name,
        compiler_params=pltpu.CompilerParams(vmem_limit_bytes=room << 20),
    )


def sublane_low(shape):
    return lax.broadcasted_iota(jnp.int32, shape, len(shape) - 2) < 4


def rotated(value, shift):
    flat = value.reshape((-1,) + value.shape[-2:])
    return pltpu.roll(flat, shift, 1).reshape(value.shape)


def far(*arrays):
    return [pltpu.with_memory_space_constraint(array, pltpu.HBM) for array in arrays]


def started(pairs, sems):
    copies = [pltpu.make_async_copy(*pair, sems.at[n]) for n, pair in enumerate(pairs)]
    for copy in copies:
        copy.start()
    return copies


def grid_kernel(
    slots_far, features_far, cotangent_far, grid, low, high,
    lines, slots, features, cotangent, sems,
):
    copies = started(
        ((features_far, features), (cotangent_far, cotangent), (slots_far, slots)), sems
    )
    copies[2].wait()
    lane = lax.broadcasted_iota(jnp.int32, (16, 4, LANES), 2)
    spot = lax.broadcasted_iota(jnp.int32, (16, SIDE, LANES), 1)
    for field, source in enumerate((features, cotangent)):
        copies[field].wait()
        whole = source[0, 0].astype(F32)

        def tiles(part):
            starts = [(3 * line + part) * LANES for line in range(16)]
            return jnp.stack([whole[:, at : at + LANES] for at in starts], axis=0)

        first, middle, last = tiles(0), tiles(1), tiles(2)
        voxels = (
            first,
            jnp.where(lane < 32, moved_lanes(first, 32), moved_lanes(middle, 32)),
            jnp.where(lane < 64, moved_lanes(middle, 64), moved_lanes(last, 64)),
            moved_lanes(last, 96),
        )
        for w in range(4):
            lines[w] = jnp.zeros((16, SIDE, LANES), F32)
            lines[w, :, 0:4] = jnp.where(lane < C, voxels[w], 1.0 - field)
        for i in range(2):
            for j in range(2):
                tile = None
                for z in range(SIDE):
                    row = lines[z % 4, :, pl.ds(slots[0, 0, i, j, z // 4], 1)]
                    row = jnp.broadcast_to(row, (16, SIDE, LANES))
                    tile = row if tile is None else jnp.where(spot == z, row, tile)
                grid[field, 4 * i : 4 * i + 4, 4 * j : 4 * j + 4] = tile.reshape(4, 4, SIDE, LANES)
    for field in range(2):
        rows = slice(field * 128, field * 128 + 128)
        low[rows] = grid[field, 0:2].reshape(128, LANES).astype(BF16)
        high[rows] = grid[field, 6:8].reshape(128, LANES).astype(BF16)


def moved_lanes(value, shift):
    return pltpu.roll(value.reshape(64, LANES), shift, 1).reshape(16, 4, LANES)


def opened(message, lead):
    return message.astype(F32).reshape(lead + (SIDE, LANES))


def rim_kernel(grid, below, above, low, high):
    lower = opened(below[...], (2, 2, SIDE))
    upper = opened(above[...], (2, 2, SIDE))
    for message, at in ((low, 0), (high, SIDE - 2)):
        for field in range(2):
            base = field * 192
            message[base : base + 32] = (
                lower[field, :, at : at + 2].reshape(32, LANES).astype(BF16)
            )
            message[base + 32 : base + 160] = (
                grid[field, :, at : at + 2].reshape(128, LANES).astype(BF16)
            )
            message[base + 160 : base + 192] = (
                upper[field, :, at : at + 2].reshape(32, LANES).astype(BF16)
            )


def with_neighbours(value):
    spot = lax.broadcasted_iota(jnp.int32, value.shape, value.ndim - 2)
    before = jnp.where(spot == 0, 0.0, rotated(value, 1))
    after = jnp.where(spot == SIDE - 1, 0.0, rotated(value, SIDE - 1))
    return jnp.concatenate([before, value, after], axis=value.ndim - 1)


def fill_windows(windows, stacked, start, extent):
    rows = extent * extent * SIDE
    for wx in range(3):
        for wy in range(3):
            at = (wx * 3 + wy) * 3 * LANES
            piece = stacked[
                start + wx : start + wx + extent, start + wy : start + wy + extent
            ]
            windows[0:rows, at : at + 3 * LANES] = piece.reshape(rows, 3 * LANES).astype(BF16)


def spread(kernel, rows_ref):
    rows_ref[...] = jnp.zeros_like(rows_ref)
    for tap in range(TAPS):
        rows_ref[tap * LANES : tap * LANES + C, 0:C] = kernel[tap]


def spread_flipped(kernel, columns_ref):
    columns_ref[...] = jnp.zeros_like(columns_ref)
    for tap in range(TAPS):
        columns_ref[0:C, tap * LANES : tap * LANES + C] = kernel[TAPS - 1 - tap]


def plain_dot(left, right):
    return jnp.dot(left, right, preferred_element_type=F32)


def turned_dot(left, right):
    return lax.dot_general(left, right, (((1,), (1,)), ((), ())), preferred_element_type=F32)


def rounded(value):
    return value.astype(BF16).astype(F32)


def gradient_kernel(
    side, grid, below, above, left, right, one_far, two_far, gain_far, bias_far,
    keep, send, inner,
    field_ref, stack_ref, windows, terms_one, terms_two, packed_all,
    rows_ref, columns_ref, weight_one, weight_two, gain_ref, bias_ref, sems,
):
    copies = started(
        ((one_far, weight_one), (two_far, weight_two), (gain_far, gain_ref), (bias_far, bias_ref)), sems
    )
    lower = opened(below[...], (2, 2, SIDE))
    upper = opened(above[...], (2, 2, SIDE))
    to_left = opened(left[...], (2, SIDE + 4, 2))
    to_right = opened(right[...], (2, SIDE + 4, 2))

    def load_field(field):
        field_ref[2 : SIDE + 2, 2 : SIDE + 2] = grid[field]
        field_ref[0:2, 2 : SIDE + 2] = lower[field]
        field_ref[SIDE + 2 : SIDE + 4, 2 : SIDE + 2] = upper[field]
        field_ref[:, 0:2] = to_left[field]
        field_ref[:, SIDE + 2 : SIDE + 4] = to_right[field]

    load_field(0)
    mark = field_ref[1 : SIDE + 3, 1 : SIDE + 3].reshape(RIM, LANES)[:, C : C + 1]
    stack_ref[...] = with_neighbours(field_ref[...])
    fill_windows(windows, stack_ref, 0, SIDE + 2)
    for copy in copies:
        copy.wait()
    spread(weight_one, rows_ref)
    spread_flipped(weight_two, columns_ref)
    blank = jnp.zeros((1, LANES - C), F32)
    gain = jnp.concatenate([gain_ref[...], blank], axis=1)
    bias = jnp.concatenate([bias_ref[...], blank], axis=1)
    first_conv = plain_dot(windows[...], rows_ref[...]) * mark
    pre = first_conv * gain + bias
    gate = 1.0 / (1.0 + jnp.exp(-pre))
    hidden = rounded(pre * gate * mark)
    slope = gate * (1.0 + pre * (1.0 - gate)) * mark
    inner[0:RIM] = hidden.astype(BF16)

    load_field(1)
    stack_ref[...] = with_neighbours(field_ref[...])
    fill_windows(windows, stack_ref, 0, SIDE + 2)
    back_hidden = turned_dot(windows[...], columns_ref[...])
    back_pre = back_hidden * slope
    back_conv = rounded(back_pre * gain)
    inner[RIM : 2 * RIM] = back_conv.astype(BF16)

    def own(value):
        lead = value.reshape(SIDE + 2, SIDE + 2, SIDE, LANES)
        return lead[1 : SIDE + 1, 1 : SIDE + 1].reshape(OWN, LANES)

    own_pre = own(back_pre)
    gain_term = jnp.sum(own_pre * own(first_conv), axis=0, keepdims=True)
    bias_term = jnp.sum(own_pre, axis=0, keepdims=True)

    fill_windows(windows, stack_ref, 1, SIDE)
    hidden_turned = own(hidden).T.astype(BF16)
    terms_two[...] = plain_dot(hidden_turned, windows[0:OWN])

    lead = back_conv.reshape(SIDE + 2, SIDE + 2, SIDE, LANES)
    stack_ref[0 : SIDE + 2, 0 : SIDE + 2] = with_neighbours(lead)
    fill_windows(windows, stack_ref, 0, SIDE)
    features_turned = grid[0].reshape(OWN, LANES).T.astype(BF16)
    terms_one[...] = plain_dot(features_turned, windows[0:OWN])

    lane = lax.broadcasted_iota(jnp.int32, (C, LANES), 1)
    for terms, packed in ((terms_one, packed_all.at[0]), (terms_two, packed_all.at[1])):

        def term(tap):
            at = (TAPS - 1 - tap) * LANES
            return terms[0:C, at : at + LANES]

        for group in range(6):
            split = term(4 * group + 3)
            for part in range(3):
                row = (3 * group + part) * C
                moved = pltpu.roll(split, C - 32 * part, 1)
                joined = jnp.where(lane < C, term(4 * group + part), moved)
                packed[row : row + C] = joined
        for tap in range(24, TAPS):
            packed[(tap - 6) * C : (tap - 5) * C] = term(tap)
    blank = jnp.zeros((HALF - 21 * C - 2, LANES), F32)
    packed_all[0, 21 * C : HALF] = jnp.zeros((HALF - 21 * C, LANES), F32)
    packed_all[1, 21 * C : HALF] = jnp.concatenate([gain_term, bias_term, blank], axis=0)
    keep[...] = packed_all[side[0]]
    send[...] = packed_all[1 - side[0]]


def output_kernel(
    slots, grid, inner, one_far, two_far, out, grad,
    stack_ref, windows, rows_ref, columns_ref, weight_one, weight_two, sems,
):
    copies = started(((one_far, weight_one), (two_far, weight_two)), sems)
    for copy in copies:
        copy.wait()
    spread(weight_two, rows_ref)
    spread_flipped(weight_one, columns_ref)
    count = out.shape[0]
    out[...] = jnp.zeros_like(out)
    grad[...] = jnp.zeros_like(grad)
    for field, target in enumerate((out, grad)):
        lead = inner[field * RIM : field * RIM + RIM].astype(F32)
        stack_ref[...] = with_neighbours(lead.reshape(SIDE + 2, SIDE + 2, SIDE, LANES))
        fill_windows(windows, stack_ref, 0, SIDE)
        if field == 0:
            total = plain_dot(windows[...], rows_ref[...])
        else:
            total = turned_dot(windows[...], columns_ref[...])
        dense = total.reshape(SIDE, SIDE, SIDE, LANES) + grid[field]
        for i in range(2):
            for j in range(2):
                column = dense[4 * i : 4 * i + 4, 4 * j : 4 * j + 4].reshape(4, 2, 2, 8, LANES)
                even = column[:, :, 0].reshape(8, 8, LANES)
                odd = column[:, :, 1].reshape(8, 8, LANES)
                is_low = sublane_low(even.shape)
                tiles = (
                    jnp.where(is_low, even, rotated(odd, 4)),
                    jnp.where(is_low, rotated(even, 4), odd),
                )
                for k in range(2):
                    slot = slots[0, 0, i, j, k]
                    brick = tiles[k].reshape(64, LANES)[:, 0:C].astype(BF16)

                    @pl.when(slot < count)
                    def _():
                        target[slot] = brick


def unpack(scale, parts, grad):
    lane = lax.broadcasted_iota(jnp.int32, (C, LANES), 1)
    for group in range(6):
        held = [
            parts[(3 * group + part) * C : (3 * group + part + 1) * C].astype(F32) * scale
            for part in range(3)
        ]
        for part in range(3):
            grad[4 * group + part] = held[part][:, 0:C]
        moved = [pltpu.roll(held[part], 32 * part + 32, 1) for part in range(3)]
        last = jnp.where(lane < 32, moved[0], jnp.where(lane < 64, moved[1], moved[2]))
        grad[4 * group + 3] = last[:, 0:C]
    for tap in range(24, TAPS):
        grad[tap] = parts[(tap - 6) * C : (tap - 5) * C].astype(F32)[:, 0:C] * scale


def finish_kernel(scale, side, mine, other, grad_one, grad_two, grad_gain, grad_bias, parts):
    parts[side[0]] = mine[...]
    parts[1 - side[0]] = other[...]
    unpack(scale, parts.at[0], grad_one)
    unpack(scale, parts.at[1], grad_two)
    rest = parts[1, 21 * C : HALF].astype(F32) * scale
    grad_gain[...] = rest[0:1, 0:C]
    grad_bias[...] = rest[1:2, 0:C]


def shape(dims, dtype):
    return jax.ShapeDtypeStruct(dims, dtype)


def dense_parts(features, cotangent, slots):
    return call(
        grid_kernel,
        (shape((2, SIDE, SIDE, SIDE, LANES), F32), shape((256, LANES), BF16), shape((256, LANES), BF16)),
        [HBM_SPEC] * 3,
        scratch=[
            pltpu.VMEM((4, 16, SIDE, LANES), F32),
            pltpu.SMEM(slots.shape, jnp.int32),
            pltpu.VMEM(features.shape, BF16),
            pltpu.VMEM(features.shape, BF16),
            pltpu.SemaphoreType.DMA((3,)),
        ],
        moved=2_000_000,
        name="dense_grid",
    )(*far(slots, features, cotangent))


def rims(grid, below, above):
    return call(
        rim_kernel,
        (shape((384, LANES), BF16), shape((384, LANES), BF16)),
        [VMEM_SPEC] * 3,
        moved=1_500_000,
        name="rims",
    )(grid, below, above)


def weight_scratch():
    return [
        pltpu.VMEM((SPAN, LANES), BF16),
        pltpu.VMEM((LANES, SPAN), BF16),
        pltpu.VMEM((TAPS, C, C), BF16),
        pltpu.VMEM((TAPS, C, C), BF16),
    ]


def gradients(side, grid, halos, weight_one, weight_two, gain, bias):
    return call(
        gradient_kernel,
        (shape((HALF, LANES), F32), shape((HALF, LANES), F32), shape((2 * RIM, LANES), BF16)),
        [SMEM_SPEC] + [VMEM_SPEC] * 5 + [HBM_SPEC] * 4,
        scratch=[
            pltpu.VMEM((SIDE + 4, SIDE + 4, SIDE, LANES), F32),
            pltpu.VMEM((SIDE + 4, SIDE + 4, SIDE, 3 * LANES), F32),
            pltpu.VMEM((RIM, SPAN), BF16),
            pltpu.VMEM((LANES, SPAN), F32),
            pltpu.VMEM((LANES, SPAN), F32),
            pltpu.VMEM((2, HALF, LANES), F32),
            *weight_scratch(),
            pltpu.VMEM((1, C), F32),
            pltpu.VMEM((1, C), F32),
            pltpu.SemaphoreType.DMA((4,)),
        ],
        flops=2_400_000_000,
        moved=8_000_000,
        name="gradients",
        room=28,
    )(side, grid, *halos, *far(weight_one, weight_two, gain.reshape(1, C), bias.reshape(1, C)))


def outputs(slots, grid, inner, weight_one, weight_two):
    result = shape((4, 64, C), BF16)
    return call(
        output_kernel,
        (result, result),
        [SMEM_SPEC] + [VMEM_SPEC] * 2 + [HBM_SPEC] * 2,
        scratch=[
            pltpu.VMEM((SIDE + 2, SIDE + 2, SIDE, 3 * LANES), F32),
            pltpu.VMEM((OWN, SPAN), BF16),
            *weight_scratch(),
            pltpu.SemaphoreType.DMA((2,)),
        ],
        flops=900_000_000,
        moved=4_000_000,
        name="outputs",
        room=18,
    )(slots, grid, inner, *far(weight_one, weight_two))


def finish(side, mine, other, scale):
    grads, line = shape((TAPS, C, C), F32), shape((1, C), F32)
    return call(
        functools.partial(finish_kernel, scale),
        (grads, grads, line, line),
        [SMEM_SPEC, VMEM_SPEC, VMEM_SPEC],
        scratch=[pltpu.VMEM((2, HALF, LANES), BF16)],
        moved=4_000_000,
        name="finish",
    )(side, mine, other)


SIZES = dict(y=4, zh=4, core=2, zl=2, zp=2, x=4)
PLANE = ("y", "x", "zp")
LINE = ("zh", "zl")


def spread_out(block, axes):
    copies = jnp.broadcast_to(block, (lax.axis_size(axes),) + block.shape)
    return lax.all_to_all(copies, axes, 0, 0)


def other_core(block):
    return lax.ppermute(block, "core", [(0, 1), (1, 0)])


def reduce_all(keep, send):
    pair = (keep + other_core(send)).astype(BF16)
    parts = lax.all_to_all(pair.reshape(lax.axis_size(PLANE), -1, LANES), PLANE, 0, 0)
    chunk = jnp.sum(parts.astype(F32), axis=0)
    chunk = jnp.sum(spread_out(chunk, LINE), axis=0)
    return spread_out(chunk.astype(BF16), PLANE).reshape(HALF, LANES)


GX = ("y", "zh", "core")
GY = ("zl", "zp", "x")


def passed_along(block, axis, distance):
    devices = range(lax.axis_size(axis))
    route = [(i - distance, i) for i in devices if i - distance in devices]
    return lax.ppermute(block, axis, route)


def body(features, cotangent, brick_slot, weight_one, weight_two, gain, bias):
    side = lax.axis_index("core").reshape(1)
    grid, low, high = dense_parts(features, cotangent, brick_slot)
    below = passed_along(high, GX, 1)
    above = passed_along(low, GX, -1)
    low, high = rims(grid, below, above)
    left = passed_along(high, GY, 1)
    right = passed_along(low, GY, -1)
    keep, send, inner = gradients(side, grid, (below, above, left, right), weight_one, weight_two, gain, bias)
    out, grad = outputs(brick_slot, grid, inner, weight_one, weight_two)
    out, grad = out.reshape(features.shape), grad.reshape(features.shape)
    mine, out, grad = lax.optimization_barrier((reduce_all(keep, send), out, grad))
    other = other_core(mine)
    scale = 1.0 / math.sqrt(lax.axis_size(GX) * lax.axis_size(GY) * 256)
    grad_one, grad_two, grad_gain, grad_bias = finish(side, mine, other, scale)
    return (
        out,
        grad,
        grad_one,
        grad_two,
        grad_gain.reshape(gain.shape),
        grad_bias.reshape(bias.shape),
    )


def solution(mesh):
    fine = jax.sharding.Mesh(mesh.devices.reshape(tuple(SIZES.values())), tuple(SIZES))
    slabs = P(GX, GY, None, None)
    in_specs = (slabs, slabs, P(GX, GY, None, None, None), P(), P(), P(), P())
    out_specs = (slabs, slabs, P(), P(), P(), P())
    return jax.shard_map(body, mesh=fine, in_specs=in_specs, out_specs=out_specs, check_vma=False)
```

time: 126 us -> 116 us (0.921)
  local copies, waits for them, and re-layouts: 8.62 us -> 2.48 us
  blocking collectives: 54.1 us -> 50.1 us
  Pallas kernels: 13.1 us -> 16.1 us
  waiting for transfers between devices: 19.5 us -> 18 us
  starting transfers between devices: 29.1 us -> 27.7 us
    all_to_all x1, waiting for transfers between devices: 8.87 us -> 2.21 us  [spread_out(): return lax.all_to_all(copies, axes, 0, 0)]
    all_to_all x1, blocking collectives: 28 us -> 22 us  [reduce_all(): lax.all_to_all(pair.reshape(lax.axis_size(PLANE), -1, LANES), PLANE, 0, 0)]
    unnamed x16 -> x2, local copies, waits for them, and re-layouts: 4.09 us -> 0.01 us
    all_to_all x1, starting transfers between devices: 7.79 us -> 3.89 us  [spread_out(): return lax.all_to_all(copies, axes, 0, 0)]
    ppermute x4, waiting for transfers between devices: 8.4 us -> 11.6 us  [passed_along(): return lax.ppermute(block, axis, route)]
    ppermute x1 -> x2, starting transfers between devices: 4.74 us -> 7.32 us  [other_core(): return lax.ppermute(block, 'core', [(0, 1), (1, 0)])]
    pallas_call x3 -> x2, Pallas kernels: 10.4 us -> 12.8 us  [the longest x1 6.51 us: gradients(): call(gradient_kernel, (shape((HALF, LANES), F32), shape((HALF, LANES), F3...]
    all_to_all x1, blocking collectives: 26.1 us -> 28.1 us  [spread_out(): return lax.all_to_all(copies, axes, 0, 0)]
  transfers between devices with their start and end apart: 6 -> 7, of which waited for: 4 -> 6; matrix products, arithmetic and copies ran while one was open for 1% -> 1% of each run, Pallas kernels for 4% -> 5%
where the time goes in v4:
time: 116 us; the launch traced here: 115 us
  blocking collectives  50.1 us (43%)
  starting transfers between devices  27.7 us (24%)
  waiting for transfers between devices  18 us (16%)
  Pallas kernels  16.1 us (14%)
  local copies, waits for them, and re-layouts  2.48 us (2%)
    all_to_all x1, blocking collectives, spread_out(): return lax.all_to_all(copies, axes, 0, 0)  28.1 us
    all_to_all x1, blocking collectives, reduce_all(): lax.all_to_all(pair.reshape(lax.axis_size(PLANE), -1, LANES), PLANE, 0, 0)  22 us
    ppermute x4, starting transfers between devices, passed_along(): return lax.ppermute(block, axis, route)  16.5 us
    ppermute x4, waiting for transfers between devices, passed_along(): return lax.ppermute(block, axis, route)  11.6 us
    ppermute x2, starting transfers between devices, other_core(): return lax.ppermute(block, 'core', [(0, 1), (1, 0)])  7.32 us
    pallas_call x1, Pallas kernels, gradients(): call(gradient_kernel, (shape((HALF, LANES), F32), shape((HALF, LANES), F3...  6.51 us
    pallas_call x1, Pallas kernels, outputs(): call(output_kernel, (result, result), [SMEM_SPEC] + [VMEM_SPEC] * 2 + [HB...  6.25 us
    ppermute x2, waiting for transfers between devices, other_core(): return lax.ppermute(block, 'core', [(0, 1), (1, 0)])  4.14 us
  transfers between devices with their start and end apart: 7, of which 6 were waited for; matrix products, arithmetic and copies ran while one was open for 1% of the time, Pallas kernels for 5%

profile of v4, /device:TPU:1, one launch (start us, length us, event | category | flops | bytes accessed | tf_op | source)
XLA Modules:
  0.0 115.4 jit_solution(10987175493710378955)
XLA Ops:
  0.6 1.3 %dense_grid.1 = (f32[2,8,8,8,128]{4,3,2,1,0:T(8,128)S(1)}, bf16[256,128]{1,0:T(8,128)(2,1)S(1)}, bf16[256,128]{1,0:T(8,128)(2,1)S(1)}) custom-call(s32[1,1,2,2,2]{4,3,2,1,0:T(2,128)} %slots.1, bf16[1,1,4,6144]{3,2,1,0:T(4,128)(2,1)} %features_far.1, bf16[1,1,4,6144]{3,2,1,0:T(4,128)(2,1)} %cotangent_far.1), custom_call_target="tpu_custom_call" | custom-call | bytes 2000000 | tf_op jit(solution)/shard_map/dense_grid/pallas_call | solution.py:328
  1.9 10.2 %collective-permute-start = (bf16[256,128]{1,0:T(8,128)(2,1)S(1)}, bf16[256,128]{1,0:T(8,128)(2,1)S(1)}, u32[]{:S(2)}, u32[]{:S(2)}) collective-permute-start(bf16[256,128]{1,0:T(8,128)(2,1)S(1)} %get-tuple-element.24), channel_id=1, source_target_pairs={{0,16},{16,32},{32,48},{48,64},{64,80},{80,96},{96,112},{112,128},... | collective-permute-start | bytes 196616 | tf_op jit(solution)/shard_map/ppermute | solution.py:447
  12.1 1.9 %collective-permute-start.1 = (bf16[256,128]{1,0:T(8,128)(2,1)S(1)}, bf16[256,128]{1,0:T(8,128)(2,1)S(1)}, u32[]{:S(2)}, u32[]{:S(2)}) collective-permute-start(bf16[256,128]{1,0:T(8,128)(2,1)S(1)} %get-tuple-element.25), channel_id=1, source_target_pairs={{16,0},{32,16},{48,32},{64,48},{80,64},{96,80},{112,96},{128,112},... | collective-permute-start | bytes 196616 | tf_op jit(solution)/shard_map/ppermute | solution.py:447
  14.1 0.0 collective-permute-done.below
  14.1 7.6 %collective-permute-done.1.above = bf16[256,128]{1,0:T(8,128)(2,1)S(1)} collective-permute-done((bf16[256,128]{1,0:T(8,128)(2,1)S(1)}, bf16[256,128]{1,0:T(8,128)(2,1)S(1)}, u32[]{:S(2)}, u32[]{:S(2)}) %collective-permute-start.1) | collective-permute-done | bytes 65568 | tf_op jit(solution)/shard_map/ppermute | solution.py:447
  21.7 3.1 %collective-permute-start.2 = (bf16[384,128]{1,0:T(8,128)(2,1)S(1)}, bf16[384,128]{1,0:T(8,128)(2,1)S(1)}, u32[]{:S(2)}, u32[]{:S(2)}) collective-permute-start(bf16[384,128]{1,0:T(8,128)(2,1)S(1)} %get-tuple-element.26), channel_id=1, source_target_pairs={{0,1},{1,2},{2,3},{3,4},{4,5},{5,6},{6,7},{7,8},{8,9},{9,10},{10,1... | collective-permute-start | bytes 294920 | tf_op jit(solution)/shard_map/ppermute | solution.py:447
  24.8 1.3 %collective-permute-start.3 = (bf16[384,128]{1,0:T(8,128)(2,1)S(1)}, bf16[384,128]{1,0:T(8,128)(2,1)S(1)}, u32[]{:S(2)}, u32[]{:S(2)}) collective-permute-start(bf16[384,128]{1,0:T(8,128)(2,1)S(1)} %get-tuple-element.27), channel_id=1, source_target_pairs={{1,0},{2,1},{3,2},{4,3},{5,4},{6,5},{7,6},{8,7},{9,8},{10,9},{11,1... | collective-permute-start | bytes 294920 | tf_op jit(solution)/shard_map/ppermute | solution.py:447
  26.1 0.3 collective-permute-done.2.left
  26.4 3.7 %collective-permute-done.3.right = bf16[384,128]{1,0:T(8,128)(2,1)S(1)} collective-permute-done((bf16[384,128]{1,0:T(8,128)(2,1)S(1)}, bf16[384,128]{1,0:T(8,128)(2,1)S(1)}, u32[]{:S(2)}, u32[]{:S(2)}) %collective-permute-start.3) | collective-permute-done | bytes 98336 | tf_op jit(solution)/shard_map/ppermute | solution.py:447
  30.2 6.5 %gradients.1 = (f32[2048,128]{1,0:T(8,128)S(1)}, f32[2048,128]{1,0:T(8,128)S(1)}, bf16[1600,128]{1,0:T(8,128)(2,1)S(1)}) custom-call(s32[1]{0:T(128)} %bitcast.side, f32[2,8,8,8,128]{4,3,2,1,0:T(8,128)S(1)} %get-tuple-element.23.grid, bf16[256,128]{1,0:T(8,128)(2,1)S(1)} %collective-permute-done.below, bf16[256,128]{1,0:T(8,128)(2,1)S(1)} %collective-permute-done.1.above, ...), custom_call_target="tpu_custom_call" | custom-call | flops 2400000000 | bytes 8000000 | tf_op jit(solution)/shard_map/gradients/pallas_call | solution.py:364
  36.7 1.9 %collective-permute-start.4 = (f32[2048,128]{1,0:T(8,128)S(1)}, f32[2048,128]{1,0:T(8,128)S(1)}, u32[]{:S(2)}, u32[]{:S(2)}) collective-permute-start(f32[2048,128]{1,0:T(8,128)S(1)} %get-tuple-element.29), channel_id=1, source_target_pairs={{0,16},{16,0},{1,17},{17,1},{2,18},{18,2},{3,19},{19,3},{4,20},{20... | collective-permute-start | bytes 3145736 | tf_op jit(solution)/shard_map/ppermute | solution.py:429
  38.6 2.6 %collective-permute-done.4 = f32[2048,128]{1,0:T(8,128)S(1)} collective-permute-done((f32[2048,128]{1,0:T(8,128)S(1)}, f32[2048,128]{1,0:T(8,128)S(1)}, u32[]{:S(2)}, u32[]{:S(2)}) %collective-permute-start.4) | collective-permute-done | bytes 1048608 | tf_op jit(solution)/shard_map/ppermute | solution.py:429
  41.2 0.1 add_convert_fusion
  41.3 22.0 %all_to_all.15 = bf16[32,64,128]{2,1,0:T(8,128)(2,1)S(1)} all-to-all(bf16[32,64,128]{2,1,0:T(8,128)(2,1)S(1)} %bitcast.9), channel_id=1, replica_groups=mesh['y'=4,'zh'=4,'core'=2,'zl'=2,'zp'=2,'x'=4] {'y','x','zp'}, dimensions={0} | all-to-all | bytes 1048576 | tf_op jit(solution)/shard_map/all_to_all | solution.py:434
  63.3 0.1 convert_reduce_fusion
  63.4 0.0 copy-start
  63.4 28.1 %all_to_all.16 = f32[8,64,128]{2,1,0:T(8,128)S(1)} all-to-all(f32[8,64,128]{2,1,0:T(8,128)S(1)} %broadcast_in_dim.6), channel_id=1, replica_groups=mesh['y'=4,'zh'=4,'core'=2,'zl'=2,'zp'=2,'x'=4] {'zh','zl'}, dimensions={0} | all-to-all | bytes 524288 | tf_op jit(solution)/shard_map/all_to_all | solution.py:425
  91.6 0.9 broadcast_in_dim.7
  92.5 3.9 %all-to-all-start.2 = ((bf16[32,64,128]{2,1,0:T(8,128)(2,1)}), bf16[32,64,128]{2,1,0:T(8,128)(2,1)S(1)}, u32[]{:S(2)}, u32[]{:S(2)}) async-start(bf16[32,64,128]{2,1,0:T(8,128)(2,1)} %broadcast_in_dim.7), calls=%async_computation.2 | async-start | bytes 1048576 | tf_op jit(solution)/shard_map/all_to_all | solution.py:425
  96.4 0.0 copy-done
  96.4 6.2 %outputs.1 = (bf16[4,64,96]{2,1,0:T(8,128)(2,1)S(1)}, bf16[4,64,96]{2,1,0:T(8,128)(2,1)S(1)}) custom-call(s32[1,1,2,2,2]{4,3,2,1,0:T(2,128)S(1)} %copy-done, f32[2,8,8,8,128]{4,3,2,1,0:T(8,128)S(1)} %get-tuple-element.23.grid, bf16[1600,128]{1,0:T(8,128)(2,1)S(1)} %get-tuple-element.30.inner, bf16[27,96,96]{2,1,0:T(8,128)(2,1)} %one_far.3, ...), custom_call_target="tpu_custom_call" | custom-call | flops 900000000 | bytes 4000000 | tf_op jit(solution)/shard_map/outputs/pallas_call | solution.py:389
  102.7 0.8 reshape.44
  103.4 0.8 reshape.45
  104.2 2.2 %all-to-all-done.2 = bf16[32,64,128]{2,1,0:T(8,128)(2,1)S(1)} async-done(((bf16[32,64,128]{2,1,0:T(8,128)(2,1)}), bf16[32,64,128]{2,1,0:T(8,128)(2,1)S(1)}, u32[]{:S(2)}, u32[]{:S(2)}) %all-to-all-start.2) | async-done | bytes 524320 | tf_op jit(solution)/shard_map/all_to_all | solution.py:425
  106.4 5.4 %collective-permute-start.5 = (bf16[2048,128]{1,0:T(8,128)(2,1)S(1)}, bf16[2048,128]{1,0:T(8,128)(2,1)S(1)}, u32[]{:S(2)}, u32[]{:S(2)}) collective-permute-start(bf16[2048,128]{1,0:T(8,128)(2,1)S(1)} %bitcast.7), channel_id=1, source_target_pairs={{0,16},{16,0},{1,17},{17,1},{2,18},{18,2},{3,19},{19,3},{4,20},{20... | collective-permute-start | bytes 1572872 | tf_op jit(solution)/shard_map/ppermute | solution.py:429
  111.8 1.5 %collective-permute-done.5.other = bf16[2048,128]{1,0:T(8,128)(2,1)S(1)} collective-permute-done((bf16[2048,128]{1,0:T(8,128)(2,1)S(1)}, bf16[2048,128]{1,0:T(8,128)(2,1)S(1)}, u32[]{:S(2)}, u32[]{:S(2)}) %collective-permute-start.5) | collective-permute-done | bytes 524320 | tf_op jit(solution)/shard_map/ppermute | solution.py:429
  113.3 2.0 %finish.1 = (f32[27,96,96]{2,1,0:T(8,128)}, f32[27,96,96]{2,1,0:T(8,128)}, f32[1,96]{1,0:T(1,128)}, f32[1,96]{1,0:T(1,128)}) custom-call(s32[1]{0:T(128)} %bitcast.side, bf16[2048,128]{1,0:T(8,128)(2,1)S(1)} %bitcast.8, bf16[2048,128]{1,0:T(8,128)(2,1)S(1)} %collective-permute-done.5.other), custom_call_target="tpu_custom_call" | custom-call | bytes 4000000 | tf_op jit(solution)/shard_map/finish/pallas_call | solution.py:408
  (3 shorter events, 0.1 us)
Async XLA Ops:
  1.9 12.1 %collective-permute-start = (bf16[256,128]{1,0:T(8,128)(2,1)S(1)}, bf16[256,128]{1,0:T(8,128)(2,1)S(1)}, u32[]{:S(2)}, u32[]{:S(2)}) collective-permute-start(bf16[256,128]{1,0:T(8,128)(2,1)S(1)} %get-tuple-element.24), channel_id=1, source_target_pairs={{0,16},{16,32},{32,48},{48,64},{64,80},{80,96},{96,112},{112,128},... | collective-permute-start | bytes 196616 | tf_op jit(solution)/shard_map/ppermute | solution.py:447
  12.1 9.5 %collective-permute-start.1 = (bf16[256,128]{1,0:T(8,128)(2,1)S(1)}, bf16[256,128]{1,0:T(8,128)(2,1)S(1)}, u32[]{:S(2)}, u32[]{:S(2)}) collective-permute-start(bf16[256,128]{1,0:T(8,128)(2,1)S(1)} %get-tuple-element.25), channel_id=1, source_target_pairs={{16,0},{32,16},{48,32},{64,48},{80,64},{96,80},{112,96},{128,112},... | collective-permute-start | bytes 196616 | tf_op jit(solution)/shard_map/ppermute | solution.py:447
  21.7 4.7 %collective-permute-start.2 = (bf16[384,128]{1,0:T(8,128)(2,1)S(1)}, bf16[384,128]{1,0:T(8,128)(2,1)S(1)}, u32[]{:S(2)}, u32[]{:S(2)}) collective-permute-start(bf16[384,128]{1,0:T(8,128)(2,1)S(1)} %get-tuple-element.26), channel_id=1, source_target_pairs={{0,1},{1,2},{2,3},{3,4},{4,5},{5,6},{6,7},{7,8},{8,9},{9,10},{10,1... | collective-permute-start | bytes 294920 | tf_op jit(solution)/shard_map/ppermute | solution.py:447
  24.8 5.4 %collective-permute-start.3 = (bf16[384,128]{1,0:T(8,128)(2,1)S(1)}, bf16[384,128]{1,0:T(8,128)(2,1)S(1)}, u32[]{:S(2)}, u32[]{:S(2)}) collective-permute-start(bf16[384,128]{1,0:T(8,128)(2,1)S(1)} %get-tuple-element.27), channel_id=1, source_target_pairs={{1,0},{2,1},{3,2},{4,3},{5,4},{6,5},{7,6},{8,7},{9,8},{10,9},{11,1... | collective-permute-start | bytes 294920 | tf_op jit(solution)/shard_map/ppermute | solution.py:447
  36.7 4.6 %collective-permute-start.4 = (f32[2048,128]{1,0:T(8,128)S(1)}, f32[2048,128]{1,0:T(8,128)S(1)}, u32[]{:S(2)}, u32[]{:S(2)}) collective-permute-start(f32[2048,128]{1,0:T(8,128)S(1)} %get-tuple-element.29), channel_id=1, source_target_pairs={{0,16},{16,0},{1,17},{17,1},{2,18},{18,2},{3,19},{19,3},{4,20},{20... | collective-permute-start | bytes 3145736 | tf_op jit(solution)/shard_map/ppermute | solution.py:429
  63.4 33.0 %copy-start = (s32[1,1,2,2,2]{4,3,2,1,0:T(2,128)S(1)}, s32[1,1,2,2,2]{4,3,2,1,0:T(2,128)}, u32[]{:S(2)}) copy-start(s32[1,1,2,2,2]{4,3,2,1,0:T(2,128)} %slots.1) | copy-start | bytes 100
  92.5 13.9 %all-to-all-start.2 = ((bf16[32,64,128]{2,1,0:T(8,128)(2,1)}), bf16[32,64,128]{2,1,0:T(8,128)(2,1)S(1)}, u32[]{:S(2)}, u32[]{:S(2)}) async-start(bf16[32,64,128]{2,1,0:T(8,128)(2,1)} %broadcast_in_dim.7), calls=%async_computation.2 | async-start | bytes 1048576 | tf_op jit(solution)/shard_map/all_to_all | solution.py:425
  106.4 6.9 %collective-permute-start.5 = (bf16[2048,128]{1,0:T(8,128)(2,1)S(1)}, bf16[2048,128]{1,0:T(8,128)(2,1)S(1)}, u32[]{:S(2)}, u32[]{:S(2)}) collective-permute-start(bf16[2048,128]{1,0:T(8,128)(2,1)S(1)} %bitcast.7), channel_id=1, source_target_pairs={{0,16},{16,0},{1,17},{17,1},{2,18},{18,2},{3,19},{19,3},{4,20},{20... | collective-permute-start | bytes 1572872 | tf_op jit(solution)/shard_map/ppermute | solution.py:429

commit v5 on v4

--- a/solution.py
+++ b/solution.py
@@ -46,7 +46,7 @@
     return pltpu.roll(flat, shift, 1).reshape(value.shape)
 
 
-def far(*arrays):
+def kept_far(*arrays):
     return [pltpu.with_memory_space_constraint(array, pltpu.HBM) for array in arrays]
 
 
@@ -58,7 +58,7 @@
 
 
 def grid_kernel(
-    slots_far, features_far, cotangent_far, grid, low, high,
+    sides, slots_far, features_far, cotangent_far, grid, far, near,
     lines, slots, features, cotangent, sems,
 ):
     copies = started(
@@ -95,8 +95,8 @@
                 grid[field, 4 * i : 4 * i + 4, 4 * j : 4 * j + 4] = tile.reshape(4, 4, SIDE, LANES)
     for field in range(2):
         rows = slice(field * 128, field * 128 + 128)
-        low[rows] = grid[field, 0:2].reshape(128, LANES).astype(BF16)
-        high[rows] = grid[field, 6:8].reshape(128, LANES).astype(BF16)
+        for message, at in ((near, 6 - 6 * sides[0]), (far, 6 * sides[0])):
+            message[rows] = grid[field, pl.ds(at, 2)].reshape(128, LANES).astype(BF16)
 
 
 def moved_lanes(value, shift):
@@ -107,21 +107,28 @@
     return message.astype(F32).reshape(lead + (SIDE, LANES))
 
 
-def rim_kernel(grid, below, above, low, high):
-    lower = opened(below[...], (2, 2, SIDE))
-    upper = opened(above[...], (2, 2, SIDE))
-    for message, at in ((low, 0), (high, SIDE - 2)):
+def lower_upper(side, near, far, lead):
+    near, far = opened(near[...], lead), opened(far[...], lead)
+    even = side == 0
+    return jnp.where(even, far, near), jnp.where(even, near, far)
+
+
+def rim_kernel(sides, grid, far_x, near_x, far, near):
+    lower, upper = lower_upper(sides[0], near_x, far_x, (2, 2, SIDE))
+    even = sides[1] == 0
+
+    def picked(block, message):
+        first, last = block[:, 0:2], block[:, SIDE - 2 : SIDE]
+        chosen = jnp.where(even, last, first) if message is near else jnp.where(even, first, last)
+        return chosen.reshape(32, LANES).astype(BF16)
+
+    for message, at in ((near, 6 - 6 * sides[1]), (far, 6 * sides[1])):
         for field in range(2):
             base = field * 192
-            message[base : base + 32] = (
-                lower[field, :, at : at + 2].reshape(32, LANES).astype(BF16)
-            )
-            message[base + 32 : base + 160] = (
-                grid[field, :, at : at + 2].reshape(128, LANES).astype(BF16)
-            )
-            message[base + 160 : base + 192] = (
-                upper[field, :, at : at + 2].reshape(32, LANES).astype(BF16)
-            )
+            message[base : base + 32] = picked(lower[field], message)
+            own = grid[field, :, pl.ds(at, 2)].reshape(128, LANES)
+            message[base + 32 : base + 160] = own.astype(BF16)
+            message[base + 160 : base + 192] = picked(upper[field], message)
 
 
 def with_neighbours(value):
@@ -167,7 +174,7 @@
 
 
 def gradient_kernel(
-    side, grid, below, above, left, right, one_far, two_far, gain_far, bias_far,
+    sides, grid, far_x, near_x, far_y, near_y, one_far, two_far, gain_far, bias_far,
     keep, send, inner,
     field_ref, stack_ref, windows, terms_one, terms_two, packed_all,
     rows_ref, columns_ref, weight_one, weight_two, gain_ref, bias_ref, sems,
@@ -175,10 +182,8 @@
     copies = started(
         ((one_far, weight_one), (two_far, weight_two), (gain_far, gain_ref), (bias_far, bias_ref)), sems
     )
-    lower = opened(below[...], (2, 2, SIDE))
-    upper = opened(above[...], (2, 2, SIDE))
-    to_left = opened(left[...], (2, SIDE + 4, 2))
-    to_right = opened(right[...], (2, SIDE + 4, 2))
+    lower, upper = lower_upper(sides[0], near_x, far_x, (2, 2, SIDE))
+    to_left, to_right = lower_upper(sides[1], near_y, far_y, (2, SIDE + 4, 2))
 
     def load_field(field):
         field_ref[2 : SIDE + 2, 2 : SIDE + 2] = grid[field]
@@ -250,8 +255,8 @@
     blank = jnp.zeros((HALF - 21 * C - 2, LANES), F32)
     packed_all[0, 21 * C : HALF] = jnp.zeros((HALF - 21 * C, LANES), F32)
     packed_all[1, 21 * C : HALF] = jnp.concatenate([gain_term, bias_term, blank], axis=0)
-    keep[...] = packed_all[side[0]]
-    send[...] = packed_all[1 - side[0]]
+    keep[...] = packed_all[sides[0]]
+    send[...] = packed_all[1 - sides[0]]
 
 
 def output_kernel(
@@ -310,9 +315,9 @@
         grad[tap] = parts[(tap - 6) * C : (tap - 5) * C].astype(F32)[:, 0:C] * scale
 
 
-def finish_kernel(scale, side, mine, other, grad_one, grad_two, grad_gain, grad_bias, parts):
-    parts[side[0]] = mine[...]
-    parts[1 - side[0]] = other[...]
+def finish_kernel(scale, sides, mine, other, grad_one, grad_two, grad_gain, grad_bias, parts):
+    parts[sides[0]] = mine[...]
+    parts[1 - sides[0]] = other[...]
     unpack(scale, parts.at[0], grad_one)
     unpack(scale, parts.at[1], grad_two)
     rest = parts[1, 21 * C : HALF].astype(F32) * scale
@@ -324,11 +329,11 @@
     return jax.ShapeDtypeStruct(dims, dtype)
 
 
-def dense_parts(features, cotangent, slots):
+def dense_parts(sides, features, cotangent, slots):
     return call(
         grid_kernel,
         (shape((2, SIDE, SIDE, SIDE, LANES), F32), shape((256, LANES), BF16), shape((256, LANES), BF16)),
-        [HBM_SPEC] * 3,
+        [SMEM_SPEC] + [HBM_SPEC] * 3,
         scratch=[
             pltpu.VMEM((4, 16, SIDE, LANES), F32),
             pltpu.SMEM(slots.shape, jnp.int32),
@@ -338,17 +343,17 @@
         ],
         moved=2_000_000,
         name="dense_grid",
-    )(*far(slots, features, cotangent))
-
-
-def rims(grid, below, above):
+    )(sides, *kept_far(slots, features, cotangent))
+
+
+def rims(sides, grid, far_x, near_x):
     return call(
         rim_kernel,
         (shape((384, LANES), BF16), shape((384, LANES), BF16)),
-        [VMEM_SPEC] * 3,
+        [SMEM_SPEC] + [VMEM_SPEC] * 3,
         moved=1_500_000,
         name="rims",
-    )(grid, below, above)
+    )(sides, grid, far_x, near_x)
 
 
 def weight_scratch():
@@ -381,7 +386,7 @@
         moved=8_000_000,
         name="gradients",
         room=28,
-    )(side, grid, *halos, *far(weight_one, weight_two, gain.reshape(1, C), bias.reshape(1, C)))
+    )(side, grid, *halos, *kept_far(weight_one, weight_two, gain.reshape(1, C), bias.reshape(1, C)))
 
 
 def outputs(slots, grid, inner, weight_one, weight_two):
@@ -400,7 +405,7 @@
         moved=4_000_000,
         name="outputs",
         room=18,
-    )(slots, grid, inner, *far(weight_one, weight_two))
+    )(slots, grid, inner, *kept_far(weight_one, weight_two))
 
 
 def finish(side, mine, other, scale):
@@ -429,39 +434,41 @@
     return lax.ppermute(block, "core", [(0, 1), (1, 0)])
 
 
-def reduce_all(keep, send):
+def reduce_all(keep, send, beside):
     pair = (keep + other_core(send)).astype(BF16)
     parts = lax.all_to_all(pair.reshape(lax.axis_size(PLANE), -1, LANES), PLANE, 0, 0)
     chunk = jnp.sum(parts.astype(F32), axis=0)
-    chunk = jnp.sum(spread_out(chunk, LINE), axis=0)
-    return spread_out(chunk.astype(BF16), PLANE).reshape(HALF, LANES)
+    chunks, beside = lax.optimization_barrier((spread_out(chunk, LINE), beside))
+    chunk = jnp.sum(chunks, axis=0)
+    return spread_out(chunk.astype(BF16), PLANE).reshape(HALF, LANES), beside
 
 
 GX = ("y", "zh", "core")
 GY = ("zl", "zp", "x")
 
 
-def passed_along(block, axis, distance):
-    devices = range(lax.axis_size(axis))
-    route = [(i - distance, i) for i in devices if i - distance in devices]
-    return lax.ppermute(block, axis, route)
+def swapped(far, near, axis):
+    count = lax.axis_size(axis)
+    ends = {n: n + 1 for n in range(1, count - 1, 2)}
+    route = [pair for low, high in ends.items() for pair in ((low, high), (high, low))]
+    far = lax.ppermute(far, axis, route)
+    near = lax.ppermute(near, axis, [(n, n ^ 1) for n in range(count)])
+    return far, near
 
 
 def body(features, cotangent, brick_slot, weight_one, weight_two, gain, bias):
-    side = lax.axis_index("core").reshape(1)
-    grid, low, high = dense_parts(features, cotangent, brick_slot)
-    below = passed_along(high, GX, 1)
-    above = passed_along(low, GX, -1)
-    low, high = rims(grid, below, above)
-    left = passed_along(high, GY, 1)
-    right = passed_along(low, GY, -1)
-    keep, send, inner = gradients(side, grid, (below, above, left, right), weight_one, weight_two, gain, bias)
+    sides = jnp.stack([lax.axis_index("core"), lax.axis_index("x") & 1])
+    grid, far, near = dense_parts(sides, features, cotangent, brick_slot)
+    around_x = swapped(far, near, GX)
+    far, near = rims(sides, grid, *around_x)
+    halos = (*around_x, *swapped(far, near, GY))
+    keep, send, inner = gradients(sides, grid, halos, weight_one, weight_two, gain, bias)
     out, grad = outputs(brick_slot, grid, inner, weight_one, weight_two)
     out, grad = out.reshape(features.shape), grad.reshape(features.shape)
-    mine, out, grad = lax.optimization_barrier((reduce_all(keep, send), out, grad))
+    mine, (out, grad) = reduce_all(keep, send, (out, grad))
     other = other_core(mine)
     scale = 1.0 / math.sqrt(lax.axis_size(GX) * lax.axis_size(GY) * 256)
-    grad_one, grad_two, grad_gain, grad_bias = finish(side, mine, other, scale)
+    grad_one, grad_two, grad_gain, grad_bias = finish(sides, mine, other, scale)
     return (
         out,
         grad,

time: 116 us -> 114 us (0.983)
  blocking collectives: 50.1 us -> 34.4 us
  starting transfers between devices: 27.7 us -> 39 us
  Pallas kernels: 16.1 us -> 18.3 us
    all_to_all x1, blocking collectives: 28.1 us -> 12.9 us  [spread_out(): return lax.all_to_all(copies, axes, 0, 0)]
    all_to_all x1, waiting for transfers between devices: 2.21 us -> 10.6 us  [spread_out(): return lax.all_to_all(copies, axes, 0, 0)]
    ppermute x4, waiting for transfers between devices: 11.6 us -> 3.93 us  [the longest x2 3.92 us: swapped(): near = lax.ppermute(near, axis, [(n, n ^ 1) for n in range(count)])]
    all_to_all x1, starting transfers between devices: 3.89 us -> 10.6 us  [spread_out(): return lax.all_to_all(copies, axes, 0, 0)]
    ppermute x2, starting transfers between devices: 7.32 us -> 10 us  [other_core(): return lax.ppermute(block, 'core', [(0, 1), (1, 0)])]
    ppermute x4, starting transfers between devices: 16.5 us -> 18.4 us  [the longest x2 10.9 us: swapped(): far = lax.ppermute(far, axis, route)]
  transfers between devices with their start and end apart: 7 -> 7, of which waited for: 6 -> 5; matrix products, arithmetic and copies ran while one was open for 1% -> 1% of each run, Pallas kernels for 5% -> 6%
where the time goes in v5:
time: 114 us; the launch traced here: 113 us
  starting transfers between devices  39 us (34%)
  blocking collectives  34.4 us (30%)
  Pallas kernels  18.3 us (16%)
  waiting for transfers between devices  18.3 us (16%)
  local copies, waits for them, and re-layouts  2.38 us (2%)
    all_to_all x1, blocking collectives, reduce_all(): lax.all_to_all(pair.reshape(lax.axis_size(PLANE), -1, LANES), PLANE, 0, 0)  21.6 us
    all_to_all x1, blocking collectives, spread_out(): return lax.all_to_all(copies, axes, 0, 0)  12.9 us
    ppermute x2, starting transfers between devices, swapped(): far = lax.ppermute(far, axis, route)  10.9 us
    all_to_all x1, starting transfers between devices, spread_out(): return lax.all_to_all(copies, axes, 0, 0)  10.6 us
    all_to_all x1, waiting for transfers between devices, spread_out(): return lax.all_to_all(copies, axes, 0, 0)  10.6 us
    ppermute x2, starting transfers between devices, other_core(): return lax.ppermute(block, 'core', [(0, 1), (1, 0)])  10 us
    ppermute x2, starting transfers between devices, swapped(): near = lax.ppermute(near, axis, [(n, n ^ 1) for n in range(count)])  7.49 us
    pallas_call x1, Pallas kernels, gradients(): call(gradient_kernel, (shape((HALF, LANES), F32), shape((HALF, LANES), F3...  7.04 us
  transfers between devices with their start and end apart: 7, of which 5 were waited for; matrix products, arithmetic and copies ran while one was open for 1% of the time, Pallas kernels for 6%

profile of v5, /device:TPU:1, one launch (start us, length us, event | category | flops | bytes accessed | tf_op | source)
XLA Modules:
  0.0 113.4 jit_solution(12281078426269261041)
XLA Ops:
  0.6 0.1 pad_add_fusion.sides
  0.7 1.8 %dense_grid.1 = (f32[2,8,8,8,128]{4,3,2,1,0:T(8,128)S(1)}, bf16[256,128]{1,0:T(8,128)(2,1)S(1)}, bf16[256,128]{1,0:T(8,128)(2,1)S(1)}) custom-call(s32[2]{0:T(128)S(1)} %pad_add_fusion.sides, s32[1,1,2,2,2]{4,3,2,1,0:T(2,128)} %slots.1, bf16[1,1,4,6144]{3,2,1,0:T(4,128)(2,1)} %features_far.1, bf16[1,1,4,6144]{3,2,1,0:T(4,128)(2,1)} %cotangent_far.1), custom_call_target="tpu_custom_call" | custom-call | bytes 2000000 | tf_op jit(solution)/shard_map/dense_grid/pallas_call | solution.py:333
  2.6 10.2 %collective-permute-start = (bf16[256,128]{1,0:T(8,128)(2,1)S(1)}, bf16[256,128]{1,0:T(8,128)(2,1)S(1)}, u32[]{:S(2)}, u32[]{:S(2)}) collective-permute-start(bf16[256,128]{1,0:T(8,128)(2,1)S(1)} %get-tuple-element.24), channel_id=1, source_target_pairs={{16,32},{32,16},{48,64},{64,48},{80,96},{96,80},{112,128},{128,112... | collective-permute-start | bytes 196616 | tf_op jit(solution)/shard_map/ppermute | solution.py:454
  12.8 1.9 %collective-permute-start.1 = (bf16[256,128]{1,0:T(8,128)(2,1)S(1)}, bf16[256,128]{1,0:T(8,128)(2,1)S(1)}, u32[]{:S(2)}, u32[]{:S(2)}) collective-permute-start(bf16[256,128]{1,0:T(8,128)(2,1)S(1)} %get-tuple-element.25), channel_id=1, source_target_pairs={{0,16},{16,0},{32,48},{48,32},{64,80},{80,64},{96,112},{112,96},{1... | collective-permute-start | bytes 196616 | tf_op jit(solution)/shard_map/ppermute | solution.py:455
  14.7 0.0 collective-permute-done.far_x
  14.7 1.2 %collective-permute-done.1.near_x = bf16[256,128]{1,0:T(8,128)(2,1)S(1)} collective-permute-done((bf16[256,128]{1,0:T(8,128)(2,1)S(1)}, bf16[256,128]{1,0:T(8,128)(2,1)S(1)}, u32[]{:S(2)}, u32[]{:S(2)}) %collective-permute-start.1) | collective-permute-done | bytes 65568 | tf_op jit(solution)/shard_map/ppermute | solution.py:455
  15.9 0.6 rims.1
  16.5 0.7 collective-permute-start.2
  17.2 5.6 %collective-permute-start.3 = (bf16[384,128]{1,0:T(8,128)(2,1)S(1)}, bf16[384,128]{1,0:T(8,128)(2,1)S(1)}, u32[]{:S(2)}, u32[]{:S(2)}) collective-permute-start(bf16[384,128]{1,0:T(8,128)(2,1)S(1)} %get-tuple-element.27), channel_id=1, source_target_pairs={{0,1},{1,0},{2,3},{3,2},{4,5},{5,4},{6,7},{7,6},{8,9},{9,8},{10,11... | collective-permute-start | bytes 294920 | tf_op jit(solution)/shard_map/ppermute | solution.py:455
  22.7 0.0 collective-permute-done.2.far_y
  22.8 2.7 %collective-permute-done.3.near_y = bf16[384,128]{1,0:T(8,128)(2,1)S(1)} collective-permute-done((bf16[384,128]{1,0:T(8,128)(2,1)S(1)}, bf16[384,128]{1,0:T(8,128)(2,1)S(1)}, u32[]{:S(2)}, u32[]{:S(2)}) %collective-permute-start.3) | collective-permute-done | bytes 98336 | tf_op jit(solution)/shard_map/ppermute | solution.py:455
  25.5 7.0 %gradients.1 = (f32[2048,128]{1,0:T(8,128)S(1)}, f32[2048,128]{1,0:T(8,128)S(1)}, bf16[1600,128]{1,0:T(8,128)(2,1)S(1)}) custom-call(s32[2]{0:T(128)S(1)} %pad_add_fusion.sides, f32[2,8,8,8,128]{4,3,2,1,0:T(8,128)S(1)} %get-tuple-element.23.grid, bf16[256,128]{1,0:T(8,128)(2,1)S(1)} %collective-permute-done.far_x, ...), custom_call_target="tpu_custom_call" | custom-call | flops 2400000000 | bytes 8000000 | tf_op jit(solution)/shard_map/gradients/pallas_call | solution.py:369
  32.5 2.9 %collective-permute-start.4 = (f32[2048,128]{1,0:T(8,128)S(1)}, f32[2048,128]{1,0:T(8,128)S(1)}, u32[]{:S(2)}, u32[]{:S(2)}) collective-permute-start(f32[2048,128]{1,0:T(8,128)S(1)} %get-tuple-element.29), channel_id=1, source_target_pairs={{0,16},{16,0},{1,17},{17,1},{2,18},{18,2},{3,19},{19,3},{4,20},{20... | collective-permute-start | bytes 3145736 | tf_op jit(solution)/shard_map/ppermute | solution.py:434
  35.4 2.3 %collective-permute-done.4 = f32[2048,128]{1,0:T(8,128)S(1)} collective-permute-done((f32[2048,128]{1,0:T(8,128)S(1)}, f32[2048,128]{1,0:T(8,128)S(1)}, u32[]{:S(2)}, u32[]{:S(2)}) %collective-permute-start.4) | collective-permute-done | bytes 1048608 | tf_op jit(solution)/shard_map/ppermute | solution.py:434
  37.7 0.1 add_convert_fusion
  37.8 0.0 copy-start
  37.8 21.6 %all_to_all.15 = bf16[32,64,128]{2,1,0:T(8,128)(2,1)S(1)} all-to-all(bf16[32,64,128]{2,1,0:T(8,128)(2,1)S(1)} %bitcast.10), channel_id=1, replica_groups=mesh['y'=4,'zh'=4,'core'=2,'zl'=2,'zp'=2,'x'=4] {'y','x','zp'}, dimensions={0} | all-to-all | bytes 1048576 | tf_op jit(solution)/shard_map/all_to_all | solution.py:439
  59.4 0.1 convert_reduce_fusion
  59.5 0.7 broadcast_in_dim.6
  60.2 10.6 %all-to-all-start.1 = ((f32[8,64,128]{2,1,0:T(8,128)}), f32[8,64,128]{2,1,0:T(8,128)S(1)}, u32[]{:S(2)}, u32[]{:S(2)}) async-start(f32[8,64,128]{2,1,0:T(8,128)} %broadcast_in_dim.6), calls=%async_computation.1 | async-start | bytes 524288 | tf_op jit(solution)/shard_map/all_to_all | solution.py:430
  70.8 0.0 copy-done
  70.8 6.2 %outputs.1 = (bf16[4,64,96]{2,1,0:T(8,128)(2,1)S(1)}, bf16[4,64,96]{2,1,0:T(8,128)(2,1)S(1)}) custom-call(s32[1,1,2,2,2]{4,3,2,1,0:T(2,128)S(1)} %copy-done, f32[2,8,8,8,128]{4,3,2,1,0:T(8,128)S(1)} %get-tuple-element.23.grid, bf16[1600,128]{1,0:T(8,128)(2,1)S(1)} %get-tuple-element.30.inner, bf16[27,96,96]{2,1,0:T(8,128)(2,1)} %one_far.3, ...), custom_call_target="tpu_custom_call" | custom-call | flops 900000000 | bytes 4000000 | tf_op jit(solution)/shard_map/outputs/pallas_call | solution.py:394
  77.1 0.8 reshape.39
  77.8 0.8 reshape.40
  78.6 10.6 %all-to-all-done.1 = f32[8,64,128]{2,1,0:T(8,128)S(1)} async-done(((f32[8,64,128]{2,1,0:T(8,128)}), f32[8,64,128]{2,1,0:T(8,128)S(1)}, u32[]{:S(2)}, u32[]{:S(2)}) %all-to-all-start.1) | async-done | bytes 262176 | tf_op jit(solution)/shard_map/all_to_all | solution.py:430
  89.2 0.1 broadcast_in_dim.7
  89.3 12.9 %all_to_all.16 = bf16[32,64,128]{2,1,0:T(8,128)(2,1)S(1)} all-to-all(bf16[32,64,128]{2,1,0:T(8,128)(2,1)S(1)} %broadcast_in_dim.7), channel_id=1, replica_groups=mesh['y'=4,'zh'=4,'core'=2,'zl'=2,'zp'=2,'x'=4] {'y','x','zp'}, dimensions={0} | all-to-all | bytes 1048576 | tf_op jit(solution)/shard_map/all_to_all | solution.py:430
  102.2 7.1 %collective-permute-start.5 = (bf16[2048,128]{1,0:T(8,128)(2,1)S(1)}, bf16[2048,128]{1,0:T(8,128)(2,1)S(1)}, u32[]{:S(2)}, u32[]{:S(2)}) collective-permute-start(bf16[2048,128]{1,0:T(8,128)(2,1)S(1)} %bitcast.8), channel_id=1, source_target_pairs={{0,16},{16,0},{1,17},{17,1},{2,18},{18,2},{3,19},{19,3},{4,20},{20... | collective-permute-start | bytes 1572872 | tf_op jit(solution)/shard_map/ppermute | solution.py:434
  109.3 1.5 %collective-permute-done.5.other = bf16[2048,128]{1,0:T(8,128)(2,1)S(1)} collective-permute-done((bf16[2048,128]{1,0:T(8,128)(2,1)S(1)}, bf16[2048,128]{1,0:T(8,128)(2,1)S(1)}, u32[]{:S(2)}, u32[]{:S(2)}) %collective-permute-start.5) | collective-permute-done | bytes 524320 | tf_op jit(solution)/shard_map/ppermute | solution.py:434
  110.8 2.6 %finish.1 = (f32[27,96,96]{2,1,0:T(8,128)}, f32[27,96,96]{2,1,0:T(8,128)}, f32[1,96]{1,0:T(1,128)}, f32[1,96]{1,0:T(1,128)}) custom-call(s32[2]{0:T(128)S(1)} %pad_add_fusion.sides, bf16[2048,128]{1,0:T(8,128)(2,1)S(1)} %bitcast.9, bf16[2048,128]{1,0:T(8,128)(2,1)S(1)} %collective-permute-done.5.other), custom_call_target="tpu_custom_call" | custom-call | bytes 4000000 | tf_op jit(solution)/shard_map/finish/pallas_call | solution.py:413
  (1 shorter events, 0.0 us)
Async XLA Ops:
  2.6 12.1 %collective-permute-start = (bf16[256,128]{1,0:T(8,128)(2,1)S(1)}, bf16[256,128]{1,0:T(8,128)(2,1)S(1)}, u32[]{:S(2)}, u32[]{:S(2)}) collective-permute-start(bf16[256,128]{1,0:T(8,128)(2,1)S(1)} %get-tuple-element.24), channel_id=1, source_target_pairs={{16,32},{32,16},{48,64},{64,48},{80,96},{96,80},{112,128},{128,112... | collective-permute-start | bytes 196616 | tf_op jit(solution)/shard_map/ppermute | solution.py:454
  12.8 3.1 %collective-permute-start.1 = (bf16[256,128]{1,0:T(8,128)(2,1)S(1)}, bf16[256,128]{1,0:T(8,128)(2,1)S(1)}, u32[]{:S(2)}, u32[]{:S(2)}) collective-permute-start(bf16[256,128]{1,0:T(8,128)(2,1)S(1)} %get-tuple-element.25), channel_id=1, source_target_pairs={{0,16},{16,0},{32,48},{48,32},{64,80},{80,64},{96,112},{112,96},{1... | collective-permute-start | bytes 196616 | tf_op jit(solution)/shard_map/ppermute | solution.py:455
  16.5 6.3 %collective-permute-start.2 = (bf16[384,128]{1,0:T(8,128)(2,1)S(1)}, bf16[384,128]{1,0:T(8,128)(2,1)S(1)}, u32[]{:S(2)}, u32[]{:S(2)}) collective-permute-start(bf16[384,128]{1,0:T(8,128)(2,1)S(1)} %get-tuple-element.26), channel_id=1, source_target_pairs={{1,2},{2,1},{3,4},{4,3},{5,6},{6,5},{7,8},{8,7},{9,10},{10,9},{11,... | collective-permute-start | bytes 294920 | tf_op jit(solution)/shard_map/ppermute | solution.py:454
  17.2 8.3 %collective-permute-start.3 = (bf16[384,128]{1,0:T(8,128)(2,1)S(1)}, bf16[384,128]{1,0:T(8,128)(2,1)S(1)}, u32[]{:S(2)}, u32[]{:S(2)}) collective-permute-start(bf16[384,128]{1,0:T(8,128)(2,1)S(1)} %get-tuple-element.27), channel_id=1, source_target_pairs={{0,1},{1,0},{2,3},{3,2},{4,5},{5,4},{6,7},{7,6},{8,9},{9,8},{10,11... | collective-permute-start | bytes 294920 | tf_op jit(solution)/shard_map/ppermute | solution.py:455
  32.5 5.2 %collective-permute-start.4 = (f32[2048,128]{1,0:T(8,128)S(1)}, f32[2048,128]{1,0:T(8,128)S(1)}, u32[]{:S(2)}, u32[]{:S(2)}) collective-permute-start(f32[2048,128]{1,0:T(8,128)S(1)} %get-tuple-element.29), channel_id=1, source_target_pairs={{0,16},{16,0},{1,17},{17,1},{2,18},{18,2},{3,19},{19,3},{4,20},{20... | collective-permute-start | bytes 3145736 | tf_op jit(solution)/shard_map/ppermute | solution.py:434
  37.8 33.0 %copy-start = (s32[1,1,2,2,2]{4,3,2,1,0:T(2,128)S(1)}, s32[1,1,2,2,2]{4,3,2,1,0:T(2,128)}, u32[]{:S(2)}) copy-start(s32[1,1,2,2,2]{4,3,2,1,0:T(2,128)} %slots.1) | copy-start | bytes 100
  60.2 29.0 %all-to-all-start.1 = ((f32[8,64,128]{2,1,0:T(8,128)}), f32[8,64,128]{2,1,0:T(8,128)S(1)}, u32[]{:S(2)}, u32[]{:S(2)}) async-start(f32[8,64,128]{2,1,0:T(8,128)} %broadcast_in_dim.6), calls=%async_computation.1 | async-start | bytes 524288 | tf_op jit(solution)/shard_map/all_to_all | solution.py:430
  102.2 8.6 %collective-permute-start.5 = (bf16[2048,128]{1,0:T(8,128)(2,1)S(1)}, bf16[2048,128]{1,0:T(8,128)(2,1)S(1)}, u32[]{:S(2)}, u32[]{:S(2)}) collective-permute-start(bf16[2048,128]{1,0:T(8,128)(2,1)S(1)} %bitcast.8), channel_id=1, source_target_pairs={{0,16},{16,0},{1,17},{17,1},{2,18},{18,2},{3,19},{19,3},{4,20},{20... | collective-permute-start | bytes 1572872 | tf_op jit(solution)/shard_map/ppermute | solution.py:434

commit v6 on v5

--- a/solution.py
+++ b/solution.py
@@ -58,13 +58,14 @@
 
 
 def grid_kernel(
-    sides, slots_far, features_far, cotangent_far, grid, far, near,
+    slots_far, features_far, cotangent_far, grid, far, near,
     lines, slots, features, cotangent, sems,
 ):
     copies = started(
         ((features_far, features), (cotangent_far, cotangent), (slots_far, slots)), sems
     )
     copies[2].wait()
+    sides = parities()
     lane = lax.broadcasted_iota(jnp.int32, (16, 4, LANES), 2)
     spot = lax.broadcasted_iota(jnp.int32, (16, SIDE, LANES), 1)
     for field, source in enumerate((features, cotangent)):
@@ -103,6 +104,10 @@
     return pltpu.roll(value.reshape(64, LANES), shift, 1).reshape(16, 4, LANES)
 
 
+def parities():
+    return lax.axis_index("core"), lax.axis_index("x") & 1
+
+
 def opened(message, lead):
     return message.astype(F32).reshape(lead + (SIDE, LANES))
 
@@ -113,7 +118,8 @@
     return jnp.where(even, far, near), jnp.where(even, near, far)
 
 
-def rim_kernel(sides, grid, far_x, near_x, far, near):
+def rim_kernel(grid, far_x, near_x, far, near):
+    sides = parities()
     lower, upper = lower_upper(sides[0], near_x, far_x, (2, 2, SIDE))
     even = sides[1] == 0
 
@@ -161,27 +167,41 @@
         columns_ref[0:C, tap * LANES : tap * LANES + C] = kernel[TAPS - 1 - tap]
 
 
-def plain_dot(left, right):
-    return jnp.dot(left, right, preferred_element_type=F32)
-
-
-def turned_dot(left, right):
-    return lax.dot_general(left, right, (((1,), (1,)), ((), ())), preferred_element_type=F32)
-
-
-def rounded(value):
-    return value.astype(BF16).astype(F32)
-
-
-def gradient_kernel(
-    sides, grid, far_x, near_x, far_y, near_y, one_far, two_far, gain_far, bias_far,
-    keep, send, inner,
-    field_ref, stack_ref, windows, terms_one, terms_two, packed_all,
-    rows_ref, columns_ref, weight_one, weight_two, gain_ref, bias_ref, sems,
+def prepare_kernel(
+    one_far, two_far, gain_far, bias_far, rows_ref, columns_ref, gain_bias,
+    weight_one, weight_two, gain_ref, bias_ref, sems,
 ):
     copies = started(
         ((one_far, weight_one), (two_far, weight_two), (gain_far, gain_ref), (bias_far, bias_ref)), sems
     )
+    for copy in copies:
+        copy.wait()
+    spread(weight_one, rows_ref)
+    spread_flipped(weight_two, columns_ref)
+    gain_bias[...] = jnp.zeros_like(gain_bias)
+    gain_bias[0:1, 0:C] = gain_ref[...]
+    gain_bias[1:2, 0:C] = bias_ref[...]
+
+
+def plain_dot(left, right):
+    return jnp.dot(left, right, preferred_element_type=F32)
+
+
+def turned_dot(left, right):
+    return lax.dot_general(left, right, (((1,), (1,)), ((), ())), preferred_element_type=F32)
+
+
+def rounded(value):
+    return value.astype(BF16).astype(F32)
+
+
+def gradient_kernel(
+    grid, far_x, near_x, far_y, near_y, rows_ref, columns_ref, gain_bias,
+    keep, send, inner,
+    field_ref, stack_ref, windows, terms_one, terms_two, packed_all,
+):
+    sides = parities()
+    gain, bias = gain_bias[0:1], gain_bias[1:2]
     lower, upper = lower_upper(sides[0], near_x, far_x, (2, 2, SIDE))
     to_left, to_right = lower_upper(sides[1], near_y, far_y, (2, SIDE + 4, 2))
 
@@ -196,13 +216,6 @@
     mark = field_ref[1 : SIDE + 3, 1 : SIDE + 3].reshape(RIM, LANES)[:, C : C + 1]
     stack_ref[...] = with_neighbours(field_ref[...])
     fill_windows(windows, stack_ref, 0, SIDE + 2)
-    for copy in copies:
-        copy.wait()
-    spread(weight_one, rows_ref)
-    spread_flipped(weight_two, columns_ref)
-    blank = jnp.zeros((1, LANES - C), F32)
-    gain = jnp.concatenate([gain_ref[...], blank], axis=1)
-    bias = jnp.concatenate([bias_ref[...], blank], axis=1)
     first_conv = plain_dot(windows[...], rows_ref[...]) * mark
     pre = first_conv * gain + bias
     gate = 1.0 / (1.0 + jnp.exp(-pre))
@@ -315,7 +328,8 @@
         grad[tap] = parts[(tap - 6) * C : (tap - 5) * C].astype(F32)[:, 0:C] * scale
 
 
-def finish_kernel(scale, sides, mine, other, grad_one, grad_two, grad_gain, grad_bias, parts):
+def finish_kernel(scale, mine, other, grad_one, grad_two, grad_gain, grad_bias, parts):
+    sides = parities()
     parts[sides[0]] = mine[...]
     parts[1 - sides[0]] = other[...]
     unpack(scale, parts.at[0], grad_one)
@@ -329,11 +343,11 @@
     return jax.ShapeDtypeStruct(dims, dtype)
 
 
-def dense_parts(sides, features, cotangent, slots):
+def dense_parts(features, cotangent, slots):
     return call(
         grid_kernel,
         (shape((2, SIDE, SIDE, SIDE, LANES), F32), shape((256, LANES), BF16), shape((256, LANES), BF16)),
-        [SMEM_SPEC] + [HBM_SPEC] * 3,
+        [HBM_SPEC] * 3,
         scratch=[
             pltpu.VMEM((4, 16, SIDE, LANES), F32),
             pltpu.SMEM(slots.shape, jnp.int32),
@@ -343,17 +357,17 @@
         ],
         moved=2_000_000,
         name="dense_grid",
-    )(sides, *kept_far(slots, features, cotangent))
-
-
-def rims(sides, grid, far_x, near_x):
+    )(*kept_far(slots, features, cotangent))
+
+
+def rims(grid, far_x, near_x):
     return call(
         rim_kernel,
         (shape((384, LANES), BF16), shape((384, LANES), BF16)),
-        [SMEM_SPEC] + [VMEM_SPEC] * 3,
+        [VMEM_SPEC] * 3,
         moved=1_500_000,
         name="rims",
-    )(sides, grid, far_x, near_x)
+    )(grid, far_x, near_x)
 
 
 def weight_scratch():
@@ -365,11 +379,29 @@
     ]
 
 
-def gradients(side, grid, halos, weight_one, weight_two, gain, bias):
+def prepare(weight_one, weight_two, gain, bias):
+    prepared = call(
+        prepare_kernel,
+        (shape((SPAN, LANES), BF16), shape((LANES, SPAN), BF16), shape((2, LANES), F32)),
+        [HBM_SPEC] * 4,
+        scratch=[
+            pltpu.VMEM((TAPS, C, C), BF16),
+            pltpu.VMEM((TAPS, C, C), BF16),
+            pltpu.VMEM((1, C), F32),
+            pltpu.VMEM((1, C), F32),
+            pltpu.SemaphoreType.DMA((4,)),
+        ],
+        moved=3_000_000,
+        name="prepare",
+    )(*kept_far(weight_one, weight_two, gain.reshape(1, C), bias.reshape(1, C)))
+    return [pltpu.with_memory_space_constraint(array, pltpu.VMEM) for array in prepared]
+
+
+def gradients(grid, halos, rows, columns, gain_bias):
     return call(
         gradient_kernel,
         (shape((HALF, LANES), F32), shape((HALF, LANES), F32), shape((2 * RIM, LANES), BF16)),
-        [SMEM_SPEC] + [VMEM_SPEC] * 5 + [HBM_SPEC] * 4,
+        [VMEM_SPEC] * 8,
         scratch=[
             pltpu.VMEM((SIDE + 4, SIDE + 4, SIDE, LANES), F32),
             pltpu.VMEM((SIDE + 4, SIDE + 4, SIDE, 3 * LANES), F32),
@@ -377,16 +409,12 @@
             pltpu.VMEM((LANES, SPAN), F32),
             pltpu.VMEM((LANES, SPAN), F32),
             pltpu.VMEM((2, HALF, LANES), F32),
-            *weight_scratch(),
-            pltpu.VMEM((1, C), F32),
-            pltpu.VMEM((1, C), F32),
-            pltpu.SemaphoreType.DMA((4,)),
         ],
         flops=2_400_000_000,
         moved=8_000_000,
         name="gradients",
         room=28,
-    )(side, grid, *halos, *kept_far(weight_one, weight_two, gain.reshape(1, C), bias.reshape(1, C)))
+    )(grid, *halos, rows, columns, gain_bias)
 
 
 def outputs(slots, grid, inner, weight_one, weight_two):
@@ -408,16 +436,16 @@
     )(slots, grid, inner, *kept_far(weight_one, weight_two))
 
 
-def finish(side, mine, other, scale):
+def finish(mine, other, scale):
     grads, line = shape((TAPS, C, C), F32), shape((1, C), F32)
     return call(
         functools.partial(finish_kernel, scale),
         (grads, grads, line, line),
-        [SMEM_SPEC, VMEM_SPEC, VMEM_SPEC],
+        [VMEM_SPEC, VMEM_SPEC],
         scratch=[pltpu.VMEM((2, HALF, LANES), BF16)],
         moved=4_000_000,
         name="finish",
-    )(side, mine, other)
+    )(mine, other)
 
 
 SIZES = dict(y=4, zh=4, core=2, zl=2, zp=2, x=4)
@@ -457,18 +485,19 @@
 
 
 def body(features, cotangent, brick_slot, weight_one, weight_two, gain, bias):
-    sides = jnp.stack([lax.axis_index("core"), lax.axis_index("x") & 1])
-    grid, far, near = dense_parts(sides, features, cotangent, brick_slot)
+    grid, far, near = dense_parts(features, cotangent, brick_slot)
+    far, near, *given = lax.optimization_barrier((far, near, weight_one, weight_two, gain, bias))
     around_x = swapped(far, near, GX)
-    far, near = rims(sides, grid, *around_x)
+    around_x, prepared = lax.optimization_barrier((around_x, prepare(*given)))
+    far, near = rims(grid, *around_x)
     halos = (*around_x, *swapped(far, near, GY))
-    keep, send, inner = gradients(sides, grid, halos, weight_one, weight_two, gain, bias)
+    keep, send, inner = gradients(grid, halos, *prepared)
     out, grad = outputs(brick_slot, grid, inner, weight_one, weight_two)
     out, grad = out.reshape(features.shape), grad.reshape(features.shape)
     mine, (out, grad) = reduce_all(keep, send, (out, grad))
     other = other_core(mine)
     scale = 1.0 / math.sqrt(lax.axis_size(GX) * lax.axis_size(GY) * 256)
-    grad_one, grad_two, grad_gain, grad_bias = finish(sides, mine, other, scale)
+    grad_one, grad_two, grad_gain, grad_bias = finish(mine, other, scale)
     return (
         out,
         grad,

time: 114 us -> 111 us (0.974)
  waiting for transfers between devices: 18.3 us -> 16.7 us
  Pallas kernels: 18.3 us -> 17 us
    pallas_call x0 -> x1, Pallas kernels: none -> 1.72 us  [prepare(): call(prepare_kernel, (shape((SPAN, LANES), BF16), shape((LANES, SPAN), BF...]
    ppermute x2, waiting for transfers between devices: 3.92 us -> 2.37 us  [swapped(): near = lax.ppermute(near, axis, [(n, n ^ 1) for n in range(count)])]
    pallas_call x1, Pallas kernels: 7.04 us -> 5.51 us  [gradients(): call(gradient_kernel, (shape((HALF, LANES), F32), shape((HALF, LANES), F3...]
  transfers between devices with their start and end apart: 7 -> 7, of which waited for: 5 -> 4; matrix products, arithmetic and copies ran while one was open for 1% -> 1% of each run, Pallas kernels for 6% -> 7%
where the time goes in v6:
time: 111 us; the launch traced here: 110 us
  starting transfers between devices  38.7 us (35%)
  blocking collectives  34.5 us (31%)
  Pallas kernels  17 us (15%)
  waiting for transfers between devices  16.7 us (15%)
  local copies, waits for them, and re-layouts  2.38 us (2%)
    all_to_all x1, blocking collectives, reduce_all(): lax.all_to_all(pair.reshape(lax.axis_size(PLANE), -1, LANES), PLANE, 0, 0)  21.6 us
    all_to_all x1, blocking collectives, spread_out(): return lax.all_to_all(copies, axes, 0, 0)  12.9 us
    ppermute x2, starting transfers between devices, swapped(): far = lax.ppermute(far, axis, route)  10.9 us
    all_to_all x1, waiting for transfers between devices, spread_out(): return lax.all_to_all(copies, axes, 0, 0)  10.6 us
    ppermute x2, starting transfers between devices, other_core(): return lax.ppermute(block, 'core', [(0, 1), (1, 0)])  10.3 us
    all_to_all x1, starting transfers between devices, spread_out(): return lax.all_to_all(copies, axes, 0, 0)  10 us
    ppermute x2, starting transfers between devices, swapped(): near = lax.ppermute(near, axis, [(n, n ^ 1) for n in range(count)])  7.49 us
    pallas_call x1, Pallas kernels, outputs(): call(output_kernel, (result, result), [SMEM_SPEC] + [VMEM_SPEC] * 2 + [HB...  6.25 us
  transfers between devices with their start and end apart: 7, of which 4 were waited for; matrix products, arithmetic and copies ran while one was open for 1% of the time, Pallas kernels for 7%

profile of v6, /device:TPU:1, one launch (start us, length us, event | category | flops | bytes accessed | tf_op | source)
XLA Modules:
  0.0 110.3 jit_solution(3929105365952237514)
XLA Ops:
  0.6 1.3 %dense_grid.1 = (f32[2,8,8,8,128]{4,3,2,1,0:T(8,128)S(1)}, bf16[256,128]{1,0:T(8,128)(2,1)S(1)}, bf16[256,128]{1,0:T(8,128)(2,1)S(1)}) custom-call(s32[1,1,2,2,2]{4,3,2,1,0:T(2,128)} %slots.1, bf16[1,1,4,6144]{3,2,1,0:T(4,128)(2,1)} %features_far.1, bf16[1,1,4,6144]{3,2,1,0:T(4,128)(2,1)} %cotangent_far.1), custom_call_target="tpu_custom_call" | custom-call | bytes 2000000 | tf_op jit(solution)/shard_map/dense_grid/pallas_call | solution.py:347
  2.0 10.2 %collective-permute-start = (bf16[256,128]{1,0:T(8,128)(2,1)S(1)}, bf16[256,128]{1,0:T(8,128)(2,1)S(1)}, u32[]{:S(2)}, u32[]{:S(2)}) collective-permute-start(bf16[256,128]{1,0:T(8,128)(2,1)S(1)} %get-tuple-element.40), channel_id=1, source_target_pairs={{16,32},{32,16},{48,64},{64,48},{80,96},{96,80},{112,128},{128,112... | collective-permute-start | bytes 196616 | tf_op jit(solution)/shard_map/ppermute | solution.py:482
  12.2 1.9 %collective-permute-start.1 = (bf16[256,128]{1,0:T(8,128)(2,1)S(1)}, bf16[256,128]{1,0:T(8,128)(2,1)S(1)}, u32[]{:S(2)}, u32[]{:S(2)}) collective-permute-start(bf16[256,128]{1,0:T(8,128)(2,1)S(1)} %get-tuple-element.41), channel_id=1, source_target_pairs={{0,16},{16,0},{32,48},{48,32},{64,80},{80,64},{96,112},{112,96},{1... | collective-permute-start | bytes 196616 | tf_op jit(solution)/shard_map/ppermute | solution.py:483
  14.1 1.7 %prepare.1 = (bf16[3456,128]{1,0:T(8,128)(2,1)S(1)}, bf16[128,3456]{1,0:T(8,128)(2,1)S(1)}, f32[2,128]{1,0:T(2,128)S(1)}) custom-call(bf16[27,96,96]{2,1,0:T(8,128)(2,1)} %one_far.2, bf16[27,96,96]{2,1,0:T(8,128)(2,1)} %two_far.2, f32[1,96]{1,0:T(1,128)} %bitcast.9, f32[1,96]{1,0:T(1,128)} %bitcast.10), custom_call_target="tpu_custom_call" | custom-call | bytes 3000000 | tf_op jit(solution)/shard_map/prepare/pallas_call | solution.py:383
  15.8 0.0 collective-permute-done.far_x
  15.8 0.0 collective-permute-done.1.near_x
  15.9 0.7 collective-permute-start.2
  16.6 5.6 %collective-permute-start.3 = (bf16[384,128]{1,0:T(8,128)(2,1)S(1)}, bf16[384,128]{1,0:T(8,128)(2,1)S(1)}, u32[]{:S(2)}, u32[]{:S(2)}) collective-permute-start(bf16[384,128]{1,0:T(8,128)(2,1)S(1)} %get-tuple-element.52), channel_id=1, source_target_pairs={{0,1},{1,0},{2,3},{3,2},{4,5},{5,4},{6,7},{7,6},{8,9},{9,8},{10,11... | collective-permute-start | bytes 294920 | tf_op jit(solution)/shard_map/ppermute | solution.py:483
  22.1 0.0 collective-permute-done.2.far_y
  22.1 2.4 %collective-permute-done.3.near_y = bf16[384,128]{1,0:T(8,128)(2,1)S(1)} collective-permute-done((bf16[384,128]{1,0:T(8,128)(2,1)S(1)}, bf16[384,128]{1,0:T(8,128)(2,1)S(1)}, u32[]{:S(2)}, u32[]{:S(2)}) %collective-permute-start.3) | collective-permute-done | bytes 98336 | tf_op jit(solution)/shard_map/ppermute | solution.py:483
  24.5 5.5 %gradients.1 = (f32[2048,128]{1,0:T(8,128)S(1)}, f32[2048,128]{1,0:T(8,128)S(1)}, bf16[1600,128]{1,0:T(8,128)(2,1)S(1)}) custom-call(f32[2,8,8,8,128]{4,3,2,1,0:T(8,128)S(1)} %get-tuple-element.37.grid, bf16[256,128]{1,0:T(8,128)(2,1)S(1)} %collective-permute-done.far_x, bf16[256,128]{1,0:T(8,128)(2,1)S(1)} %collective-permute-done.1.near_x, ...), custom_call_target="tpu_custom_call" | custom-call | flops 2400000000 | bytes 8000000 | tf_op jit(solution)/shard_map/gradients/pallas_call | solution.py:401
  30.0 3.3 %collective-permute-start.4 = (f32[2048,128]{1,0:T(8,128)S(1)}, f32[2048,128]{1,0:T(8,128)S(1)}, u32[]{:S(2)}, u32[]{:S(2)}) collective-permute-start(f32[2048,128]{1,0:T(8,128)S(1)} %get-tuple-element.57), channel_id=1, source_target_pairs={{0,16},{16,0},{1,17},{17,1},{2,18},{18,2},{3,19},{19,3},{4,20},{20... | collective-permute-start | bytes 3145736 | tf_op jit(solution)/shard_map/ppermute | solution.py:462
  33.3 2.3 %collective-permute-done.4 = f32[2048,128]{1,0:T(8,128)S(1)} collective-permute-done((f32[2048,128]{1,0:T(8,128)S(1)}, f32[2048,128]{1,0:T(8,128)S(1)}, u32[]{:S(2)}, u32[]{:S(2)}) %collective-permute-start.4) | collective-permute-done | bytes 1048608 | tf_op jit(solution)/shard_map/ppermute | solution.py:462
  35.6 0.1 add_convert_fusion
  35.7 0.0 copy-start
  35.7 21.6 %all_to_all.15 = bf16[32,64,128]{2,1,0:T(8,128)(2,1)S(1)} all-to-all(bf16[32,64,128]{2,1,0:T(8,128)(2,1)S(1)} %bitcast.8), channel_id=1, replica_groups=mesh['y'=4,'zh'=4,'core'=2,'zl'=2,'zp'=2,'x'=4] {'y','x','zp'}, dimensions={0} | all-to-all | bytes 1048576 | tf_op jit(solution)/shard_map/all_to_all | solution.py:467
  57.3 0.1 convert_reduce_fusion
  57.4 0.7 broadcast_in_dim.6
  58.1 10.0 %all-to-all-start.1 = ((f32[8,64,128]{2,1,0:T(8,128)}), f32[8,64,128]{2,1,0:T(8,128)S(1)}, u32[]{:S(2)}, u32[]{:S(2)}) async-start(f32[8,64,128]{2,1,0:T(8,128)} %broadcast_in_dim.6), calls=%async_computation.1 | async-start | bytes 524288 | tf_op jit(solution)/shard_map/all_to_all | solution.py:458
  68.1 0.0 copy-done
  68.1 6.2 %outputs.1 = (bf16[4,64,96]{2,1,0:T(8,128)(2,1)S(1)}, bf16[4,64,96]{2,1,0:T(8,128)(2,1)S(1)}) custom-call(s32[1,1,2,2,2]{4,3,2,1,0:T(2,128)S(1)} %copy-done, f32[2,8,8,8,128]{4,3,2,1,0:T(8,128)S(1)} %get-tuple-element.37.grid, bf16[1600,128]{1,0:T(8,128)(2,1)S(1)} %get-tuple-element.58.inner, bf16[27,96,96]{2,1,0:T(8,128)(2,1)} %one_far.2, ...), custom_call_target="tpu_custom_call" | custom-call | flops 900000000 | bytes 4000000 | tf_op jit(solution)/shard_map/outputs/pallas_call | solution.py:422
  74.4 0.8 reshape.39
  75.2 0.8 reshape.40
  75.9 10.6 %all-to-all-done.1 = f32[8,64,128]{2,1,0:T(8,128)S(1)} async-done(((f32[8,64,128]{2,1,0:T(8,128)}), f32[8,64,128]{2,1,0:T(8,128)S(1)}, u32[]{:S(2)}, u32[]{:S(2)}) %all-to-all-start.1) | async-done | bytes 262176 | tf_op jit(solution)/shard_map/all_to_all | solution.py:458
  86.6 0.1 broadcast_in_dim.7
  86.7 12.9 %all_to_all.16 = bf16[32,64,128]{2,1,0:T(8,128)(2,1)S(1)} all-to-all(bf16[32,64,128]{2,1,0:T(8,128)(2,1)S(1)} %broadcast_in_dim.7), channel_id=1, replica_groups=mesh['y'=4,'zh'=4,'core'=2,'zl'=2,'zp'=2,'x'=4] {'y','x','zp'}, dimensions={0} | all-to-all | bytes 1048576 | tf_op jit(solution)/shard_map/all_to_all | solution.py:458
  99.5 7.1 %collective-permute-start.5 = (bf16[2048,128]{1,0:T(8,128)(2,1)S(1)}, bf16[2048,128]{1,0:T(8,128)(2,1)S(1)}, u32[]{:S(2)}, u32[]{:S(2)}) collective-permute-start(bf16[2048,128]{1,0:T(8,128)(2,1)S(1)} %bitcast.6), channel_id=1, source_target_pairs={{0,16},{16,0},{1,17},{17,1},{2,18},{18,2},{3,19},{19,3},{4,20},{20... | collective-permute-start | bytes 1572872 | tf_op jit(solution)/shard_map/ppermute | solution.py:462
  106.6 1.5 %collective-permute-done.5.other = bf16[2048,128]{1,0:T(8,128)(2,1)S(1)} collective-permute-done((bf16[2048,128]{1,0:T(8,128)(2,1)S(1)}, bf16[2048,128]{1,0:T(8,128)(2,1)S(1)}, u32[]{:S(2)}, u32[]{:S(2)}) %collective-permute-start.5) | collective-permute-done | bytes 524320 | tf_op jit(solution)/shard_map/ppermute | solution.py:462
  108.1 2.2 %finish.1 = (f32[27,96,96]{2,1,0:T(8,128)}, f32[27,96,96]{2,1,0:T(8,128)}, f32[1,96]{1,0:T(1,128)}, f32[1,96]{1,0:T(1,128)}) custom-call(bf16[2048,128]{1,0:T(8,128)(2,1)S(1)} %bitcast.7, bf16[2048,128]{1,0:T(8,128)(2,1)S(1)} %collective-permute-done.5.other), custom_call_target="tpu_custom_call" | custom-call | bytes 4000000 | tf_op jit(solution)/shard_map/finish/pallas_call | solution.py:441
  (2 shorter events, 0.1 us)
Async XLA Ops:
  2.0 13.9 %collective-permute-start = (bf16[256,128]{1,0:T(8,128)(2,1)S(1)}, bf16[256,128]{1,0:T(8,128)(2,1)S(1)}, u32[]{:S(2)}, u32[]{:S(2)}) collective-permute-start(bf16[256,128]{1,0:T(8,128)(2,1)S(1)} %get-tuple-element.40), channel_id=1, source_target_pairs={{16,32},{32,16},{48,64},{64,48},{80,96},{96,80},{112,128},{128,112... | collective-permute-start | bytes 196616 | tf_op jit(solution)/shard_map/ppermute | solution.py:482
  12.2 3.7 %collective-permute-start.1 = (bf16[256,128]{1,0:T(8,128)(2,1)S(1)}, bf16[256,128]{1,0:T(8,128)(2,1)S(1)}, u32[]{:S(2)}, u32[]{:S(2)}) collective-permute-start(bf16[256,128]{1,0:T(8,128)(2,1)S(1)} %get-tuple-element.41), channel_id=1, source_target_pairs={{0,16},{16,0},{32,48},{48,32},{64,80},{80,64},{96,112},{112,96},{1... | collective-permute-start | bytes 196616 | tf_op jit(solution)/shard_map/ppermute | solution.py:483
  15.9 6.3 %collective-permute-start.2 = (bf16[384,128]{1,0:T(8,128)(2,1)S(1)}, bf16[384,128]{1,0:T(8,128)(2,1)S(1)}, u32[]{:S(2)}, u32[]{:S(2)}) collective-permute-start(bf16[384,128]{1,0:T(8,128)(2,1)S(1)} %get-tuple-element.51), channel_id=1, source_target_pairs={{1,2},{2,1},{3,4},{4,3},{5,6},{6,5},{7,8},{8,7},{9,10},{10,9},{11,... | collective-permute-start | bytes 294920 | tf_op jit(solution)/shard_map/ppermute | solution.py:482
  16.6 8.0 %collective-permute-start.3 = (bf16[384,128]{1,0:T(8,128)(2,1)S(1)}, bf16[384,128]{1,0:T(8,128)(2,1)S(1)}, u32[]{:S(2)}, u32[]{:S(2)}) collective-permute-start(bf16[384,128]{1,0:T(8,128)(2,1)S(1)} %get-tuple-element.52), channel_id=1, source_target_pairs={{0,1},{1,0},{2,3},{3,2},{4,5},{5,4},{6,7},{7,6},{8,9},{9,8},{10,11... | collective-permute-start | bytes 294920 | tf_op jit(solution)/shard_map/ppermute | solution.py:483
  30.0 5.5 %collective-permute-start.4 = (f32[2048,128]{1,0:T(8,128)S(1)}, f32[2048,128]{1,0:T(8,128)S(1)}, u32[]{:S(2)}, u32[]{:S(2)}) collective-permute-start(f32[2048,128]{1,0:T(8,128)S(1)} %get-tuple-element.57), channel_id=1, source_target_pairs={{0,16},{16,0},{1,17},{17,1},{2,18},{18,2},{3,19},{19,3},{4,20},{20... | collective-permute-start | bytes 3145736 | tf_op jit(solution)/shard_map/ppermute | solution.py:462
  35.7 32.4 %copy-start = (s32[1,1,2,2,2]{4,3,2,1,0:T(2,128)S(1)}, s32[1,1,2,2,2]{4,3,2,1,0:T(2,128)}, u32[]{:S(2)}) copy-start(s32[1,1,2,2,2]{4,3,2,1,0:T(2,128)} %slots.1) | copy-start | bytes 100
  58.1 28.4 %all-to-all-start.1 = ((f32[8,64,128]{2,1,0:T(8,128)}), f32[8,64,128]{2,1,0:T(8,128)S(1)}, u32[]{:S(2)}, u32[]{:S(2)}) async-start(f32[8,64,128]{2,1,0:T(8,128)} %broadcast_in_dim.6), calls=%async_computation.1 | async-start | bytes 524288 | tf_op jit(solution)/shard_map/all_to_all | solution.py:458
  99.5 8.6 %collective-permute-start.5 = (bf16[2048,128]{1,0:T(8,128)(2,1)S(1)}, bf16[2048,128]{1,0:T(8,128)(2,1)S(1)}, u32[]{:S(2)}, u32[]{:S(2)}) collective-permute-start(bf16[2048,128]{1,0:T(8,128)(2,1)S(1)} %bitcast.6), channel_id=1, source_target_pairs={{0,16},{16,0},{1,17},{17,1},{2,18},{18,2},{3,19},{19,3},{4,20},{20... | collective-permute-start | bytes 1572872 | tf_op jit(solution)/shard_map/ppermute | solution.py:462

commit v7 on v6

--- a/solution.py
+++ b/solution.py
@@ -328,13 +328,29 @@
         grad[tap] = parts[(tap - 6) * C : (tap - 5) * C].astype(F32)[:, 0:C] * scale
 
 
-def finish_kernel(scale, mine, other, grad_one, grad_two, grad_gain, grad_bias, parts):
-    sides = parities()
-    parts[sides[0]] = mine[...]
-    parts[1 - sides[0]] = other[...]
-    unpack(scale, parts.at[0], grad_one)
-    unpack(scale, parts.at[1], grad_two)
-    rest = parts[1, 21 * C : HALF].astype(F32) * scale
+def put(held, first, grads, sem):
+    for place in range(2):
+
+        @pl.when(first == place)
+        def _():
+            copy = pltpu.make_async_copy(held, grads[place], sem)
+            copy.start()
+            copy.wait()
+
+
+def half_kernel(scale, parts, grad_one, grad_two, held, sem):
+    unpack(scale, parts, held)
+    put(held, parities()[0], (grad_one, grad_two), sem)
+
+
+def finish_kernel(
+    scale, one_in, two_in, mine, other, grad_one, grad_two, grad_gain, grad_bias, held, sem
+):
+    core = parities()[0]
+    unpack(scale, other, held)
+    put(held, core, (grad_two, grad_one), sem)
+    last = slice(21 * C, HALF)
+    rest = jnp.where(core == 1, mine[last].astype(F32), other[last].astype(F32)) * scale
     grad_gain[...] = rest[0:1, 0:C]
     grad_bias[...] = rest[1:2, 0:C]
 
@@ -436,16 +452,36 @@
     )(slots, grid, inner, *kept_far(weight_one, weight_two))
 
 
-def finish(mine, other, scale):
+FAR_OUT = pl.BlockSpec(memory_space=pltpu.HBM)
+
+
+def half_finished(mine, scale):
+    grads = shape((TAPS, C, C), F32)
+    return pl.pallas_call(
+        functools.partial(half_kernel, scale),
+        out_shape=(grads, grads),
+        in_specs=[VMEM_SPEC],
+        out_specs=(FAR_OUT, FAR_OUT),
+        scratch_shapes=[pltpu.VMEM((TAPS, C, C), F32), pltpu.SemaphoreType.DMA],
+        cost_estimate=pl.CostEstimate(flops=0, bytes_accessed=3_000_000, transcendentals=0),
+        compiler_params=pltpu.CompilerParams(vmem_limit_bytes=8 << 20),
+        name="half_finish",
+    )(mine)
+
+
+def finish(halves, mine, other, scale):
     grads, line = shape((TAPS, C, C), F32), shape((1, C), F32)
-    return call(
+    return pl.pallas_call(
         functools.partial(finish_kernel, scale),
-        (grads, grads, line, line),
-        [VMEM_SPEC, VMEM_SPEC],
-        scratch=[pltpu.VMEM((2, HALF, LANES), BF16)],
-        moved=4_000_000,
+        out_shape=(grads, grads, line, line),
+        in_specs=[HBM_SPEC, HBM_SPEC, VMEM_SPEC, VMEM_SPEC],
+        out_specs=(FAR_OUT, FAR_OUT, VMEM_SPEC, VMEM_SPEC),
+        scratch_shapes=[pltpu.VMEM((TAPS, C, C), F32), pltpu.SemaphoreType.DMA],
+        input_output_aliases={0: 0, 1: 1},
+        cost_estimate=pl.CostEstimate(flops=0, bytes_accessed=3_000_000, transcendentals=0),
+        compiler_params=pltpu.CompilerParams(vmem_limit_bytes=8 << 20),
         name="finish",
-    )(mine, other)
+    )(*halves, mine, other)
 
 
 SIZES = dict(y=4, zh=4, core=2, zl=2, zp=2, x=4)
@@ -497,7 +533,8 @@
     mine, (out, grad) = reduce_all(keep, send, (out, grad))
     other = other_core(mine)
     scale = 1.0 / math.sqrt(lax.axis_size(GX) * lax.axis_size(GY) * 256)
-    grad_one, grad_two, grad_gain, grad_bias = finish(mine, other, scale)
+    halves = half_finished(mine, scale)
+    grad_one, grad_two, grad_gain, grad_bias = finish(halves, mine, other, scale)
     return (
         out,
         grad,

time: 111 us -> 111 us (level)
  waiting for transfers between devices: 16.7 us -> 15.4 us
    ppermute x2, waiting for transfers between devices: 3.78 us -> 2.4 us  [other_core(): return lax.ppermute(block, 'core', [(0, 1), (1, 0)])]
    pallas_call x1 -> x2, Pallas kernels: 2.18 us -> 3.25 us  [the longest x1 1.89 us: finish(): pl.pallas_call(functools.partial(finish_kernel, scale), out_shape=(grads,...]
  transfers between devices with their start and end apart: 7 -> 7, of which waited for: 4 -> 4; matrix products, arithmetic and copies ran while one was open for 1% -> 1% of each run, Pallas kernels for 7% -> 8%
where the time goes in v7:
time: 111 us; the launch traced here: 110 us
  starting transfers between devices  38.7 us (35%)
  blocking collectives  34.5 us (31%)
  Pallas kernels  18.1 us (16%)
  waiting for transfers between devices  15.4 us (14%)
  local copies, waits for them, and re-layouts  2.38 us (2%)
    all_to_all x1, blocking collectives, reduce_all(): lax.all_to_all(pair.reshape(lax.axis_size(PLANE), -1, LANES), PLANE, 0, 0)  21.6 us
    all_to_all x1, blocking collectives, spread_out(): return lax.all_to_all(copies, axes, 0, 0)  12.9 us
    ppermute x2, starting transfers between devices, swapped(): far = lax.ppermute(far, axis, route)  10.9 us
    all_to_all x1, waiting for transfers between devices, spread_out(): return lax.all_to_all(copies, axes, 0, 0)  10.6 us
    ppermute x2, starting transfers between devices, other_core(): return lax.ppermute(block, 'core', [(0, 1), (1, 0)])  10.3 us
    all_to_all x1, starting transfers between devices, spread_out(): return lax.all_to_all(copies, axes, 0, 0)  10 us
    ppermute x2, starting transfers between devices, swapped(): near = lax.ppermute(near, axis, [(n, n ^ 1) for n in range(count)])  7.49 us
    pallas_call x1, Pallas kernels, outputs(): call(output_kernel, (result, result), [SMEM_SPEC] + [VMEM_SPEC] * 2 + [HB...  6.24 us
  transfers between devices with their start and end apart: 7, of which 4 were waited for; matrix products, arithmetic and copies ran while one was open for 1% of the time, Pallas kernels for 8%

profile of v7, /device:TPU:1, one launch (start us, length us, event | category | flops | bytes accessed | tf_op | source)
XLA Modules:
  0.0 110.0 jit_solution(2812040900440025116)
XLA Ops:
  0.6 1.3 %dense_grid.1 = (f32[2,8,8,8,128]{4,3,2,1,0:T(8,128)S(1)}, bf16[256,128]{1,0:T(8,128)(2,1)S(1)}, bf16[256,128]{1,0:T(8,128)(2,1)S(1)}) custom-call(s32[1,1,2,2,2]{4,3,2,1,0:T(2,128)} %slots.1, bf16[1,1,4,6144]{3,2,1,0:T(4,128)(2,1)} %features_far.1, bf16[1,1,4,6144]{3,2,1,0:T(4,128)(2,1)} %cotangent_far.1), custom_call_target="tpu_custom_call" | custom-call | bytes 2000000 | tf_op jit(solution)/shard_map/dense_grid/pallas_call | solution.py:363
  2.0 10.2 %collective-permute-start = (bf16[256,128]{1,0:T(8,128)(2,1)S(1)}, bf16[256,128]{1,0:T(8,128)(2,1)S(1)}, u32[]{:S(2)}, u32[]{:S(2)}) collective-permute-start(bf16[256,128]{1,0:T(8,128)(2,1)S(1)} %get-tuple-element.42), channel_id=1, source_target_pairs={{16,32},{32,16},{48,64},{64,48},{80,96},{96,80},{112,128},{128,112... | collective-permute-start | bytes 196616 | tf_op jit(solution)/shard_map/ppermute | solution.py:518
  12.2 1.9 %collective-permute-start.1 = (bf16[256,128]{1,0:T(8,128)(2,1)S(1)}, bf16[256,128]{1,0:T(8,128)(2,1)S(1)}, u32[]{:S(2)}, u32[]{:S(2)}) collective-permute-start(bf16[256,128]{1,0:T(8,128)(2,1)S(1)} %get-tuple-element.43), channel_id=1, source_target_pairs={{0,16},{16,0},{32,48},{48,32},{64,80},{80,64},{96,112},{112,96},{1... | collective-permute-start | bytes 196616 | tf_op jit(solution)/shard_map/ppermute | solution.py:519
  14.1 1.7 %prepare.1 = (bf16[3456,128]{1,0:T(8,128)(2,1)S(1)}, bf16[128,3456]{1,0:T(8,128)(2,1)S(1)}, f32[2,128]{1,0:T(2,128)S(1)}) custom-call(bf16[27,96,96]{2,1,0:T(8,128)(2,1)} %one_far.2, bf16[27,96,96]{2,1,0:T(8,128)(2,1)} %two_far.2, f32[1,96]{1,0:T(1,128)} %bitcast.10, f32[1,96]{1,0:T(1,128)} %bitcast.11), custom_call_target="tpu_custom_call" | custom-call | bytes 3000000 | tf_op jit(solution)/shard_map/prepare/pallas_call | solution.py:399
  15.8 0.0 collective-permute-done.far_x
  15.8 0.0 collective-permute-done.1.near_x
  15.9 0.7 collective-permute-start.2
  16.6 5.6 %collective-permute-start.3 = (bf16[384,128]{1,0:T(8,128)(2,1)S(1)}, bf16[384,128]{1,0:T(8,128)(2,1)S(1)}, u32[]{:S(2)}, u32[]{:S(2)}) collective-permute-start(bf16[384,128]{1,0:T(8,128)(2,1)S(1)} %get-tuple-element.54), channel_id=1, source_target_pairs={{0,1},{1,0},{2,3},{3,2},{4,5},{5,4},{6,7},{7,6},{8,9},{9,8},{10,11... | collective-permute-start | bytes 294920 | tf_op jit(solution)/shard_map/ppermute | solution.py:519
  22.1 0.0 collective-permute-done.2.far_y
  22.1 2.4 %collective-permute-done.3.near_y = bf16[384,128]{1,0:T(8,128)(2,1)S(1)} collective-permute-done((bf16[384,128]{1,0:T(8,128)(2,1)S(1)}, bf16[384,128]{1,0:T(8,128)(2,1)S(1)}, u32[]{:S(2)}, u32[]{:S(2)}) %collective-permute-start.3) | collective-permute-done | bytes 98336 | tf_op jit(solution)/shard_map/ppermute | solution.py:519
  24.5 5.5 %gradients.1 = (f32[2048,128]{1,0:T(8,128)S(1)}, f32[2048,128]{1,0:T(8,128)S(1)}, bf16[1600,128]{1,0:T(8,128)(2,1)S(1)}) custom-call(f32[2,8,8,8,128]{4,3,2,1,0:T(8,128)S(1)} %get-tuple-element.39.grid, bf16[256,128]{1,0:T(8,128)(2,1)S(1)} %collective-permute-done.far_x, bf16[256,128]{1,0:T(8,128)(2,1)S(1)} %collective-permute-done.1.near_x, ...), custom_call_target="tpu_custom_call" | custom-call | flops 2400000000 | bytes 8000000 | tf_op jit(solution)/shard_map/gradients/pallas_call | solution.py:417
  30.0 3.3 %collective-permute-start.4 = (f32[2048,128]{1,0:T(8,128)S(1)}, f32[2048,128]{1,0:T(8,128)S(1)}, u32[]{:S(2)}, u32[]{:S(2)}) collective-permute-start(f32[2048,128]{1,0:T(8,128)S(1)} %get-tuple-element.59), channel_id=1, source_target_pairs={{0,16},{16,0},{1,17},{17,1},{2,18},{18,2},{3,19},{19,3},{4,20},{20... | collective-permute-start | bytes 3145736 | tf_op jit(solution)/shard_map/ppermute | solution.py:498
  33.3 2.3 %collective-permute-done.4 = f32[2048,128]{1,0:T(8,128)S(1)} collective-permute-done((f32[2048,128]{1,0:T(8,128)S(1)}, f32[2048,128]{1,0:T(8,128)S(1)}, u32[]{:S(2)}, u32[]{:S(2)}) %collective-permute-start.4) | collective-permute-done | bytes 1048608 | tf_op jit(solution)/shard_map/ppermute | solution.py:498
  35.6 0.1 add_convert_fusion
  35.7 0.0 copy-start
  35.7 21.6 %all_to_all.15 = bf16[32,64,128]{2,1,0:T(8,128)(2,1)S(1)} all-to-all(bf16[32,64,128]{2,1,0:T(8,128)(2,1)S(1)} %bitcast.9), channel_id=1, replica_groups=mesh['y'=4,'zh'=4,'core'=2,'zl'=2,'zp'=2,'x'=4] {'y','x','zp'}, dimensions={0} | all-to-all | bytes 1048576 | tf_op jit(solution)/shard_map/all_to_all | solution.py:503
  57.3 0.1 convert_reduce_fusion
  57.4 0.7 broadcast_in_dim.6
  58.1 10.0 %all-to-all-start.1 = ((f32[8,64,128]{2,1,0:T(8,128)}), f32[8,64,128]{2,1,0:T(8,128)S(1)}, u32[]{:S(2)}, u32[]{:S(2)}) async-start(f32[8,64,128]{2,1,0:T(8,128)} %broadcast_in_dim.6), calls=%async_computation.1 | async-start | bytes 524288 | tf_op jit(solution)/shard_map/all_to_all | solution.py:494
  68.1 0.0 copy-done
  68.1 6.2 %outputs.1 = (bf16[4,64,96]{2,1,0:T(8,128)(2,1)S(1)}, bf16[4,64,96]{2,1,0:T(8,128)(2,1)S(1)}) custom-call(s32[1,1,2,2,2]{4,3,2,1,0:T(2,128)S(1)} %copy-done, f32[2,8,8,8,128]{4,3,2,1,0:T(8,128)S(1)} %get-tuple-element.39.grid, bf16[1600,128]{1,0:T(8,128)(2,1)S(1)} %get-tuple-element.60.inner, bf16[27,96,96]{2,1,0:T(8,128)(2,1)} %one_far.2, ...), custom_call_target="tpu_custom_call" | custom-call | flops 900000000 | bytes 4000000 | tf_op jit(solution)/shard_map/outputs/pallas_call | solution.py:438
  74.4 0.8 reshape.39
  75.2 0.8 reshape.40
  75.9 10.6 %all-to-all-done.1 = f32[8,64,128]{2,1,0:T(8,128)S(1)} async-done(((f32[8,64,128]{2,1,0:T(8,128)}), f32[8,64,128]{2,1,0:T(8,128)S(1)}, u32[]{:S(2)}, u32[]{:S(2)}) %all-to-all-start.1) | async-done | bytes 262176 | tf_op jit(solution)/shard_map/all_to_all | solution.py:494
  86.6 0.1 broadcast_in_dim.7
  86.7 12.9 %all_to_all.16 = bf16[32,64,128]{2,1,0:T(8,128)(2,1)S(1)} all-to-all(bf16[32,64,128]{2,1,0:T(8,128)(2,1)S(1)} %broadcast_in_dim.7), channel_id=1, replica_groups=mesh['y'=4,'zh'=4,'core'=2,'zl'=2,'zp'=2,'x'=4] {'y','x','zp'}, dimensions={0} | all-to-all | bytes 1048576 | tf_op jit(solution)/shard_map/all_to_all | solution.py:494
  99.5 7.1 %collective-permute-start.5 = (bf16[2048,128]{1,0:T(8,128)(2,1)S(1)}, bf16[2048,128]{1,0:T(8,128)(2,1)S(1)}, u32[]{:S(2)}, u32[]{:S(2)}) collective-permute-start(bf16[2048,128]{1,0:T(8,128)(2,1)S(1)} %bitcast.6), channel_id=1, source_target_pairs={{0,16},{16,0},{1,17},{17,1},{2,18},{18,2},{3,19},{19,3},{4,20},{20... | collective-permute-start | bytes 1572872 | tf_op jit(solution)/shard_map/ppermute | solution.py:498
  106.6 1.4 %half_finish.1 = (f32[27,96,96]{2,1,0:T(8,128)}, f32[27,96,96]{2,1,0:T(8,128)}) custom-call(bf16[2048,128]{1,0:T(8,128)(2,1)S(1)} %bitcast.7), custom_call_target="tpu_custom_call" | custom-call | bytes 3000000 | tf_op jit(solution)/shard_map/half_finish/pallas_call | solution.py:460
  108.0 0.1 collective-permute-done.5.other
  108.1 1.9 %finish.1 = (f32[27,96,96]{2,1,0:T(8,128)}, f32[27,96,96]{2,1,0:T(8,128)}, f32[1,96]{1,0:T(1,128)}, f32[1,96]{1,0:T(1,128)}) custom-call(f32[27,96,96]{2,1,0:T(8,128)} %get-tuple-element.66.one_in, f32[27,96,96]{2,1,0:T(8,128)} %get-tuple-element.67.two_in, bf16[2048,128]{1,0:T(8,128)(2,1)S(1)} %bitcast.8, ...), custom_call_target="tpu_custom_call", output_to_operand_aliasing={{0}: (0, {}), {1}: (1, {})} | custom-call | bytes 3000000 | tf_op jit(solution)/shard_map/finish/pallas_call | solution.py:474
  (2 shorter events, 0.1 us)
Async XLA Ops:
  2.0 13.9 %collective-permute-start = (bf16[256,128]{1,0:T(8,128)(2,1)S(1)}, bf16[256,128]{1,0:T(8,128)(2,1)S(1)}, u32[]{:S(2)}, u32[]{:S(2)}) collective-permute-start(bf16[256,128]{1,0:T(8,128)(2,1)S(1)} %get-tuple-element.42), channel_id=1, source_target_pairs={{16,32},{32,16},{48,64},{64,48},{80,96},{96,80},{112,128},{128,112... | collective-permute-start | bytes 196616 | tf_op jit(solution)/shard_map/ppermute | solution.py:518
  12.2 3.7 %collective-permute-start.1 = (bf16[256,128]{1,0:T(8,128)(2,1)S(1)}, bf16[256,128]{1,0:T(8,128)(2,1)S(1)}, u32[]{:S(2)}, u32[]{:S(2)}) collective-permute-start(bf16[256,128]{1,0:T(8,128)(2,1)S(1)} %get-tuple-element.43), channel_id=1, source_target_pairs={{0,16},{16,0},{32,48},{48,32},{64,80},{80,64},{96,112},{112,96},{1... | collective-permute-start | bytes 196616 | tf_op jit(solution)/shard_map/ppermute | solution.py:519
  15.9 6.3 %collective-permute-start.2 = (bf16[384,128]{1,0:T(8,128)(2,1)S(1)}, bf16[384,128]{1,0:T(8,128)(2,1)S(1)}, u32[]{:S(2)}, u32[]{:S(2)}) collective-permute-start(bf16[384,128]{1,0:T(8,128)(2,1)S(1)} %get-tuple-element.53), channel_id=1, source_target_pairs={{1,2},{2,1},{3,4},{4,3},{5,6},{6,5},{7,8},{8,7},{9,10},{10,9},{11,... | collective-permute-start | bytes 294920 | tf_op jit(solution)/shard_map/ppermute | solution.py:518
  16.6 8.0 %collective-permute-start.3 = (bf16[384,128]{1,0:T(8,128)(2,1)S(1)}, bf16[384,128]{1,0:T(8,128)(2,1)S(1)}, u32[]{:S(2)}, u32[]{:S(2)}) collective-permute-start(bf16[384,128]{1,0:T(8,128)(2,1)S(1)} %get-tuple-element.54), channel_id=1, source_target_pairs={{0,1},{1,0},{2,3},{3,2},{4,5},{5,4},{6,7},{7,6},{8,9},{9,8},{10,11... | collective-permute-start | bytes 294920 | tf_op jit(solution)/shard_map/ppermute | solution.py:519
  30.0 5.5 %collective-permute-start.4 = (f32[2048,128]{1,0:T(8,128)S(1)}, f32[2048,128]{1,0:T(8,128)S(1)}, u32[]{:S(2)}, u32[]{:S(2)}) collective-permute-start(f32[2048,128]{1,0:T(8,128)S(1)} %get-tuple-element.59), channel_id=1, source_target_pairs={{0,16},{16,0},{1,17},{17,1},{2,18},{18,2},{3,19},{19,3},{4,20},{20... | collective-permute-start | bytes 3145736 | tf_op jit(solution)/shard_map/ppermute | solution.py:498
  35.7 32.4 %copy-start = (s32[1,1,2,2,2]{4,3,2,1,0:T(2,128)S(1)}, s32[1,1,2,2,2]{4,3,2,1,0:T(2,128)}, u32[]{:S(2)}) copy-start(s32[1,1,2,2,2]{4,3,2,1,0:T(2,128)} %slots.1) | copy-start | bytes 100
  58.1 28.4 %all-to-all-start.1 = ((f32[8,64,128]{2,1,0:T(8,128)}), f32[8,64,128]{2,1,0:T(8,128)S(1)}, u32[]{:S(2)}, u32[]{:S(2)}) async-start(f32[8,64,128]{2,1,0:T(8,128)} %broadcast_in_dim.6), calls=%async_computation.1 | async-start | bytes 524288 | tf_op jit(solution)/shard_map/all_to_all | solution.py:494
  99.5 8.6 %collective-permute-start.5 = (bf16[2048,128]{1,0:T(8,128)(2,1)S(1)}, bf16[2048,128]{1,0:T(8,128)(2,1)S(1)}, u32[]{:S(2)}, u32[]{:S(2)}) collective-permute-start(bf16[2048,128]{1,0:T(8,128)(2,1)S(1)} %bitcast.6), channel_id=1, source_target_pairs={{0,16},{16,0},{1,17},{17,1},{2,18},{18,2},{3,19},{19,3},{4,20},{20... | collective-permute-start | bytes 1572872 | tf_op jit(solution)/shard_map/ppermute | solution.py:498

commit v8 on v7

--- a/solution.py
+++ b/solution.py
@@ -312,7 +312,7 @@
                         target[slot] = brick
 
 
-def unpack(scale, parts, grad):
+def unpack(scale, parts, grad, ready):
     lane = lax.broadcasted_iota(jnp.int32, (C, LANES), 1)
     for group in range(6):
         held = [
@@ -324,35 +324,54 @@
         moved = [pltpu.roll(held[part], 32 * part + 32, 1) for part in range(3)]
         last = jnp.where(lane < 32, moved[0], jnp.where(lane < 64, moved[1], moved[2]))
         grad[4 * group + 3] = last[:, 0:C]
+        if group % 2:
+            ready(group // 2)
     for tap in range(24, TAPS):
         grad[tap] = parts[(tap - 6) * C : (tap - 5) * C].astype(F32)[:, 0:C] * scale
 
 
-def put(held, first, grads, sem):
+PIECES = ((0, 8), (8, 16), (16, 24), (24, TAPS))
+
+
+def sent(scale, parts, held, first, grads, sems):
+    def piece(place, index):
+        at = slice(*PIECES[index])
+        return pltpu.make_async_copy(held.at[at], grads[place].at[at], sems.at[index])
+
+    def ready(index):
+        for place in range(2):
+
+            @pl.when(first == place)
+            def _():
+                piece(place, index).start()
+
+    unpack(scale, parts, held, ready)
+    ready(3)
     for place in range(2):
 
         @pl.when(first == place)
         def _():
-            copy = pltpu.make_async_copy(held, grads[place], sem)
-            copy.start()
-            copy.wait()
-
-
-def half_kernel(scale, parts, grad_one, grad_two, held, sem):
-    unpack(scale, parts, held)
-    put(held, parities()[0], (grad_one, grad_two), sem)
+            for index in range(4):
+                piece(place, index).wait()
+
+
+def half_kernel(scale, parts, grad_one, grad_two, held, sems):
+    sent(scale, parts, held, parities()[0], (grad_one, grad_two), sems)
 
 
 def finish_kernel(
-    scale, one_in, two_in, mine, other, grad_one, grad_two, grad_gain, grad_bias, held, sem
+    scale, one_in, two_in, mine, other, grad_one, grad_two, grad_gain, grad_bias,
+    held, sems, gain_line, bias_line, line_sems,
 ):
     core = parities()[0]
-    unpack(scale, other, held)
-    put(held, core, (grad_two, grad_one), sem)
     last = slice(21 * C, HALF)
     rest = jnp.where(core == 1, mine[last].astype(F32), other[last].astype(F32)) * scale
-    grad_gain[...] = rest[0:1, 0:C]
-    grad_bias[...] = rest[1:2, 0:C]
+    gain_line[...] = rest[0:1, 0:C]
+    bias_line[...] = rest[1:2, 0:C]
+    copies = started(((gain_line, grad_gain), (bias_line, grad_bias)), line_sems)
+    sent(scale, other, held, core, (grad_two, grad_one), sems)
+    for copy in copies:
+        copy.wait()
 
 
 def shape(dims, dtype):
@@ -462,7 +481,7 @@
         out_shape=(grads, grads),
         in_specs=[VMEM_SPEC],
         out_specs=(FAR_OUT, FAR_OUT),
-        scratch_shapes=[pltpu.VMEM((TAPS, C, C), F32), pltpu.SemaphoreType.DMA],
+        scratch_shapes=[pltpu.VMEM((TAPS, C, C), F32), pltpu.SemaphoreType.DMA((4,))],
         cost_estimate=pl.CostEstimate(flops=0, bytes_accessed=3_000_000, transcendentals=0),
         compiler_params=pltpu.CompilerParams(vmem_limit_bytes=8 << 20),
         name="half_finish",
@@ -475,8 +494,14 @@
         functools.partial(finish_kernel, scale),
         out_shape=(grads, grads, line, line),
         in_specs=[HBM_SPEC, HBM_SPEC, VMEM_SPEC, VMEM_SPEC],
-        out_specs=(FAR_OUT, FAR_OUT, VMEM_SPEC, VMEM_SPEC),
-        scratch_shapes=[pltpu.VMEM((TAPS, C, C), F32), pltpu.SemaphoreType.DMA],
+        out_specs=(FAR_OUT,) * 4,
+        scratch_shapes=[
+            pltpu.VMEM((TAPS, C, C), F32),
+            pltpu.SemaphoreType.DMA((4,)),
+            pltpu.VMEM((1, C), F32),
+            pltpu.VMEM((1, C), F32),
+            pltpu.SemaphoreType.DMA((2,)),
+        ],
         input_output_aliases={0: 0, 1: 1},
         cost_estimate=pl.CostEstimate(flops=0, bytes_accessed=3_000_000, transcendentals=0),
         compiler_params=pltpu.CompilerParams(vmem_limit_bytes=8 << 20),

time: 111 us -> 110 us (level)
  no operation moved by 1% of the time
where the time goes in v8:
time: 110 us; the launch traced here: 109 us
  starting transfers between devices  38.7 us (35%)
  blocking collectives  34.5 us (31%)
  Pallas kernels  17.3 us (16%)
  waiting for transfers between devices  15.5 us (14%)
  local copies, waits for them, and re-layouts  2.38 us (2%)
    all_to_all x1, blocking collectives, reduce_all(): lax.all_to_all(pair.reshape(lax.axis_size(PLANE), -1, LANES), PLANE, 0, 0)  21.6 us
    all_to_all x1, blocking collectives, spread_out(): return lax.all_to_all(copies, axes, 0, 0)  12.9 us
    ppermute x2, starting transfers between devices, swapped(): far = lax.ppermute(far, axis, route)  10.9 us
    all_to_all x1, waiting for transfers between devices, spread_out(): return lax.all_to_all(copies, axes, 0, 0)  10.6 us
    ppermute x2, starting transfers between devices, other_core(): return lax.ppermute(block, 'core', [(0, 1), (1, 0)])  10.3 us
    all_to_all x1, starting transfers between devices, spread_out(): return lax.all_to_all(copies, axes, 0, 0)  10 us
    ppermute x2, starting transfers between devices, swapped(): near = lax.ppermute(near, axis, [(n, n ^ 1) for n in range(count)])  7.49 us
    pallas_call x1, Pallas kernels, outputs(): call(output_kernel, (result, result), [SMEM_SPEC] + [VMEM_SPEC] * 2 + [HB...  6.24 us
  transfers between devices with their start and end apart: 7, of which 4 were waited for; matrix products, arithmetic and copies ran while one was open for 1% of the time, Pallas kernels for 8%

profile of v8, /device:TPU:1, one launch (start us, length us, event | category | flops | bytes accessed | tf_op | source)
XLA Modules:
  0.0 109.4 jit_solution(6009820383476423511)
XLA Ops:
  0.6 1.3 %dense_grid.1 = (f32[2,8,8,8,128]{4,3,2,1,0:T(8,128)S(1)}, bf16[256,128]{1,0:T(8,128)(2,1)S(1)}, bf16[256,128]{1,0:T(8,128)(2,1)S(1)}) custom-call(s32[1,1,2,2,2]{4,3,2,1,0:T(2,128)} %slots.1, bf16[1,1,4,6144]{3,2,1,0:T(4,128)(2,1)} %features_far.1, bf16[1,1,4,6144]{3,2,1,0:T(4,128)(2,1)} %cotangent_far.1), custom_call_target="tpu_custom_call" | custom-call | bytes 2000000 | tf_op jit(solution)/shard_map/dense_grid/pallas_call | solution.py:382
  2.0 10.2 %collective-permute-start = (bf16[256,128]{1,0:T(8,128)(2,1)S(1)}, bf16[256,128]{1,0:T(8,128)(2,1)S(1)}, u32[]{:S(2)}, u32[]{:S(2)}) collective-permute-start(bf16[256,128]{1,0:T(8,128)(2,1)S(1)} %get-tuple-element.42), channel_id=1, source_target_pairs={{16,32},{32,16},{48,64},{64,48},{80,96},{96,80},{112,128},{128,112... | collective-permute-start | bytes 196616 | tf_op jit(solution)/shard_map/ppermute | solution.py:543
  12.2 1.9 %collective-permute-start.1 = (bf16[256,128]{1,0:T(8,128)(2,1)S(1)}, bf16[256,128]{1,0:T(8,128)(2,1)S(1)}, u32[]{:S(2)}, u32[]{:S(2)}) collective-permute-start(bf16[256,128]{1,0:T(8,128)(2,1)S(1)} %get-tuple-element.43), channel_id=1, source_target_pairs={{0,16},{16,0},{32,48},{48,32},{64,80},{80,64},{96,112},{112,96},{1... | collective-permute-start | bytes 196616 | tf_op jit(solution)/shard_map/ppermute | solution.py:544
  14.1 1.7 %prepare.1 = (bf16[3456,128]{1,0:T(8,128)(2,1)S(1)}, bf16[128,3456]{1,0:T(8,128)(2,1)S(1)}, f32[2,128]{1,0:T(2,128)S(1)}) custom-call(bf16[27,96,96]{2,1,0:T(8,128)(2,1)} %one_far.2, bf16[27,96,96]{2,1,0:T(8,128)(2,1)} %two_far.2, f32[1,96]{1,0:T(1,128)} %bitcast.10, f32[1,96]{1,0:T(1,128)} %bitcast.11), custom_call_target="tpu_custom_call" | custom-call | bytes 3000000 | tf_op jit(solution)/shard_map/prepare/pallas_call | solution.py:418
  15.8 0.0 collective-permute-done.far_x
  15.8 0.0 collective-permute-done.1.near_x
  15.9 0.7 collective-permute-start.2
  16.6 5.6 %collective-permute-start.3 = (bf16[384,128]{1,0:T(8,128)(2,1)S(1)}, bf16[384,128]{1,0:T(8,128)(2,1)S(1)}, u32[]{:S(2)}, u32[]{:S(2)}) collective-permute-start(bf16[384,128]{1,0:T(8,128)(2,1)S(1)} %get-tuple-element.54), channel_id=1, source_target_pairs={{0,1},{1,0},{2,3},{3,2},{4,5},{5,4},{6,7},{7,6},{8,9},{9,8},{10,11... | collective-permute-start | bytes 294920 | tf_op jit(solution)/shard_map/ppermute | solution.py:544
  22.1 0.0 collective-permute-done.2.far_y
  22.1 2.4 %collective-permute-done.3.near_y = bf16[384,128]{1,0:T(8,128)(2,1)S(1)} collective-permute-done((bf16[384,128]{1,0:T(8,128)(2,1)S(1)}, bf16[384,128]{1,0:T(8,128)(2,1)S(1)}, u32[]{:S(2)}, u32[]{:S(2)}) %collective-permute-start.3) | collective-permute-done | bytes 98336 | tf_op jit(solution)/shard_map/ppermute | solution.py:544
  24.5 5.5 %gradients.1 = (f32[2048,128]{1,0:T(8,128)S(1)}, f32[2048,128]{1,0:T(8,128)S(1)}, bf16[1600,128]{1,0:T(8,128)(2,1)S(1)}) custom-call(f32[2,8,8,8,128]{4,3,2,1,0:T(8,128)S(1)} %get-tuple-element.39.grid, bf16[256,128]{1,0:T(8,128)(2,1)S(1)} %collective-permute-done.far_x, bf16[256,128]{1,0:T(8,128)(2,1)S(1)} %collective-permute-done.1.near_x, ...), custom_call_target="tpu_custom_call" | custom-call | flops 2400000000 | bytes 8000000 | tf_op jit(solution)/shard_map/gradients/pallas_call | solution.py:436
  30.0 3.3 %collective-permute-start.4 = (f32[2048,128]{1,0:T(8,128)S(1)}, f32[2048,128]{1,0:T(8,128)S(1)}, u32[]{:S(2)}, u32[]{:S(2)}) collective-permute-start(f32[2048,128]{1,0:T(8,128)S(1)} %get-tuple-element.59), channel_id=1, source_target_pairs={{0,16},{16,0},{1,17},{17,1},{2,18},{18,2},{3,19},{19,3},{4,20},{20... | collective-permute-start | bytes 3145736 | tf_op jit(solution)/shard_map/ppermute | solution.py:523
  33.3 2.3 %collective-permute-done.4 = f32[2048,128]{1,0:T(8,128)S(1)} collective-permute-done((f32[2048,128]{1,0:T(8,128)S(1)}, f32[2048,128]{1,0:T(8,128)S(1)}, u32[]{:S(2)}, u32[]{:S(2)}) %collective-permute-start.4) | collective-permute-done | bytes 1048608 | tf_op jit(solution)/shard_map/ppermute | solution.py:523
  35.6 0.1 add_convert_fusion
  35.7 0.0 copy-start
  35.7 21.6 %all_to_all.15 = bf16[32,64,128]{2,1,0:T(8,128)(2,1)S(1)} all-to-all(bf16[32,64,128]{2,1,0:T(8,128)(2,1)S(1)} %bitcast.9), channel_id=1, replica_groups=mesh['y'=4,'zh'=4,'core'=2,'zl'=2,'zp'=2,'x'=4] {'y','x','zp'}, dimensions={0} | all-to-all | bytes 1048576 | tf_op jit(solution)/shard_map/all_to_all | solution.py:528
  57.3 0.1 convert_reduce_fusion
  57.4 0.7 broadcast_in_dim.6
  58.1 10.0 %all-to-all-start.1 = ((f32[8,64,128]{2,1,0:T(8,128)}), f32[8,64,128]{2,1,0:T(8,128)S(1)}, u32[]{:S(2)}, u32[]{:S(2)}) async-start(f32[8,64,128]{2,1,0:T(8,128)} %broadcast_in_dim.6), calls=%async_computation.1 | async-start | bytes 524288 | tf_op jit(solution)/shard_map/all_to_all | solution.py:519
  68.1 0.0 copy-done
  68.1 6.2 %outputs.1 = (bf16[4,64,96]{2,1,0:T(8,128)(2,1)S(1)}, bf16[4,64,96]{2,1,0:T(8,128)(2,1)S(1)}) custom-call(s32[1,1,2,2,2]{4,3,2,1,0:T(2,128)S(1)} %copy-done, f32[2,8,8,8,128]{4,3,2,1,0:T(8,128)S(1)} %get-tuple-element.39.grid, bf16[1600,128]{1,0:T(8,128)(2,1)S(1)} %get-tuple-element.60.inner, bf16[27,96,96]{2,1,0:T(8,128)(2,1)} %one_far.2, ...), custom_call_target="tpu_custom_call" | custom-call | flops 900000000 | bytes 4000000 | tf_op jit(solution)/shard_map/outputs/pallas_call | solution.py:457
  74.4 0.8 reshape.39
  75.2 0.8 reshape.40
  75.9 10.6 %all-to-all-done.1 = f32[8,64,128]{2,1,0:T(8,128)S(1)} async-done(((f32[8,64,128]{2,1,0:T(8,128)}), f32[8,64,128]{2,1,0:T(8,128)S(1)}, u32[]{:S(2)}, u32[]{:S(2)}) %all-to-all-start.1) | async-done | bytes 262176 | tf_op jit(solution)/shard_map/all_to_all | solution.py:519
  86.6 0.1 broadcast_in_dim.7
  86.7 12.9 %all_to_all.16 = bf16[32,64,128]{2,1,0:T(8,128)(2,1)S(1)} all-to-all(bf16[32,64,128]{2,1,0:T(8,128)(2,1)S(1)} %broadcast_in_dim.7), channel_id=1, replica_groups=mesh['y'=4,'zh'=4,'core'=2,'zl'=2,'zp'=2,'x'=4] {'y','x','zp'}, dimensions={0} | all-to-all | bytes 1048576 | tf_op jit(solution)/shard_map/all_to_all | solution.py:519
  99.5 7.1 %collective-permute-start.5 = (bf16[2048,128]{1,0:T(8,128)(2,1)S(1)}, bf16[2048,128]{1,0:T(8,128)(2,1)S(1)}, u32[]{:S(2)}, u32[]{:S(2)}) collective-permute-start(bf16[2048,128]{1,0:T(8,128)(2,1)S(1)} %bitcast.6), channel_id=1, source_target_pairs={{0,16},{16,0},{1,17},{17,1},{2,18},{18,2},{3,19},{19,3},{4,20},{20... | collective-permute-start | bytes 1572872 | tf_op jit(solution)/shard_map/ppermute | solution.py:523
  106.6 1.2 %half_finish.1 = (f32[27,96,96]{2,1,0:T(8,128)}, f32[27,96,96]{2,1,0:T(8,128)}) custom-call(bf16[2048,128]{1,0:T(8,128)(2,1)S(1)} %bitcast.7), custom_call_target="tpu_custom_call" | custom-call | bytes 3000000 | tf_op jit(solution)/shard_map/half_finish/pallas_call | solution.py:479
  107.9 0.3 collective-permute-done.5.other
  108.1 1.3 %finish.1 = (f32[27,96,96]{2,1,0:T(8,128)}, f32[27,96,96]{2,1,0:T(8,128)}, f32[1,96]{1,0:T(1,128)}, f32[1,96]{1,0:T(1,128)}) custom-call(f32[27,96,96]{2,1,0:T(8,128)} %get-tuple-element.66.one_in, f32[27,96,96]{2,1,0:T(8,128)} %get-tuple-element.67.two_in, bf16[2048,128]{1,0:T(8,128)(2,1)S(1)} %bitcast.8, ...), custom_call_target="tpu_custom_call", output_to_operand_aliasing={{0}: (0, {}), {1}: (1, {})} | custom-call | bytes 3000000 | tf_op jit(solution)/shard_map/finish/pallas_call | solution.py:493
  (2 shorter events, 0.1 us)
Async XLA Ops:
  2.0 13.9 %collective-permute-start = (bf16[256,128]{1,0:T(8,128)(2,1)S(1)}, bf16[256,128]{1,0:T(8,128)(2,1)S(1)}, u32[]{:S(2)}, u32[]{:S(2)}) collective-permute-start(bf16[256,128]{1,0:T(8,128)(2,1)S(1)} %get-tuple-element.42), channel_id=1, source_target_pairs={{16,32},{32,16},{48,64},{64,48},{80,96},{96,80},{112,128},{128,112... | collective-permute-start | bytes 196616 | tf_op jit(solution)/shard_map/ppermute | solution.py:543
  12.2 3.7 %collective-permute-start.1 = (bf16[256,128]{1,0:T(8,128)(2,1)S(1)}, bf16[256,128]{1,0:T(8,128)(2,1)S(1)}, u32[]{:S(2)}, u32[]{:S(2)}) collective-permute-start(bf16[256,128]{1,0:T(8,128)(2,1)S(1)} %get-tuple-element.43), channel_id=1, source_target_pairs={{0,16},{16,0},{32,48},{48,32},{64,80},{80,64},{96,112},{112,96},{1... | collective-permute-start | bytes 196616 | tf_op jit(solution)/shard_map/ppermute | solution.py:544
  15.9 6.3 %collective-permute-start.2 = (bf16[384,128]{1,0:T(8,128)(2,1)S(1)}, bf16[384,128]{1,0:T(8,128)(2,1)S(1)}, u32[]{:S(2)}, u32[]{:S(2)}) collective-permute-start(bf16[384,128]{1,0:T(8,128)(2,1)S(1)} %get-tuple-element.53), channel_id=1, source_target_pairs={{1,2},{2,1},{3,4},{4,3},{5,6},{6,5},{7,8},{8,7},{9,10},{10,9},{11,... | collective-permute-start | bytes 294920 | tf_op jit(solution)/shard_map/ppermute | solution.py:543
  16.6 8.0 %collective-permute-start.3 = (bf16[384,128]{1,0:T(8,128)(2,1)S(1)}, bf16[384,128]{1,0:T(8,128)(2,1)S(1)}, u32[]{:S(2)}, u32[]{:S(2)}) collective-permute-start(bf16[384,128]{1,0:T(8,128)(2,1)S(1)} %get-tuple-element.54), channel_id=1, source_target_pairs={{0,1},{1,0},{2,3},{3,2},{4,5},{5,4},{6,7},{7,6},{8,9},{9,8},{10,11... | collective-permute-start | bytes 294920 | tf_op jit(solution)/shard_map/ppermute | solution.py:544
  30.0 5.5 %collective-permute-start.4 = (f32[2048,128]{1,0:T(8,128)S(1)}, f32[2048,128]{1,0:T(8,128)S(1)}, u32[]{:S(2)}, u32[]{:S(2)}) collective-permute-start(f32[2048,128]{1,0:T(8,128)S(1)} %get-tuple-element.59), channel_id=1, source_target_pairs={{0,16},{16,0},{1,17},{17,1},{2,18},{18,2},{3,19},{19,3},{4,20},{20... | collective-permute-start | bytes 3145736 | tf_op jit(solution)/shard_map/ppermute | solution.py:523
  35.7 32.4 %copy-start = (s32[1,1,2,2,2]{4,3,2,1,0:T(2,128)S(1)}, s32[1,1,2,2,2]{4,3,2,1,0:T(2,128)}, u32[]{:S(2)}) copy-start(s32[1,1,2,2,2]{4,3,2,1,0:T(2,128)} %slots.1) | copy-start | bytes 100
  58.1 28.4 %all-to-all-start.1 = ((f32[8,64,128]{2,1,0:T(8,128)}), f32[8,64,128]{2,1,0:T(8,128)S(1)}, u32[]{:S(2)}, u32[]{:S(2)}) async-start(f32[8,64,128]{2,1,0:T(8,128)} %broadcast_in_dim.6), calls=%async_computation.1 | async-start | bytes 524288 | tf_op jit(solution)/shard_map/all_to_all | solution.py:519
  99.5 8.6 %collective-permute-start.5 = (bf16[2048,128]{1,0:T(8,128)(2,1)S(1)}, bf16[2048,128]{1,0:T(8,128)(2,1)S(1)}, u32[]{:S(2)}, u32[]{:S(2)}) collective-permute-start(bf16[2048,128]{1,0:T(8,128)(2,1)S(1)} %bitcast.6), channel_id=1, source_target_pairs={{0,16},{16,0},{1,17},{17,1},{2,18},{18,2},{3,19},{19,3},{4,20},{20... | collective-permute-start | bytes 1572872 | tf_op jit(solution)/shard_map/ppermute | solution.py:523
